TPU v7x, 32 devices: a whole 2x2x4 slice. The times are simulated.
32 devices in a mesh: seq: 2 (over x), ctx: 16 (over z, y, core).
Axes of the slice: x: 2, y: 2, z: 4, core: 2. Of those that a mesh axis runs over, the one named last changes fastest.
Arguments:
- layer_input: bfloat16 [2, 2048, 768], P('seq', 'ctx'), may hold values from -6 to 6
- cotangent: bfloat16 [2, 2048, 768], P('seq', 'ctx'), may hold values from -6 to 6
- lengths: int32 [2], P('seq'), may hold values from 1024 to 2048, as said below
- query_weight: bfloat16 [768, 768], P(('seq', 'ctx')), may hold values from -0.4375 to 0.4375
- query_bias: bfloat16 [768], P(('seq', 'ctx')), may hold values from -3 to 3
- key_weight: bfloat16 [768, 768], P(('seq', 'ctx')), may hold values from -0.21875 to 0.21875
- value_weight: bfloat16 [768, 768], P(('seq', 'ctx')), may hold values from -0.21875 to 0.21875
- value_bias: bfloat16 [768], P(('seq', 'ctx')), may hold values from -0.1796875 to 0.1796875
- output_weight: bfloat16 [768, 768], P(('seq', 'ctx')), may hold values from -1.25 to 1.25
- output_bias: bfloat16 [768], P(('seq', 'ctx')), may hold values from -1.796875 to 1.796875
- attn_gain: bfloat16 [768], P(('seq', 'ctx')), may hold values from 0.099609375 to 1.8984375
- attn_shift: bfloat16 [768], P(('seq', 'ctx')), may hold values from -1.796875 to 1.796875
- expand_weight: bfloat16 [768, 3072], P(('seq', 'ctx')), may hold values from -0.21875 to 0.21875
- expand_bias: bfloat16 [3072], P(('seq', 'ctx')), may hold values from -1.796875 to 1.796875
- reduce_weight: bfloat16 [3072, 768], P(('seq', 'ctx')), may hold values from -0.109375 to 0.109375
- reduce_bias: bfloat16 [768], P(('seq', 'ctx')), may hold values from -1.796875 to 1.796875
- final_gain: bfloat16 [768], P(('seq', 'ctx')), may hold values from 0.099609375 to 1.8984375
- final_shift: bfloat16 [768], P(('seq', 'ctx')), may hold values from -1.796875 to 1.796875
Outputs:
- layer_output: bfloat16 [2, 2048, 768], P('seq', 'ctx')
- input_grad: float32 [2, 2048, 768], P('seq', 'ctx')
- query_weight_grad: float32 [768, 768], P(('seq', 'ctx'))
- query_bias_grad: float32 [768], P(('seq', 'ctx'))
- key_weight_grad: float32 [768, 768], P(('seq', 'ctx'))
- value_weight_grad: float32 [768, 768], P(('seq', 'ctx'))
- value_bias_grad: float32 [768], P(('seq', 'ctx'))
- output_weight_grad: float32 [768, 768], P(('seq', 'ctx'))
- output_bias_grad: float32 [768], P(('seq', 'ctx'))
- attn_gain_grad: float32 [768], P(('seq', 'ctx'))
- attn_shift_grad: float32 [768], P(('seq', 'ctx'))
- expand_weight_grad: float32 [768, 3072], P(('seq', 'ctx'))
- expand_bias_grad: float32 [3072], P(('seq', 'ctx'))
- reduce_weight_grad: float32 [3072, 768], P(('seq', 'ctx'))
- reduce_bias_grad: float32 [768], P(('seq', 'ctx'))
- final_gain_grad: float32 [768], P(('seq', 'ctx'))
- final_shift_grad: float32 [768], P(('seq', 'ctx'))
Inputs may be any that keep to these rules, and one draw needn't show every extreme that they name: `lengths`: the number of valid tokens of each sequence; slots from it on are padding; some sequence is full in every draw.
All inputs are finite; a program needn't handle non-finite values.
Results may differ from a plain program's by a relative error of at most 0.025.
Values may be sent and summed in bfloat16 or wider, within the bound.
No kernel may reach another device: no remote copies, remote signals or barrier semaphores. Data moves between devices by JAX's collectives and lax.ppermute only.
A program may use at most 576 MiB of HBM per device.

v0:
```python
import jax
import jax.numpy as jnp
from jax import lax
from jax.sharding import PartitionSpec as P

HEADS = 12
HEAD_DIM = 64


EPSILON = 1e-12
MASKED = -1000000000.0


def layer_norm(values, gain, shift):
    center = values - jnp.mean(values, axis=-1, keepdims=True)
    variance = jnp.mean(center * center, axis=-1, keepdims=True)
    return center * lax.rsqrt(variance + EPSILON) * gain + shift


def gelu_exact(values):
    return jax.nn.gelu(values, approximate=False)


def contract_rows(left, right):
    return lax.dot_general(
        left, right, (((0,), (0,)), ((), ())), preferred_element_type=jnp.float32
    )


def times_transpose(left, right):
    return lax.dot_general(
        left, right, (((1,), (1,)), ((), ())), preferred_element_type=jnp.float32
    )


def block_scores(queries, keys, length):
    scores = jnp.einsum("qhd,khd->hqk", queries, keys, preferred_element_type=jnp.float32) * 0.125
    positions = jnp.arange(keys.shape[0], dtype=jnp.int32)
    return jnp.where((positions < length)[None, None, :], scores, MASKED)


def body(
    layer_input,
    cotangent,
    lengths,
    query_weight,
    query_bias,
    key_weight,
    value_weight,
    value_bias,
    output_weight,
    output_bias,
    attn_gain,
    attn_shift,
    expand_weight,
    expand_bias,
    reduce_weight,
    reduce_bias,
    final_gain,
    final_shift,
):
    rows = layer_input.shape[1]
    width = layer_input.shape[2]
    inputs = layer_input[0]
    length = lengths[0]
    own_start = lax.axis_index("ctx") * rows
    own_rows = own_start + jnp.arange(rows, dtype=jnp.int32)
    row_valid = (own_rows < length).astype(jnp.float32)
    (
        query_matrix,
        query_offset,
        key_matrix,
        value_matrix,
        value_offset,
        output_matrix,
        output_offset,
        first_gain,
        first_shift,
    ) = (
        lax.all_gather(query_weight, ("seq", "ctx"), axis=0, tiled=True),
        lax.all_gather(query_bias, ("seq", "ctx"), axis=0, tiled=True),
        lax.all_gather(key_weight, ("seq", "ctx"), axis=0, tiled=True),
        lax.all_gather(value_weight, ("seq", "ctx"), axis=0, tiled=True),
        lax.all_gather(value_bias, ("seq", "ctx"), axis=0, tiled=True),
        lax.all_gather(output_weight, ("seq", "ctx"), axis=0, tiled=True),
        lax.all_gather(output_bias, ("seq", "ctx"), axis=0, tiled=True),
        lax.all_gather(attn_gain, ("seq", "ctx"), axis=0, tiled=True),
        lax.all_gather(attn_shift, ("seq", "ctx"), axis=0, tiled=True),
    )
    query = (
        jnp.dot(inputs, query_matrix, preferred_element_type=jnp.float32)
        + query_offset.astype(jnp.float32)
    ).astype(jnp.bfloat16)
    key = jnp.dot(inputs, key_matrix, preferred_element_type=jnp.float32).astype(jnp.bfloat16)
    value = (
        jnp.dot(inputs, value_matrix, preferred_element_type=jnp.float32)
        + value_offset.astype(jnp.float32)
    ).astype(jnp.bfloat16)
    query3 = query.reshape(rows, HEADS, HEAD_DIM)
    pieces = (
        lax.all_gather(key, "ctx", axis=0, tiled=True),
        lax.all_gather(value, "ctx", axis=0, tiled=True),
    )
    maxima = jnp.full((HEADS, rows), -1e30, jnp.float32)
    keys3 = pieces[0].reshape(-1, HEADS, HEAD_DIM)
    values3 = pieces[1].reshape(-1, HEADS, HEAD_DIM)
    scores = block_scores(query3, keys3, length)
    new_max = jnp.maximum(maxima, jnp.max(scores, axis=-1))
    weights = jnp.exp(scores - new_max[:, :, None])
    totals = jnp.sum(weights, axis=-1)
    update = jnp.einsum(
        "hqk,khd->qhd", weights.astype(jnp.bfloat16), values3, preferred_element_type=jnp.float32
    )
    gathered = update
    maxima, totals, gathered = (new_max, totals, gathered)
    attended = gathered / jnp.transpose(totals)[:, :, None]
    log_sums = maxima + jnp.log(totals)
    attended_low = attended.reshape(rows, width).astype(jnp.bfloat16)
    gain_one = first_gain.astype(jnp.float32)
    shift_one = first_shift.astype(jnp.float32)
    hidden = (
        inputs.astype(jnp.float32)
        + jnp.dot(attended_low, output_matrix, preferred_element_type=jnp.float32)
        + output_offset.astype(jnp.float32)
    )
    middle = layer_norm(hidden, gain_one, shift_one)
    expand_matrix, expand_offset, reduce_matrix, reduce_offset, second_gain, second_shift = (
        lax.all_gather(expand_weight, ("seq", "ctx"), axis=0, tiled=True),
        lax.all_gather(expand_bias, ("seq", "ctx"), axis=0, tiled=True),
        lax.all_gather(reduce_weight, ("seq", "ctx"), axis=0, tiled=True),
        lax.all_gather(reduce_bias, ("seq", "ctx"), axis=0, tiled=True),
        lax.all_gather(final_gain, ("seq", "ctx"), axis=0, tiled=True),
        lax.all_gather(final_shift, ("seq", "ctx"), axis=0, tiled=True),
    )
    gain_two = second_gain.astype(jnp.float32)
    shift_two = second_shift.astype(jnp.float32)
    middle_low = middle.astype(jnp.bfloat16)
    expanded = jnp.dot(
        middle_low, expand_matrix, preferred_element_type=jnp.float32
    ) + expand_offset.astype(jnp.float32)
    active_low = gelu_exact(expanded).astype(jnp.bfloat16)
    combined = (
        middle
        + jnp.dot(active_low, reduce_matrix, preferred_element_type=jnp.float32)
        + reduce_offset.astype(jnp.float32)
    )
    layer_output = layer_norm(combined, gain_two, shift_two)
    upstream = cotangent[0].astype(jnp.float32) * row_valid[:, None]
    unused_two, second_back = jax.vjp(layer_norm, combined, gain_two, shift_two)
    grad_combined, grad_gain_two, grad_shift_two = second_back(upstream)
    combined_low = grad_combined.astype(jnp.bfloat16)
    grad_reduce = contract_rows(active_low, combined_low)
    grad_reduce_bias = jnp.sum(grad_combined, axis=0)
    grad_active = times_transpose(combined_low, reduce_matrix).astype(jnp.bfloat16)
    unused_gelu, gelu_back = jax.vjp(gelu_exact, expanded)
    grad_expanded = gelu_back(grad_active.astype(jnp.float32))[0].astype(jnp.bfloat16)
    grad_expand = contract_rows(middle_low, grad_expanded)
    grad_expand_bias = jnp.sum(grad_expanded.astype(jnp.float32), axis=0)
    grad_middle = grad_combined + times_transpose(grad_expanded, expand_matrix)
    expand_w_out, expand_b_out, reduce_w_out, reduce_b_out, gain_two_out, shift_two_out = (
        lax.psum_scatter(grad_expand, ("seq", "ctx"), scatter_dimension=0, tiled=True),
        lax.psum_scatter(grad_expand_bias, ("seq", "ctx"), scatter_dimension=0, tiled=True),
        lax.psum_scatter(grad_reduce, ("seq", "ctx"), scatter_dimension=0, tiled=True),
        lax.psum_scatter(grad_reduce_bias, ("seq", "ctx"), scatter_dimension=0, tiled=True),
        lax.psum_scatter(grad_gain_two, ("seq", "ctx"), scatter_dimension=0, tiled=True),
        lax.psum_scatter(grad_shift_two, ("seq", "ctx"), scatter_dimension=0, tiled=True),
    )
    unused_one, first_back = jax.vjp(layer_norm, hidden, gain_one, shift_one)
    grad_hidden, grad_gain_one, grad_shift_one = first_back(grad_middle)
    hidden_low = grad_hidden.astype(jnp.bfloat16)
    grad_output = contract_rows(attended_low, hidden_low)
    grad_output_bias = jnp.sum(grad_hidden, axis=0)
    grad_attended = times_transpose(hidden_low, output_matrix).astype(jnp.bfloat16)
    grad3 = grad_attended.reshape(rows, HEADS, HEAD_DIM)
    row_dots = jnp.einsum("qhd,qhd->hq", grad3.astype(jnp.float32), attended)
    pieces = (
        lax.all_gather(key, "ctx", axis=0, tiled=True),
        lax.all_gather(value, "ctx", axis=0, tiled=True),
    )
    keys3 = pieces[0].reshape(-1, HEADS, HEAD_DIM)
    values3 = pieces[1].reshape(-1, HEADS, HEAD_DIM)
    scores = block_scores(query3, keys3, length)
    probs = jnp.exp(scores - log_sums[:, :, None])
    grad_probs = jnp.einsum("qhd,khd->hqk", grad3, values3, preferred_element_type=jnp.float32)
    grad_scores = (probs * (grad_probs - row_dots[:, :, None])).astype(jnp.bfloat16)
    probs, grad_scores = (probs, grad_scores)
    grad_query = (
        jnp.einsum("hqk,khd->qhd", grad_scores, keys3, preferred_element_type=jnp.float32) * 0.125
    )
    key_part = (
        jnp.einsum("hqk,qhd->khd", grad_scores, query3, preferred_element_type=jnp.float32).reshape(
            -1, width
        )
        * 0.125
    )
    value_part = jnp.einsum(
        "hqk,qhd->khd", probs.astype(jnp.bfloat16), grad3, preferred_element_type=jnp.float32
    ).reshape(-1, width)
    key_sum, value_sum = (
        lax.psum_scatter(key_part, "ctx", scatter_dimension=0, tiled=True),
        lax.psum_scatter(value_part, "ctx", scatter_dimension=0, tiled=True),
    )
    grad_query_low = grad_query.reshape(rows, width).astype(jnp.bfloat16)
    grad_key_low = key_sum.astype(jnp.bfloat16)
    grad_value_low = value_sum.astype(jnp.bfloat16)
    grad_query_w = contract_rows(inputs, grad_query_low)
    grad_query_b = jnp.sum(grad_query_low.astype(jnp.float32), axis=0)
    grad_key_w = contract_rows(inputs, grad_key_low)
    grad_value_w = contract_rows(inputs, grad_value_low)
    grad_value_b = jnp.sum(grad_value_low.astype(jnp.float32), axis=0)
    input_grad = (
        grad_hidden
        + times_transpose(grad_query_low, query_matrix)
        + times_transpose(grad_key_low, key_matrix)
        + times_transpose(grad_value_low, value_matrix)
    )
    (
        query_w_out,
        query_b_out,
        key_w_out,
        value_w_out,
        value_b_out,
        output_w_out,
        output_b_out,
        gain_one_out,
        shift_one_out,
    ) = (
        lax.psum_scatter(grad_query_w, ("seq", "ctx"), scatter_dimension=0, tiled=True),
        lax.psum_scatter(grad_query_b, ("seq", "ctx"), scatter_dimension=0, tiled=True),
        lax.psum_scatter(grad_key_w, ("seq", "ctx"), scatter_dimension=0, tiled=True),
        lax.psum_scatter(grad_value_w, ("seq", "ctx"), scatter_dimension=0, tiled=True),
        lax.psum_scatter(grad_value_b, ("seq", "ctx"), scatter_dimension=0, tiled=True),
        lax.psum_scatter(grad_output, ("seq", "ctx"), scatter_dimension=0, tiled=True),
        lax.psum_scatter(grad_output_bias, ("seq", "ctx"), scatter_dimension=0, tiled=True),
        lax.psum_scatter(grad_gain_one, ("seq", "ctx"), scatter_dimension=0, tiled=True),
        lax.psum_scatter(grad_shift_one, ("seq", "ctx"), scatter_dimension=0, tiled=True),
    )
    return (
        layer_output.astype(jnp.bfloat16)[None],
        input_grad[None],
        query_w_out,
        query_b_out,
        key_w_out,
        value_w_out,
        value_b_out,
        output_w_out,
        output_b_out,
        gain_one_out,
        shift_one_out,
        expand_w_out,
        expand_b_out,
        reduce_w_out,
        reduce_b_out,
        gain_two_out,
        shift_two_out,
    )


def solution(mesh):
    placed = (
        P("seq", "ctx", None),
        P("seq", "ctx", None),
        P("seq"),
        P(("seq", "ctx"), None),
        P(("seq", "ctx")),
        P(("seq", "ctx"), None),
        P(("seq", "ctx"), None),
        P(("seq", "ctx")),
        P(("seq", "ctx"), None),
        P(("seq", "ctx")),
        P(("seq", "ctx")),
        P(("seq", "ctx")),
        P(("seq", "ctx"), None),
        P(("seq", "ctx")),
        P(("seq", "ctx"), None),
        P(("seq", "ctx")),
        P(("seq", "ctx")),
        P(("seq", "ctx")),
    )
    return jax.shard_map(
        body,
        mesh=mesh,
        in_specs=placed,
        out_specs=(
            P("seq", "ctx", None),
            P("seq", "ctx", None),
            P(("seq", "ctx"), None),
            P(("seq", "ctx")),
            P(("seq", "ctx"), None),
            P(("seq", "ctx"), None),
            P(("seq", "ctx")),
            P(("seq", "ctx"), None),
            P(("seq", "ctx")),
            P(("seq", "ctx")),
            P(("seq", "ctx")),
            P(("seq", "ctx"), None),
            P(("seq", "ctx")),
            P(("seq", "ctx"), None),
            P(("seq", "ctx")),
            P(("seq", "ctx")),
            P(("seq", "ctx")),
        ),
        check_vma=False,
    )
```

profile of v0, /device:TPU:0, one launch (start us, length us, event | category | flops | bytes accessed | tf_op | source)
XLA Modules:
  0.0 1365.1 jit_solution(9434398050229030703)
XLA Ops:
  17.0 42.4 %all-reduce.19 = (bf16[3072]{0:T(1024)(128)(2,1)S(1)}, bf16[768]{0:T(1024)(128)(2,1)S(1)}, bf16[768]{0:T(1024)(128)(2,1)S(1)}, bf16[768]{0:T(1024)(128)(2,1)S(1)...) all-reduce(bf16[3072]{0:T(1024)(128)(2,1)S(1)} %dynamic-update-slic, ...), channel_id=1, replica_groups=mesh['seq'=2,'ctx'=16] {'seq','ctx'}, use_global_device_ids=true, to_apply=%add.5 | all-reduce | flops 9216 | bytes 36864
  59.4 8.7 all-gather.9.cloned.1.call-done
  70.6 53.3 %all-gather.15.cloned.1.call-done = bf16[768,768]{1,0:T(8,128)(2,1)} async-done(((bf16[24,768]{1,0:T(8,128)(2,1)}), bf16[768,768]{1,0:T(8,128)(2,1)}) %all-gather.15.cloned.1.call-update) | async-done | bytes 1179664 | tf_op jit(solution)/shard_map/all_gather | solution.py:82
  133.3 46.6 %all-gather.13.cloned.1.call-done = bf16[768,768]{1,0:T(8,128)(2,1)} async-done(((bf16[24,768]{1,0:T(8,128)(2,1)}), bf16[768,768]{1,0:T(8,128)(2,1)}) %all-gather.13.cloned.1.call-update) | async-done | bytes 1179664 | tf_op jit(solution)/shard_map/all_gather | solution.py:80
  181.6 45.0 %all-gather.11.cloned.1.call-done = bf16[2048,768]{1,0:T(8,128)(2,1)} async-done(((bf16[128,768]{1,0:T(8,128)(2,1)}), bf16[2048,768]{1,0:T(8,128)(2,1)}) %all-gather.11.cloned.1.call-update) | async-done | bytes 3145744 | tf_op jit(solution)/shard_map/all_gather | solution.py:102
  231.4 41.9 %all-gather.17.cloned.1.call-done = bf16[2048,768]{1,0:T(8,128)(2,1)} async-done(((bf16[128,768]{1,0:T(8,128)(2,1)}), bf16[2048,768]{1,0:T(8,128)(2,1)}) %all-gather.17.cloned.1.call-update) | async-done | bytes 3145744 | tf_op jit(solution)/shard_map/all_gather | solution.py:101
  287.7 41.4 %all-gather.19.cloned.1.call-done = bf16[768,768]{1,0:T(8,128)(2,1)} async-done(((bf16[24,768]{1,0:T(8,128)(2,1)}), bf16[768,768]{1,0:T(8,128)(2,1)}) %all-gather.19.cloned.1.call-update) | async-done | bytes 1179664 | tf_op jit(solution)/shard_map/all_gather | solution.py:85
  332.8 61.6 %all-gather.21.cloned.1.call-done = bf16[768,3072]{1,0:T(8,128)(2,1)} async-done(((bf16[24,3072]{1,0:T(8,128)(2,1)}), bf16[768,3072]{1,0:T(8,128)(2,1)}) %all-gather.21.cloned.1.call-update) | async-done | bytes 4718608 | tf_op jit(solution)/shard_map/all_gather | solution.py:128
  394.4 8.5 multiply_convert_fusion.1
  403.0 56.7 %all-gather.23.cloned.1.call-done = bf16[3072,768]{1,0:T(8,128)(2,1)} async-done(((bf16[96,768]{1,0:T(8,128)(2,1)}), bf16[3072,768]{1,0:T(8,128)(2,1)}) %all-gather.23.cloned.1.call-update) | async-done | bytes 4718608 | tf_op jit(solution)/shard_map/all_gather | solution.py:130
  474.7 10.1 fusion.4
  486.1 10.6 multiply_convert_fusion
  505.5 5.2 convert_reduce_fusion.2
  513.9 55.2 %reduce-scatter.17.cloned.1.call-done = f32[128,768]{0,1:T(8,128)} async-done(((f32[2048,768]{0,1:T(8,128)}), f32[128,768]{0,1:T(8,128)}) %reduce-scatter.17.cloned.1.call-update) | async-done | bytes 393232 | tf_op jit(solution)/shard_map/reduce_scatter | solution.py:201
  572.7 85.1 %reduce-scatter.15.cloned.1.call-done = f32[128,768]{0,1:T(8,128)} async-done(((f32[2048,768]{0,1:T(8,128)}), f32[128,768]{0,1:T(8,128)}) %reduce-scatter.15.cloned.1.call-update) | async-done | bytes 393232 | tf_op jit(solution)/shard_map/reduce_scatter | solution.py:200
  662.3 5.2 fusion.60
  668.7 5.1 fusion.58
  677.9 40.8 %all-reduce.18 = (f32[768]{0:T(1024)S(1)}, f32[768]{0:T(1024)S(1)}, f32[768]{0:T(1024)S(1)}, f32[768]{0:T(1024)S(1)}, f32[768]{0:T(1024)S(1)}, /*index=5*/f32[30...) all-reduce(f32[768]{0:T(1024)} %reduce_sum.177, ...), channel_id=5, replica_groups=mesh['seq'=2,'ctx'=16] {'seq','ctx'}, use_global_device_ids=true, to_apply=%region_14.15.clone | all-reduce | flops 9216 | bytes 73728
  726.9 35.5 %reduce-scatter.19.cloned.1.call-done = f32[24,768]{1,0:T(8,128)} async-done(((f32[768,768]{1,0:T(8,128)}), f32[24,768]{1,0:T(8,128)}) %reduce-scatter.19.cloned.1.call-update) | async-done | bytes 73744 | tf_op jit(solution)/shard_map/reduce_scatter | solution.py:233
  762.4 104.6 %reduce-scatter.25.cloned.1.call-done = f32[24,768]{1,0:T(8,128)} async-done(((f32[768,768]{1,0:T(8,128)}), f32[24,768]{1,0:T(8,128)}) %reduce-scatter.25.cloned.1.call-update) | async-done | bytes 73744
  867.1 103.9 %reduce-scatter.29.cloned.1.call-done = f32[24,768]{1,0:T(8,128)} async-done(((f32[768,768]{1,0:T(8,128)}), f32[24,768]{1,0:T(8,128)}) %reduce-scatter.29.cloned.1.call-update) | async-done | bytes 73744
  971.0 104.7 %reduce-scatter.27.cloned.1.call-done = f32[24,768]{1,0:T(8,128)} async-done(((f32[768,768]{1,0:T(8,128)}), f32[24,768]{1,0:T(8,128)}) %reduce-scatter.27.cloned.1.call-update) | async-done | bytes 73744
  1075.7 140.9 %reduce-scatter.21.cloned.1.call-done = f32[24,3072]{1,0:T(8,128)} async-done(((f32[768,3072]{1,0:T(8,128)}), f32[24,3072]{1,0:T(8,128)}) %reduce-scatter.21.cloned.1.call-update) | async-done | bytes 294928 | tf_op jit(solution)/shard_map/reduce_scatter | solution.py:161
  1216.6 142.0 %reduce-scatter.23.cloned.1.call-done = f32[96,768]{1,0:T(8,128)} async-done(((f32[3072,768]{1,0:T(8,128)}), f32[96,768]{1,0:T(8,128)}) %reduce-scatter.23.cloned.1.call-update) | async-done | bytes 294928 | tf_op jit(solution)/shard_map/reduce_scatter | solution.py:163
  (224 shorter events, 94.7 us)
Async XLA Ops:
  7.2 116.7 %copy-start.4 = (bf16[1,128,768]{2,1,0:T(8,128)(2,1)S(1)}, bf16[1,128,768]{2,1,0:T(8,128)(2,1)}, u32[]{:S(2)}) copy-start(bf16[1,128,768]{2,1,0:T(8,128)(2,1)} %param.18) | copy-start | bytes 589828
  7.2 60.9 %all-gather.9.cloned.1.call-start = ((), (), s32[]{:S(2)}) async-start(), calls=%async_computation.8 | async-start | bytes 1216512 | tf_op jit(solution)/shard_map/all_gather | solution.py:83
  7.9 116.0 %all-gather.15.cloned.1.call-start = ((), (), s32[]{:S(2)}) async-start(), calls=%async_computation.11 | async-start | bytes 1216512 | tf_op jit(solution)/shard_map/all_gather | solution.py:82
  8.7 171.1 %all-gather.13.cloned.1.call-start = ((), (), s32[]{:S(2)}) async-start(), calls=%async_computation.10 | async-start | bytes 1216512 | tf_op jit(solution)/shard_map/all_gather | solution.py:80
  9.4 217.2 %all-gather.11.cloned.1.call-start = ((), (), s32[]{:S(2)}) async-start(), calls=%async_computation.9 | async-start | bytes 3342336 | tf_op jit(solution)/shard_map/all_gather | solution.py:102
  70.5 202.9 %all-gather.17.cloned.1.call-start = ((), (), s32[]{:S(2)}) async-start(), calls=%async_computation.12 | async-start | bytes 3342336 | tf_op jit(solution)/shard_map/all_gather | solution.py:101
  126.2 202.9 %all-gather.19.cloned.1.call-start = ((), (), s32[]{:S(2)}) async-start(), calls=%async_computation.13 | async-start | bytes 1216512 | tf_op jit(solution)/shard_map/all_gather | solution.py:85
  126.8 267.6 %all-gather.21.cloned.1.call-start = ((), (), s32[]{:S(2)}) async-start(), calls=%async_computation.14 | async-start | bytes 4866048 | tf_op jit(solution)/shard_map/all_gather | solution.py:128
  127.5 332.2 %all-gather.23.cloned.1.call-start = ((), (), s32[]{:S(2)}) async-start(), calls=%async_computation.15 | async-start | bytes 4866048 | tf_op jit(solution)/shard_map/all_gather | solution.py:130
  128.3 440.8 %reduce-scatter.17.cloned.1.call-start = ((), (), s32[]{:S(2)}) async-start(), calls=%async_computation.17 | async-start | bytes 6684672 | tf_op jit(solution)/shard_map/reduce_scatter | solution.py:201
  181.6 95.0 %copy-start.18 = (bf16[128,768]{0,1:T(8,128)(2,1)}, bf16[128,768]{0,1:T(8,128)(2,1)S(1)}, u32[]{:S(2)}) copy-start(bf16[128,768]{0,1:T(8,128)(2,1)S(1)} %copy.54) | copy-start | bytes 589828
  332.8 126.9 %copy-start.29 = (f32[128]{0:T(128)S(1)}, f32[128]{0:T(128)}, u32[]{:S(2)}) copy-start(f32[128]{0:T(128)} %copy-done.28) | copy-start | bytes 1540
  332.8 126.9 %copy-start.33 = (f32[768]{0:T(1024)S(1)}, f32[768]{0:T(1024)}, u32[]{:S(2)}) copy-start(f32[768]{0:T(1024)} %convert_element_type.138) | copy-start | bytes 9220
  484.9 172.8 %reduce-scatter.15.cloned.1.call-start = ((), (), s32[]{:S(2)}) async-start(), calls=%async_computation.16 | async-start | bytes 6684672 | tf_op jit(solution)/shard_map/reduce_scatter | solution.py:200
  501.7 260.7 %reduce-scatter.19.cloned.1.call-start = ((), (), s32[]{:S(2)}) async-start(), calls=%async_computation.18 | async-start | bytes 2433024 | tf_op jit(solution)/shard_map/reduce_scatter | solution.py:233
  505.4 361.6 %reduce-scatter.25.cloned.1.call-start = ((), (), s32[]{:S(2)}) async-start(), calls=%async_computation.21 | async-start | bytes 2433024
  513.8 55.3 %copy-start.6 = (bf16[1,128,768]{2,1,0:T(8,128)(2,1)S(1)}, bf16[1,128,768]{2,1,0:T(8,128)(2,1)}, u32[]{:S(2)}) copy-start(bf16[1,128,768]{2,1,0:T(8,128)(2,1)} %param.18) | copy-start | bytes 589828
  513.8 457.2 %reduce-scatter.29.cloned.1.call-start = ((), (), s32[]{:S(2)}) async-start(), calls=%async_computation.23 | async-start | bytes 2433024
  572.6 503.1 %reduce-scatter.27.cloned.1.call-start = ((), (), s32[]{:S(2)}) async-start(), calls=%async_computation.22 | async-start | bytes 2433024
  661.2 555.4 %reduce-scatter.21.cloned.1.call-start = ((), (), s32[]{:S(2)}) async-start(), calls=%async_computation.19 | async-start | bytes 9732096 | tf_op jit(solution)/shard_map/reduce_scatter | solution.py:161
  667.5 691.1 %reduce-scatter.23.cloned.1.call-start = ((), (), s32[]{:S(2)}) async-start(), calls=%async_computation.20 | async-start | bytes 9732096 | tf_op jit(solution)/shard_map/reduce_scatter | solution.py:163
  674.9 49.0 %copy-start.10 = (bf16[768,768]{1,0:T(8,128)(2,1)S(1)}, bf16[768,768]{1,0:T(8,128)(2,1)}, u32[]{:S(2)}) copy-start(bf16[768,768]{1,0:T(8,128)(2,1)} %all-gather.15.cloned.1.call-done) | copy-start | bytes 3538948
  676.5 49.1 %copy-start.9 = (bf16[768,768]{1,0:T(8,128)(2,1)S(1)}, bf16[768,768]{1,0:T(8,128)(2,1)}, u32[]{:S(2)}) copy-start(bf16[768,768]{1,0:T(8,128)(2,1)} %all-gather.9.cloned.1.call-done) | copy-start | bytes 3538948
  676.5 49.1 %copy-start.14 = (f32[128,768]{0,1:T(8,128)S(1)}, f32[128,768]{0,1:T(8,128)}, u32[]{:S(2)}) copy-start(f32[128,768]{0,1:T(8,128)} %reduce-scatter.17.cloned.1.call-done) | copy-start | bytes 1179652
  (45 other events, 167.6 us)
Sparse Core Ops, SparseCore 0:
  10.9 57.1 all-gather.8
  71.0 52.8 all-gather.14
  126.8 52.9 all-gather.12
  182.5 44.0 all-gather.10
  229.4 43.9 all-gather.16
  276.1 52.9 all-gather.18
  332.0 62.3 all-gather.20
  397.3 62.3 all-gather.22
  485.0 84.0 reduce-scatter.16
  573.4 84.2 reduce-scatter.14
  663.6 98.7 reduce-scatter.18
  769.0 98.0 reduce-scatter.24
  872.9 98.0 reduce-scatter.28
  977.6 98.0 reduce-scatter.26
  1082.0 134.5 reduce-scatter.20
  1223.9 134.6 reduce-scatter.22
where the time goes:
time: 1370 us
  waiting for transfers between devices  1130 us (82%)
  blocking collectives  83.2 us (6%)
  matrix products  82.9 us (6%)
  local copies, waits for them, and re-layouts  38.2 us (3%)
  between operations  15.2 us (1%)
    unnamed x19, waiting for transfers between devices  317 us
    reduce_scatter x1, waiting for transfers between devices, body(): lax.psum_scatter(grad_reduce, ('seq', 'ctx'), scatter_dimension=0, tiled=...  142 us
    reduce_scatter x1, waiting for transfers between devices, body(): lax.psum_scatter(grad_expand, ('seq', 'ctx'), scatter_dimension=0, tiled=...  141 us
    reduce_scatter x1, waiting for transfers between devices, body(): lax.psum_scatter(key_part, 'ctx', scatter_dimension=0, tiled=True)  85.1 us
    unnamed x2, blocking collectives  83.2 us
    all_gather x1, waiting for transfers between devices, body(): lax.all_gather(expand_weight, ('seq', 'ctx'), axis=0, tiled=True)  61.6 us
    all_gather x1, waiting for transfers between devices, body(): lax.all_gather(reduce_weight, ('seq', 'ctx'), axis=0, tiled=True)  56.7 us
    reduce_scatter x1, waiting for transfers between devices, body(): lax.psum_scatter(value_part, 'ctx', scatter_dimension=0, tiled=True)  55.2 us
  transfers between devices with their start and end apart: 16, of which 16 were waited for; matrix products, arithmetic and copies ran while one was open for 7% of the time, Pallas kernels for 0%

commit v1 on v0

v1 whole, which is shorter than its diff:
```python
import functools

import jax
import jax.numpy as jnp
import numpy as np
from jax import lax
from jax.experimental import pallas as pl
from jax.experimental.pallas import tpu as pltpu
from jax.sharding import PartitionSpec as P

HEADS = 12
HEAD_DIM = 64
EPSILON = 1e-12
MASKED = -1000000000.0
EVERY = ("seq", "ctx")
F32 = jnp.float32
BF16 = jnp.bfloat16
VMEM = pl.BlockSpec(memory_space=pltpu.VMEM)
SMEM = pl.BlockSpec(memory_space=pltpu.SMEM)
QUERY_B, VALUE_B, OUTPUT_B, GAIN_1, SHIFT_1, REDUCE_B, GAIN_2, SHIFT_2, EXPAND_B = range(9)
VECTOR_ROWS = 16
HELD_BYTES = 16 << 20


def dot(left, right):
    return jnp.dot(left, right, preferred_element_type=F32)


def contract_rows(left, right):
    return lax.dot_general(left, right, (((0,), (0,)), ((), ())), preferred_element_type=F32)


def times_transpose(left, right):
    return lax.dot_general(left, right, (((1,), (1,)), ((), ())), preferred_element_type=F32)


def shaped(shape, dtype):
    return jax.ShapeDtypeStruct(tuple(shape), dtype)


def after(array, *earlier):
    return lax.optimization_barrier((array, *earlier))[0]


def call(kernel, name, outs, *args, scalars=0, flops=0, moved=0, scratch=(), room=16, held=True):
    many = isinstance(outs, (tuple, list))
    flat = tuple(outs) if many else (outs,)
    size = sum(a.size * a.dtype.itemsize for a in (*args, *flat))
    if held and size < HELD_BYTES:
        args = args[:scalars] + tuple(pltpu.with_memory_space_constraint(a, pltpu.VMEM) for a in args[scalars:])
        flat = tuple(pltpu.VMEM(o.shape, o.dtype) for o in flat)
    return pl.pallas_call(
        kernel,
        out_shape=flat if many else flat[0],
        in_specs=[SMEM] * scalars + [VMEM] * (len(args) - scalars),
        out_specs=tuple(VMEM for _ in flat) if many else VMEM,
        scratch_shapes=list(scratch),
        cost_estimate=pl.CostEstimate(flops=int(flops), bytes_accessed=int(moved), transcendentals=0),
        compiler_params=pltpu.CompilerParams(vmem_limit_bytes=room << 20 if size < HELD_BYTES else None),
        name=name,
    )(*args)


def limit(tokens, mebibytes):
    return pltpu.CompilerParams(vmem_limit_bytes=mebibytes << 20 if tokens <= 4096 else None)


class Place:
    def __init__(self):
        self.ctx = lax.axis_size("ctx")
        self.count = lax.axis_size("seq") * self.ctx
        self.bits = self.count.bit_length() - 1
        self.context = lax.axis_index("ctx")
        self.number = lax.axis_index("seq") * self.ctx + self.context
        self.core = self.number & 1
        top = self.bits - 1
        middle = list(range(2, top))
        self.weight_stages = list(zip(middle[::-1], middle)) + [(1, top), (top, 1)]
        self.token_stages = [(1, 1)] + list(zip(middle[::-1], middle))

    def swap(self, array, even, odd=None):
        odd = even if odd is None else odd
        pairs = [(i, i ^ (1 << (odd if i & 1 else even))) for i in range(self.count)]
        return lax.ppermute(array, EVERY, pairs)

    def others(self, stages, core):
        masks = [0]
        for stage in stages:
            masks = masks + [m ^ (1 << stage[core]) for m in masks]
        return np.array(masks, np.int32)

    def gather(self, blocks, stages, stop=0):
        other = None
        for at, stage in enumerate(stages):
            if at:
                blocks = jnp.concatenate([blocks, other])
            other = self.swap(blocks, *stage)
        return blocks, other

    def scatter(self, mine, theirs, stages):
        for at, stage in enumerate(stages[::-1]):
            if at:
                half = mine.shape[0] // 2
                mine, theirs = mine[:half], mine[half:]
            got = self.swap(theirs, *stage)
            mine = (mine.astype(F32) + got.astype(F32)).astype(F32 if at == len(stages) - 1 else BF16)
        return mine[0]


def pack_vectors_kernel(number_ref, *refs):
    *in_refs, expand_ref, out_ref, rows_ref = refs
    own, units, width = in_refs[0].shape[1], expand_ref.shape[1], out_ref.shape[1]
    number = number_ref[0]
    rows_ref[...] = jnp.zeros_like(rows_ref)
    for i, ref in enumerate(in_refs):
        rows_ref[i : i + 1, :own] = ref[...].astype(F32)
    rows_ref[EXPAND_B : EXPAND_B + 1, :units] = expand_ref[...].astype(F32)
    first = pltpu.roll(rows_ref[:8, :], number * own, 1)
    offset = (number // 2) * units
    second = pltpu.roll(rows_ref[8:, :], offset % width, 1)
    here = lax.broadcasted_iota(jnp.int32, second.shape, 0) == offset // width
    second = jnp.where(here, jnp.broadcast_to(second[:1], second.shape), 0.0)
    out_ref[...] = jnp.concatenate([first, second], 0).astype(BF16)


def unpack_vectors_kernel(number_ref, sums_ref, *out_refs):
    own, units, width = out_refs[0].shape[1], out_refs[-1].shape[1], sums_ref.shape[1]
    number = number_ref[0]
    first = pltpu.roll(sums_ref[:8, :], width - number * own, 1)
    for i, ref in enumerate(out_refs[:-1]):
        ref[...] = first[i : i + 1, :own]
    offset = (number // 2) * units
    here = lax.broadcasted_iota(jnp.int32, (VECTOR_ROWS - 8, width), 0) == offset // width
    row = jnp.sum(jnp.where(here, sums_ref[8:, :], 0.0), axis=0, keepdims=True)
    row = pltpu.roll(jnp.broadcast_to(row, (8, width)), width - offset % width, 1)
    out_refs[-1][...] = row[:1, :units]


def place_attention_kernel(table_ref, core_ref, mine_ref, other_ref, vector_ref, kv_ref, q_ref, o_ref, bias_ref):
    half = kv_ref.shape[0] // 2
    rows, side = q_ref.shape[1], q_ref.shape[2]
    tile = mine_ref.shape[1]
    tiles = rows // tile

    def body(j, carry):
        for ref, at in ((mine_ref, j), (other_ref, j + half)):
            chip = table_ref[at]
            for i in range(tiles):
                to = slice(i * tile, (i + 1) * tile)
                kv_ref[chip, to] = ref[j * (2 * tiles) + i]
                q_ref[chip, to] = ref[j * (2 * tiles) + tiles + i, :, :side]
                o_ref[chip, to] = ref[j * (2 * tiles) + tiles + i, :, side:]
        return carry

    lax.fori_loop(0, half, body, 0)
    values = vector_ref[...].astype(F32)
    values = jnp.where(core_ref[0] == 0, values[:8, :side], values[:8, side:])
    bias_ref[:, :side] = jnp.zeros((8, side), F32)
    bias_ref[:, side : 2 * side] = jnp.broadcast_to(values[VALUE_B : VALUE_B + 1], (8, side))
    bias_ref[:, 2 * side :] = jnp.broadcast_to(values[QUERY_B : QUERY_B + 1], (8, side))


def place_expand_kernel(table_ref, mine_ref, other_ref, expand_ref):
    half = mine_ref.shape[0]
    rows, width = expand_ref.shape[1], mine_ref.shape[2]

    def body(j, carry):
        for ref, at in ((mine_ref, j), (other_ref, j + half)):
            chip = table_ref[at]
            for i in range(expand_ref.shape[2] // width):
                expand_ref[chip, :, i * width : (i + 1) * width] = ref[j, i * rows : (i + 1) * rows]
        return carry

    lax.fori_loop(0, half, body, 0)


def place_reduce_kernel(table_ref, mine_ref, other_ref, reduce_ref):
    half = mine_ref.shape[0]

    def body(j, carry):
        reduce_ref[table_ref[j]] = mine_ref[j]
        reduce_ref[table_ref[j + half]] = other_ref[j]
        return carry

    lax.fori_loop(0, half, body, 0)


def split_expand_kernel(table_ref, expand_ref, mine_ref, other_ref):
    half = mine_ref.shape[0]
    rows, width = expand_ref.shape[1], mine_ref.shape[2]

    def body(j, carry):
        for ref, at in ((mine_ref, j), (other_ref, j + half)):
            chip = table_ref[at]
            for i in range(expand_ref.shape[2] // width):
                ref[j, i * rows : (i + 1) * rows] = expand_ref[chip, :, i * width : (i + 1) * width]
        return carry

    lax.fori_loop(0, half, body, 0)


def split_reduce_kernel(table_ref, reduce_ref, mine_ref, other_ref):
    half = mine_ref.shape[0]

    def body(j, carry):
        mine_ref[j] = reduce_ref[table_ref[j]]
        other_ref[j] = reduce_ref[table_ref[j + half]]
        return carry

    lax.fori_loop(0, half, body, 0)


def split_attention_kernel(table_ref, kv_ref, q_ref, o_ref, mine_ref, other_ref):
    half = mine_ref.shape[0]
    rows, side = q_ref.shape[1], q_ref.shape[2]

    def body(j, carry):
        for ref, at in ((mine_ref, j), (other_ref, j + half)):
            chip = table_ref[at]
            ref[j, :rows] = kv_ref[chip]
            ref[j, rows:, :side] = q_ref[chip]
            ref[j, rows:, side:] = o_ref[chip]
        return carry

    lax.fori_loop(0, half, body, 0)


def fold_kernel(keep_ref, got_ref, *out_refs):
    if len(out_refs) == 1:
        out_refs[0][...] = keep_ref[...].astype(F32) + got_ref[...].astype(F32)
        return
    half = out_refs[0].shape[0]
    for i, ref in enumerate(out_refs):
        at = slice(i * half, (i + 1) * half)
        ref[...] = (keep_ref[at].astype(F32) + got_ref[at].astype(F32)).astype(BF16)


def fold(keep, got):
    blocks = keep.shape[0]
    out = shaped(keep.shape, F32) if blocks == 1 else (shaped((blocks // 2,) + keep.shape[1:], BF16),) * 2
    out = call(fold_kernel, "fold", out, keep, got, moved=2 * keep.size)
    return out[0] if blocks == 1 else out


def fold_vectors_kernel(keep_ref, got_ref, vector_ref, *out_refs):
    rows = keep_ref.shape[0]
    vectors = vector_ref[...] + got_ref[rows:, :].astype(F32)
    out_refs[-1][...] = vectors
    if len(out_refs) == 2:
        out_refs[0][...] = keep_ref[...].astype(F32) + got_ref[:rows, :].astype(F32)
        return
    half = rows // 2
    total = keep_ref[...].astype(F32) + got_ref[:rows, :].astype(F32)
    out_refs[0][...] = total[:half].astype(BF16)
    out_refs[1][:half, :] = total[half:].astype(BF16)
    out_refs[1][half:, :] = vectors.astype(BF16)


def fold_vectors(keep, got, vectors, last):
    rows, width = keep.shape
    if last:
        out = (shaped((rows, width), F32), shaped(vectors.shape, F32))
    else:
        out = (
            shaped((rows // 2, width), BF16),
            shaped((rows // 2 + VECTOR_ROWS, width), BF16),
            shaped(vectors.shape, F32),
        )
    return call(fold_vectors_kernel, "fold_vectors", out, keep, got, vectors, moved=2 * keep.size)


def project_kernel(mine_ref, other_ref, weight_ref, bias_ref, out_ref):
    width = weight_ref.shape[1]
    bias = bias_ref[:1, :width]

    @pl.when(pl.program_id(0) == 0)
    def _():
        out_ref[...] = (dot(mine_ref[...], weight_ref[...]) + bias).astype(BF16)

    @pl.when(pl.program_id(0) == 1)
    def _():
        out_ref[...] = (dot(other_ref[...], weight_ref[...]) + bias).astype(BF16)


def project(mine, other, weight, bias):
    rows, width = mine.shape
    step = min(rows, 512)
    steps = rows // step
    return pl.pallas_call(
        project_kernel,
        out_shape=shaped((2 * rows, width), BF16),
        grid=(2, steps),
        in_specs=[
            pl.BlockSpec((step, width), lambda i, j: (jnp.where(i == 0, j, steps - 1), 0)),
            pl.BlockSpec((step, width), lambda i, j: (jnp.where(i == 0, 0, j), 0)),
            pl.BlockSpec(weight.shape, lambda i, j: (0, 0)),
            pl.BlockSpec(bias.shape, lambda i, j: (0, 0)),
        ],
        out_specs=pl.BlockSpec((step, width), lambda i, j: (i * steps + j, 0)),
        cost_estimate=pl.CostEstimate(
            flops=4 * rows * width * width, bytes_accessed=8 * rows * width, transcendentals=0
        ),
        compiler_params=limit(2 * rows, 20),
        name="project",
    )(mine, other, weight, bias)


def attend_kernel(q_ref, k_ref, v_ref, mask_ref, out_ref, logs_ref):
    mask = mask_ref[:, :1].astype(F32)
    outs = []
    for half in range(2):
        at = slice(half * HEAD_DIM, (half + 1) * HEAD_DIM)
        scores = times_transpose(k_ref[:, at], q_ref[:, at]) * 0.125 + mask
        top = jnp.max(scores, axis=0, keepdims=True)
        weights = jnp.exp(scores - top)
        total = jnp.sum(weights, axis=0, keepdims=True)
        outs.append(contract_rows(v_ref[:, at], weights.astype(BF16)) / total)
        logs_ref[0, half : half + 1, :] = top + jnp.log(total)
    out_ref[...] = jnp.transpose(jnp.concatenate(outs, 0))


def attend(query, keys, mask):
    rows, width = query.shape
    tokens = keys.shape[0]
    step = rows if tokens <= 4096 else 128
    pair = 2 * HEAD_DIM
    pairs = width // pair
    spec_q = pl.BlockSpec((step, pair), lambda h, i: (i, h))
    flops = 16 * rows * tokens * width
    return pl.pallas_call(
        attend_kernel,
        out_shape=(shaped((rows, width), F32), shaped((pairs, 8, rows), F32)),
        grid=(pairs, rows // step),
        in_specs=[
            spec_q,
            pl.BlockSpec((tokens, pair), lambda h, i: (0, h)),
            pl.BlockSpec((tokens, pair), lambda h, i: (0, h + pairs)),
            pl.BlockSpec((tokens, 128), lambda h, i: (0, 0)),
        ],
        out_specs=[spec_q, pl.BlockSpec((1, 8, step), lambda h, i: (h, 0, i))],
        cost_estimate=pl.CostEstimate(flops=flops, bytes_accessed=4 * tokens * width, transcendentals=0),
        compiler_params=limit(tokens, 28),
        name="attend",
    )(query, keys, keys, mask)


def attend_back_kernel(
    q_ref, k_ref, v_ref, g_ref, o_ref, logs_ref, mask_ref, dq_ref, dk_ref, dv_ref, bias_ref, dk_sum, dv_sum
):
    step = pl.program_id(0)
    mask = mask_ref[:, :1].astype(F32)

    @pl.when(step == 0)
    def _():
        dk_sum[...] = jnp.zeros_like(dk_sum)
        dv_sum[...] = jnp.zeros_like(dv_sum)

    products = jnp.transpose(g_ref[...].astype(F32) * o_ref[...])
    grads = []
    for half in range(2):
        at = slice(half * HEAD_DIM, (half + 1) * HEAD_DIM)
        query, key, value, grad = q_ref[:, at], k_ref[:, at], v_ref[:, at], g_ref[:, at]
        scores = times_transpose(key, query) * 0.125 + mask
        probs = jnp.exp(scores - logs_ref[0, half : half + 1, :])
        dots = jnp.sum(products[at], axis=0, keepdims=True)
        grad_scores = (probs * (times_transpose(value, grad) - dots)).astype(BF16)
        grads.append(contract_rows(key, grad_scores))
        dk_sum[:, at] += dot(grad_scores, query)
        dv_sum[:, at] += dot(probs.astype(BF16), grad)
    dq_ref[...] = jnp.transpose(jnp.concatenate(grads, 0) * 0.125).astype(BF16)

    @pl.when(step == pl.num_programs(0) - 1)
    def _():
        dk_ref[...] = (dk_sum[...] * 0.125).astype(BF16)
        dv_ref[...] = dv_sum[...].astype(BF16)
        bias_ref[...] = jnp.broadcast_to(columns(dv_sum[...]), bias_ref.shape)


def attend_back(which, query, keys, grad, attended, logs, mask):
    rows, width = query.shape
    tokens = keys.shape[0]
    step = rows if tokens <= 4096 else 128
    pair = 2 * HEAD_DIM
    pairs = width // pair
    single = {"pipeline_mode": pl.Buffered(1)} if tokens > 4096 else {}
    spec_q = pl.BlockSpec((step, pair), lambda i: (i, which))
    spec_dq = pl.BlockSpec((step, pair), lambda i: (i, 0))
    spec_k = pl.BlockSpec((tokens, pair), lambda i: (0, which), **single)
    spec_v = pl.BlockSpec((tokens, pair), lambda i: (0, which + pairs), **single)
    spec_dk = pl.BlockSpec((tokens, pair), lambda i: (0, 0))
    flops = 40 * rows * tokens * pair
    return pl.pallas_call(
        attend_back_kernel,
        out_shape=(
            shaped((rows, pair), BF16),
            shaped((tokens, pair), BF16),
            shaped((tokens, pair), BF16),
            shaped((8, pair), F32),
        ),
        grid=(rows // step,),
        in_specs=[
            spec_q,
            spec_k,
            spec_v,
            spec_q,
            spec_q,
            pl.BlockSpec((1, 8, step), lambda i: (which, 0, i)),
            pl.BlockSpec((tokens, 128), lambda i: (0, 0), **single),
        ],
        out_specs=[spec_dq, spec_dk, spec_dk, pl.BlockSpec((8, pair), lambda i: (0, 0))],
        scratch_shapes=[pltpu.VMEM((tokens, pair), F32), pltpu.VMEM((tokens, pair), F32)],
        cost_estimate=pl.CostEstimate(flops=flops, bytes_accessed=8 * tokens * pair, transcendentals=0),
        compiler_params=limit(tokens, 28),
        name="attend_back",
    )(query, keys, keys, grad, attended, logs, mask)


def keys_inputs_kernel(*refs):
    *part_refs, weight_ref, out_ref = refs
    total = None
    for i, ref in enumerate(part_refs):
        width = ref.shape[1]
        if i % 2:
            continue
        both = jnp.concatenate([ref[...], part_refs[i + 1][...]], axis=1)
        term = times_transpose(both, weight_ref[:, i * width : (i + 2) * width])
        total = term if total is None else total + term
    out_ref[...] = total.astype(BF16)


def keys_inputs(which, parts, weight):
    tokens, pair = parts[0].shape
    tokens //= 2
    width = weight.shape[0]
    step = min(tokens, 512)
    spec = pl.BlockSpec((step, pair), lambda i: (i + which * (tokens // step), 0))
    return pl.pallas_call(
        keys_inputs_kernel,
        out_shape=shaped((tokens, width), BF16),
        grid=(tokens // step,),
        in_specs=[spec] * len(parts) + [pl.BlockSpec(weight.shape, lambda i: (0, 0))],
        out_specs=pl.BlockSpec((step, width), lambda i: (i, 0)),
        cost_estimate=pl.CostEstimate(
            flops=2 * tokens * width * width, bytes_accessed=5 * tokens * width, transcendentals=0
        ),
        compiler_params=limit(tokens, 20),
        name="keys_inputs",
    )(*parts, weight)


def keys_weights_kernel(table_ref, mine_ref, other_ref, q_ref, o_ref, *refs):
    *part_refs, keep_ref, send_ref, sum_ref, held_ref = refs
    first = (pl.program_id(0) == 0) & (pl.program_id(1) == 0)
    last = (pl.program_id(0) == 1) & (pl.program_id(1) == pl.num_programs(1) - 1)
    both = jnp.concatenate([ref[...] for ref in part_refs], axis=1)
    chips, rows, width = held_ref.shape
    half, side = chips // 2, width // 2

    @pl.when(first)
    def _():
        sum_ref[...] = contract_rows(mine_ref[...], both)

    @pl.when((pl.program_id(0) == 0) & (pl.program_id(1) > 0))
    def _():
        sum_ref[...] += contract_rows(mine_ref[...], both)

    @pl.when(pl.program_id(0) == 1)
    def _():
        sum_ref[...] += contract_rows(other_ref[...], both)

    @pl.when(last)
    def _():
        held_ref[...] = sum_ref[...].astype(BF16).reshape(held_ref.shape)

        def body(j, carry):
            for ref, at in ((keep_ref, j), (send_ref, j + half)):
                chip = table_ref[at]
                ref[j, :rows] = held_ref[chip]
                ref[j, rows:, :side] = q_ref[chip]
                ref[j, rows:, side:] = o_ref[chip]
            return carry

        lax.fori_loop(0, half, body, 0)


def flat_keys_weights_kernel(mine_ref, other_ref, *refs):
    *part_refs, grad_ref, sum_ref = refs
    first = (pl.program_id(0) == 0) & (pl.program_id(1) == 0)
    last = (pl.program_id(0) == 1) & (pl.program_id(1) == pl.num_programs(1) - 1)
    both = jnp.concatenate([ref[...] for ref in part_refs], axis=1)

    @pl.when(first)
    def _():
        sum_ref[...] = jnp.zeros_like(sum_ref)

    @pl.when(pl.program_id(0) == 0)
    def _():
        sum_ref[...] += contract_rows(mine_ref[...], both)

    @pl.when(pl.program_id(0) == 1)
    def _():
        sum_ref[...] += contract_rows(other_ref[...], both)

    @pl.when(last)
    def _():
        grad_ref[...] = sum_ref[...].astype(BF16)


def keys_weights(table, mine, other, grad_q, grad_o, parts):
    rows, width = mine.shape
    pair = parts[0].shape[1]
    chips, own = grad_q.shape[:2]
    step = min(rows, 512)
    steps = rows // step
    fused = own % 16 == 0
    block = shaped((chips // 2, 2 * own, width), BF16)
    tokens = [
        pl.BlockSpec((step, width), lambda i, j, *t: (jnp.where(i == 0, j, steps - 1), 0)),
        pl.BlockSpec((step, width), lambda i, j, *t: (jnp.where(i == 0, 0, j), 0)),
    ]
    spec = pl.BlockSpec((step, pair), lambda i, j, *t: (i * steps + j, 0))
    whole = pl.BlockSpec((chips, own, width // 2), lambda i, j, *t: (0, 0, 0))
    blocks = pl.BlockSpec(block.shape, lambda i, j, *t: (0, 0, 0))
    cost = pl.CostEstimate(flops=4 * rows * width * width, bytes_accessed=8 * rows * width, transcendentals=0)
    if fused:
        return pl.pallas_call(
            keys_weights_kernel,
            out_shape=(block, block),
            grid_spec=pltpu.PrefetchScalarGridSpec(
                num_scalar_prefetch=1,
                grid=(2, steps),
                in_specs=tokens + [whole, whole] + [spec] * len(parts),
                out_specs=[blocks, blocks],
                scratch_shapes=[pltpu.VMEM((width, width), F32), pltpu.VMEM((chips, own, width), BF16)],
            ),
            cost_estimate=cost,
            compiler_params=limit(2 * rows, 24),
            name="keys_weights",
        )(table, mine, other, grad_q, grad_o, *parts)
    grad = pl.pallas_call(
        flat_keys_weights_kernel,
        out_shape=shaped((width, width), BF16),
        grid=(2, steps),
        in_specs=tokens + [spec] * len(parts),
        out_specs=pl.BlockSpec((width, width), lambda i, j: (0, 0)),
        scratch_shapes=[pltpu.VMEM((width, width), F32)],
        cost_estimate=cost,
        name="keys_weights",
    )(mine, other, *parts)
    return call(
        split_attention_kernel,
        "split_attention",
        (block, block),
        table,
        grad.reshape(chips, own, width),
        grad_q,
        grad_o,
        scalars=1,
        moved=8 * width * width,
    )


def normalize(values):
    center = values - jnp.mean(values, axis=-1, keepdims=True)
    scale = lax.rsqrt(jnp.mean(center * center, axis=-1, keepdims=True) + EPSILON)
    return center * scale, scale


def normalize_back(grad, normal, scale):
    return scale * (
        grad
        - jnp.mean(grad, axis=-1, keepdims=True)
        - normal * jnp.mean(grad * normal, axis=-1, keepdims=True)
    )


def row(ref, which):
    return ref[which : which + 1, :].astype(F32)


def columns(values):
    return jnp.sum(values, axis=0, keepdims=True)


def output_kernel(
    core_ref, inputs_ref, mine_ref, other_ref, near_ref, far_ref, vector_ref, normal_ref, scale_ref, low_ref
):
    side = mine_ref.shape[1]
    core = core_ref[0]
    here, there = pl.ds(core * side, side), pl.ds((1 - core) * side, side)

    def product(ref):
        return dot(mine_ref[...], ref[here, :]) + dot(other_ref[...], ref[there, :])

    near, far = product(near_ref), product(far_ref)
    even = core == 0
    hidden = jnp.concatenate([jnp.where(even, near, far), jnp.where(even, far, near)], axis=1)
    hidden = inputs_ref[...].astype(F32) + hidden + row(vector_ref, OUTPUT_B)
    normal, scale = normalize(hidden)
    normal_ref[...] = normal
    scale_ref[...] = jnp.broadcast_to(scale, scale_ref.shape)
    low_ref[...] = (normal * row(vector_ref, GAIN_1) + row(vector_ref, SHIFT_1)).astype(BF16)


def hidden_kernel(mine_ref, other_ref, expand_ref, reduce_ref, bias_ref, active_ref, slope_ref, near_ref, far_ref):
    rows = mine_ref.shape[0]
    width = mine_ref.shape[1]
    both = jnp.concatenate([mine_ref[...], other_ref[...]], axis=0)
    total = None
    for i in range(expand_ref.shape[1] // width):
        at = slice(i * width, (i + 1) * width)
        value = dot(both, expand_ref[:, at]) + row(bias_ref, EXPAND_B + 0 + i)
        normal = 0.5 + 0.5 * lax.erf(value * np.float32(0.7071067811865476))
        active = (value * normal).astype(BF16)
        active_ref[:, at] = active
        density = jnp.exp(value * value * -0.5) * np.float32(0.3989422804014327)
        slope_ref[:, at] = normal + value * density
        term = dot(active, reduce_ref[at, :])
        total = term if total is None else total + term
    near_ref[...] = total[:rows]
    far_ref[...] = total[rows:]


def final_kernel(
    start_ref, normal_one_ref, near_ref, far_ref, cotangent_ref, vector_ref, out_ref, grad_ref, low_ref, sums_ref
):
    middle = normal_one_ref[...] * row(vector_ref, GAIN_1) + row(vector_ref, SHIFT_1)
    combined = middle + near_ref[...] + far_ref[...] + row(vector_ref, REDUCE_B)
    normal, scale = normalize(combined)
    gain = row(vector_ref, GAIN_2)
    out_ref[...] = (normal * gain + row(vector_ref, SHIFT_2)).astype(BF16)
    place = start_ref[0] + lax.broadcasted_iota(jnp.int32, combined.shape, 0)
    upstream = jnp.where(place < start_ref[1], cotangent_ref[...].astype(F32), 0.0)
    grad = normalize_back(upstream * gain, normal, scale)
    grad_ref[...] = grad
    low_ref[...] = grad.astype(BF16)
    sums_ref[...] = jnp.zeros_like(sums_ref)
    sums_ref[REDUCE_B : REDUCE_B + 1, :] = columns(grad)
    sums_ref[GAIN_2 : GAIN_2 + 1, :] = columns(upstream * normal)
    sums_ref[SHIFT_2 : SHIFT_2 + 1, :] = columns(upstream)


def hidden_back_kernel(mine_ref, other_ref, expand_ref, reduce_ref, slope_ref, low_ref, near_ref, far_ref, sums_ref):
    rows, width = mine_ref.shape
    both = jnp.concatenate([mine_ref[...], other_ref[...]], axis=0)
    total = None
    sums_ref[...] = jnp.zeros_like(sums_ref)
    for i in range(expand_ref.shape[1] // width):
        at = slice(i * width, (i + 1) * width)
        active = times_transpose(both, reduce_ref[at, :]).astype(BF16)
        grad = (active.astype(F32) * slope_ref[:, at]).astype(BF16)
        low_ref[:, at] = grad
        sums_ref[i : i + 1, :] = columns(grad.astype(F32))
        term = times_transpose(grad, expand_ref[:, at])
        total = term if total is None else total + term
    near_ref[...] = total[:rows]
    far_ref[...] = total[rows:]


def reduce_grads_kernel(table_ref, low_mine_ref, low_other_ref, active_ref, *refs):
    width = low_mine_ref.shape[1]
    low = jnp.concatenate([low_mine_ref[...], low_other_ref[...]], axis=0)
    held = refs[-1]
    chips, rows = held.shape[0], held.shape[1]
    for i in range(active_ref.shape[1] // width):
        part = contract_rows(active_ref[:, i * width : (i + 1) * width], low).astype(BF16)
        if len(refs) == 3:
            held[i * width // rows : (i + 1) * width // rows] = part.reshape(width // rows, rows, width)
        else:
            held[i * width : (i + 1) * width, :] = part
    if len(refs) == 3:
        split_reduce_kernel(table_ref, held, refs[0], refs[1])


def expand_grads_kernel(table_ref, mid_mine_ref, mid_other_ref, low_ref, *refs):
    width = mid_mine_ref.shape[1]
    mid = jnp.concatenate([mid_mine_ref[...], mid_other_ref[...]], axis=0)
    held = refs[-1]
    chips, rows = held.shape[0], held.shape[1]
    for i in range(low_ref.shape[1] // width):
        at = slice(i * width, (i + 1) * width)
        part = contract_rows(mid, low_ref[:, at]).astype(BF16)
        if len(refs) == 3:
            held[:, :, at] = part.reshape(width // rows, rows, width)
        else:
            held[:, at] = part
    if len(refs) == 3:
        split_expand_kernel(table_ref, held, refs[0], refs[1])


def output_back_kernel(
    core_ref, normal_ref, scale_ref, grad_ref, near_sum_ref, far_sum_ref, near_ref, far_ref, vector_ref,
    hidden_ref, low_ref, mine_ref, other_ref, sums_ref,
):
    side = near_ref.shape[1]
    core = core_ref[0]
    even = core == 0
    normal = normal_ref[...]
    grad_middle = grad_ref[...] + near_sum_ref[...] + far_sum_ref[...]
    grad = normalize_back(grad_middle * row(vector_ref, GAIN_1), normal, scale_ref[:, :1])
    hidden_ref[...] = grad
    low = grad.astype(BF16)
    low_ref[...] = low
    low_near = jnp.where(even, low[:, :side], low[:, side:])
    low_far = jnp.where(even, low[:, side:], low[:, :side])
    here, there = pl.ds(core * side, side), pl.ds((1 - core) * side, side)

    def product(rows):
        return times_transpose(low_near, near_ref[rows, :]) + times_transpose(low_far, far_ref[rows, :])

    mine_ref[...] = product(here).astype(BF16)
    other_ref[...] = product(there).astype(BF16)
    sums_ref[...] = jnp.zeros_like(sums_ref)
    sums_ref[OUTPUT_B : OUTPUT_B + 1, :] = columns(grad)
    sums_ref[GAIN_1 : GAIN_1 + 1, :] = columns(grad_middle * normal)
    sums_ref[SHIFT_1 : SHIFT_1 + 1, :] = columns(grad_middle)


def output_grads_kernel(core_ref, mine_ref, other_ref, low_ref, near_ref, far_ref):
    side = mine_ref.shape[1]
    core = core_ref[0]
    even = core == 0
    here, there = pl.ds(core * side, side), pl.ds((1 - core) * side, side)
    for rows, ref in ((here, mine_ref), (there, other_ref)):
        product = contract_rows(ref[...], low_ref[...])
        near_ref[rows, :] = jnp.where(even, product[:, :side], product[:, side:])
        far_ref[rows, :] = jnp.where(even, product[:, side:], product[:, :side]).astype(BF16)


def query_back_kernel(mine_ref, other_ref, weight_ref, *refs):
    *dq_refs, near_ref, far_ref, grad_ref, sums_ref = refs
    rows = mine_ref.shape[0]
    grads = jnp.concatenate([ref[...] for ref in dq_refs], axis=1)
    product = times_transpose(grads, weight_ref[...])
    near_ref[...] = product[:rows]
    far_ref[...] = product[rows:]
    both = jnp.concatenate([mine_ref[...], other_ref[...]], axis=0)
    grad_ref[...] = contract_rows(both, grads).astype(BF16)
    sums_ref[...] = jnp.broadcast_to(columns(grads.astype(F32)), sums_ref.shape)


def body(
    layer_input,
    cotangent,
    lengths,
    query_weight,
    query_bias,
    key_weight,
    value_weight,
    value_bias,
    output_weight,
    output_bias,
    attn_gain,
    attn_shift,
    expand_weight,
    expand_bias,
    reduce_weight,
    reduce_bias,
    final_gain,
    final_shift,
):
    place = Place()
    core = place.core
    core_s = core.reshape(1)
    number_s = place.number.reshape(1)
    chips = place.count // 2
    inputs = layer_input[0]
    rows, width = inputs.shape
    side = width // 2
    own = query_weight.shape[0]
    units = reduce_weight.shape[0]
    hidden_units = units * chips
    times = hidden_units // width
    length = lengths[0]
    even = core == 0

    masks = [place.others(place.weight_stages, k) for k in range(2)]
    table = (place.number ^ jnp.where(even, masks[0], masks[1])) // 2
    token_masks = [place.others(place.token_stages, k) for k in range(2)]
    near_ctx = place.context ^ jnp.where(even, token_masks[0], token_masks[1])
    far_ctx = (place.context ^ 1) ^ jnp.where(even, token_masks[1], token_masks[0])
    blocks = jnp.concatenate([near_ctx, far_ctx])
    positions = (blocks[:, None] * rows + jnp.arange(rows, dtype=jnp.int32)).reshape(-1, 1)
    mask = jnp.broadcast_to(jnp.where(positions < length, 0.0, MASKED).astype(BF16), (positions.shape[0], 128))

    def halves(weight, which):
        return jnp.where(which == 0, weight[:, :side], weight[:, side:])

    def attention_part(which):
        k, v, q, o = (halves(w, which) for w in (key_weight, value_weight, query_weight, output_weight))
        return jnp.stack([jnp.concatenate([k, v], 1), jnp.concatenate([q, o], 1)])

    expand4 = expand_weight.reshape(own, chips, 2, units)

    def expand_part(which):
        part = jnp.where(which == 0, expand4[:, :, 0], expand4[:, :, 1]).reshape(own, hidden_units)
        return jnp.stack([part[:, i * width : (i + 1) * width] for i in range(times)])

    def joined(mine, other):
        return jnp.where(
            even, jnp.concatenate([mine, other], 1), jnp.concatenate([other, mine], 1)
        ).reshape(-1, width)

    vector_list = [query_bias, value_bias, output_bias, attn_gain, attn_shift, reduce_bias, final_gain, final_shift]
    vectors = call(
        pack_vectors_kernel,
        "pack_vectors",
        shaped((VECTOR_ROWS, width), BF16),
        number_s,
        *[v.reshape(1, own) for v in vector_list],
        expand_bias.reshape(1, units),
        scalars=1,
        held=False,
        scratch=[pltpu.VMEM((VECTOR_ROWS, width), F32)],
    )
    vector_swap = place.swap(vectors, 0)
    vectors = vectors + jnp.where(jnp.arange(VECTOR_ROWS)[:, None] < 8, vector_swap, 0)

    stages = place.weight_stages
    token_stages = place.token_stages

    def swap(stage, array, *earlier):
        return place.swap(after(array, *earlier) if earlier else array, *stage)

    def grow(held, got):
        return jnp.concatenate([held, got])

    other_inputs = place.swap(inputs, 0)
    b_held = joined(attention_part(core), place.swap(attention_part(1 - core), 0))
    a_held = joined(expand_part(core), place.swap(expand_part(1 - core), 0))[None]
    d_held = reduce_weight[None]
    x_held = inputs[None]
    block_rows = b_held.shape[0]
    last = len(stages) - 1
    b_gots, x_gots, a_gots, d_gots = [], [], [], []
    for at in range(last + 1):
        b_gots.append(swap(stages[at], jnp.concatenate([b_held, vectors])))
        vectors = vectors + b_gots[-1][-VECTOR_ROWS:]
        if at < len(token_stages):
            if at:
                x_held = grow(x_held, x_gots[-1])
            x_gots.append(swap(token_stages[at], x_held, *b_gots[at - 1 : at] if at else ()))
        if at < last:
            b_held = grow(b_held, b_gots[-1][:-VECTOR_ROWS])
    for at in range(last - 1):
        if at:
            a_held = grow(a_held, after(a_gots[-1], b_gots[at]))
            d_held = grow(d_held, after(d_gots[-1], a_gots[-1], b_gots[at + 1]))
        a_gots.append(swap(stages[at], a_held, *b_gots[at : at + 1] if at else ()))
        d_gots.append(swap(stages[at], d_held, a_gots[-1]))
    a_held = grow(a_held, after(a_gots[-1], b_gots[last - 1]))
    a_gots.append(swap(stages[last - 1], a_held))

    aligned = (2 * own) % 16 == 0
    tile = 16 if aligned else 2 * own

    def tiles(array):
        array = array if aligned else array[: array.shape[0] // block_rows * block_rows]
        return array.reshape(-1, tile, width)

    weights_kv, weights_q, output_near, bias = call(
        place_attention_kernel,
        "place_attention",
        (
            shaped((chips, 2 * own, width), BF16),
            shaped((chips, 2 * own, side), BF16),
            shaped((chips, 2 * own, side), BF16),
            shaped((8, 3 * side), F32),
        ),
        table,
        core_s,
        tiles(b_held),
        tiles(b_gots[-1]),
        vectors,
        scalars=2,
        moved=8 * width * width,
    )
    weights_kv = weights_kv.reshape(width, width)
    weights_q = weights_q.reshape(width, side)
    output_near = output_near.reshape(width, side)
    sequence_near = grow(x_held, x_gots[-1]).reshape(-1, width)
    sequence_far = place.swap(sequence_near, 0)
    keys = project(sequence_near, sequence_far, weights_kv, bias)
    a_held = grow(a_held, after(a_gots[-1], weights_kv))
    a_gots.append(swap(stages[last], a_held))
    d_held = grow(d_held, after(d_gots[-1], weights_kv))
    d_gots.append(swap(stages[last - 1], d_held))
    d_held = grow(d_held, after(d_gots[-1], keys))
    d_got = swap(stages[last], d_held)
    query = jnp.concatenate([inputs, other_inputs])
    query = (dot(query, weights_q) + bias[:1, 2 * side :]).astype(BF16)
    attended, logs = attend(query, keys, mask)
    output_far = place.swap(output_near, 0)
    expand_matrix = call(
        place_expand_kernel,
        "place_expand",
        shaped((chips, 2 * own, hidden_units), BF16),
        table,
        a_held,
        a_gots[-1],
        scalars=1,
        moved=4 * hidden_units * width,
    ).reshape(width, hidden_units)
    reduce_matrix = call(
        place_reduce_kernel,
        "place_reduce",
        shaped((chips, units, width), BF16),
        table,
        d_held,
        d_got,
        scalars=1,
        moved=4 * hidden_units * width,
    ).reshape(hidden_units, width)
    attended_low = attended.astype(BF16)
    attended_mine = attended_low[:rows]
    attended_other = place.swap(attended_low[rows:], 0)

    normal_one, scale_one, middle_low = call(
        output_kernel,
        "output",
        (shaped((rows, width), F32), shaped((rows, 128), F32), shaped((rows, width), BF16)),
        core_s,
        after(inputs, expand_matrix),
        attended_mine,
        attended_other,
        output_near,
        output_far,
        vectors,
        scalars=1,
        flops=2 * rows * width * width,
        moved=4 * width * width,
    )

    middle_other = place.swap(middle_low, 0)
    active, slope, near, far = call(
        hidden_kernel,
        "hidden",
        (
            shaped((2 * rows, hidden_units), BF16),
            shaped((2 * rows, hidden_units), F32),
            shaped((rows, width), F32),
            shaped((rows, width), F32),
        ),
        middle_low,
        middle_other,
        expand_matrix,
        reduce_matrix,
        vectors,
        flops=8 * rows * width * hidden_units,
        moved=4 * width * hidden_units,
    )
    far = place.swap(far, 0)
    start_s = jnp.stack([place.context * rows, length])
    layer_output, grad_combined, combined_low, sums_two = call(
        final_kernel,
        "final",
        (
            shaped((rows, width), BF16),
            shaped((rows, width), F32),
            shaped((rows, width), BF16),
            shaped((8, width), F32),
        ),
        start_s,
        normal_one,
        near,
        far,
        cotangent[0],
        vectors,
        scalars=1,
        moved=12 * rows * width,
    )
    combined_other = place.swap(combined_low, 0)
    grad_expanded, near, far, sums_expand = call(
        hidden_back_kernel,
        "hidden_back",
        (
            shaped((2 * rows, hidden_units), BF16),
            shaped((rows, width), F32),
            shaped((rows, width), F32),
            shaped((8, width), F32),
        ),
        combined_low,
        combined_other,
        expand_matrix,
        reduce_matrix,
        slope,
        flops=8 * rows * width * hidden_units,
        moved=4 * width * hidden_units,
    )
    far = place.swap(far, 0)
    def weight_grads(kernel, split, name, shape, blocks, *args):
        out = (shaped((chips // 2,) + blocks, BF16),) * 2
        cost = dict(flops=4 * rows * width * hidden_units, moved=6 * width * hidden_units)
        if (2 * own) % 16 == 0:
            rows_each = shape[0] // chips
            scratch = [pltpu.VMEM((chips, rows_each, shape[1]), BF16)]
            return call(kernel, name, out, table, *args, scalars=1, scratch=scratch, **cost)
        flat = call(kernel, name, shaped(shape, BF16), table, *args, scalars=1, **cost)
        return call(split, name + "_split", out, table, flat.reshape(chips, -1, shape[1]), scalars=1, **cost)

    reduce_keep, reduce_send = weight_grads(
        reduce_grads_kernel,
        split_reduce_kernel,
        "reduce_grads",
        (hidden_units, width),
        (units, width),
        combined_low,
        combined_other,
        active,
    )
    expand_keep, expand_send = weight_grads(
        expand_grads_kernel,
        split_expand_kernel,
        "expand_grads",
        (width, hidden_units),
        (times * 2 * own, width),
        middle_low,
        middle_other,
        grad_expanded,
    )

    grad_hidden, hidden_low, grad_mine, grad_other, sums_one = call(
        output_back_kernel,
        "output_back",
        (
            shaped((rows, width), F32),
            shaped((rows, width), BF16),
            shaped((rows, side), BF16),
            shaped((rows, side), BF16),
            shaped((8, width), F32),
        ),
        core_s,
        normal_one,
        scale_one,
        grad_combined,
        near,
        far,
        output_near,
        output_far,
        vectors,
        scalars=1,
        flops=2 * rows * width * width,
        moved=4 * width * width,
    )
    grad_heads = jnp.concatenate([grad_mine, place.swap(grad_other, 0)])
    output_near_grad, output_far_grad = call(
        output_grads_kernel,
        "output_grads",
        (shaped((width, side), F32), shaped((width, side), BF16)),
        core_s,
        attended_mine,
        attended_other,
        hidden_low,
        scalars=1,
        flops=2 * rows * width * width,
        moved=4 * width * width,
    )
    grad_output = (output_near_grad + place.swap(output_far_grad, 0).astype(F32)).astype(BF16)

    back = place.weight_stages[::-1]

    def own_half(array, axis):
        first, second = lax.index_in_dim(array, 0, axis, False), lax.index_in_dim(array, 1, axis, False)
        return jnp.where(even, first, second), jnp.where(even, second, first)

    d_keep, d_send = reduce_keep, reduce_send
    a_keep, a_send = expand_keep, expand_send
    done = len(back) - 1
    d_at = a_at = 0

    def d_start():
        return swap(back[d_at], d_send)

    def a_start():
        return swap(back[a_at], a_send)

    def d_end(got, *earlier):
        nonlocal d_keep, d_send, d_at
        out = fold(d_keep, after(got, *earlier) if earlier else got)
        d_keep, d_send = (out, None) if d_at == done else out
        d_at += 1
        return d_start() if d_at <= done else None

    def a_end(got, *earlier):
        nonlocal a_keep, a_send, a_at
        out = fold(a_keep, after(got, *earlier) if earlier else got)
        a_keep, a_send = (out, None) if a_at == done else out
        a_at += 1
        return a_start() if a_at <= done else None

    d_got, a_got = d_start(), a_start()
    first_got = d_got
    parts = []
    pairs = side // (2 * HEAD_DIM)
    for which in range(pairs):
        pinned = after(query, first_got) if which else query
        parts.append(attend_back(which, pinned, keys, grad_heads, attended, logs, mask))
    d_got = d_end(d_got)
    grad_query, grad_keys, grad_values, value_bias_sums = zip(*parts)
    parts = grad_keys + grad_values
    far_part = keys_inputs(1, parts, weights_kv)
    far_got = place.swap(far_part, 0)
    near_part = keys_inputs(0, parts, weights_kv)
    tokens = sequence_near.shape[0]
    blocks_shape = (tokens // rows, rows, width)
    x_keep, x_send = fold(near_part.reshape(blocks_shape), far_got.reshape(blocks_shape))
    first_got = a_got
    a_got = a_end(a_got, far_part)
    near, far, grad_query_w, query_bias_sum = call(
        query_back_kernel,
        "query_back",
        (
            shaped((rows, width), F32),
            shaped((rows, width), F32),
            shaped((width, side), BF16),
            shaped((8, side), F32),
        ),
        inputs,
        other_inputs,
        weights_q,
        *grad_query,
        flops=8 * rows * width * side,
        moved=6 * width * width,
    )
    query_part = grad_hidden + near + place.swap(far, 0)

    mine_rows = jnp.stack([query_bias_sum[0], jnp.concatenate([v[0] for v in value_bias_sums])])
    zero = jnp.zeros_like(mine_rows)
    mine_rows = jnp.where(even, jnp.concatenate([mine_rows, zero], 1), jnp.concatenate([zero, mine_rows], 1))
    vector_sums = jnp.concatenate([mine_rows, (sums_one + sums_two)[2:], sums_expand])
    vector_swap = place.swap(vector_sums, 0)
    vector_sums = vector_sums + jnp.where(jnp.arange(VECTOR_ROWS)[:, None] < 8, vector_swap, 0)

    keep, send = keys_weights(
        table,
        after(sequence_near, first_got, x_send),
        sequence_far,
        grad_query_w.reshape(chips, 2 * own, side),
        grad_output.reshape(chips, 2 * own, side),
        parts,
    )
    keep = keep.reshape(-1, width)
    send = jnp.concatenate([send.reshape(-1, width), vector_sums.astype(BF16)])
    token_back = token_stages[::-1]
    x_count, count = len(token_back), len(back)
    d_got = d_end(d_got, keep)
    a_got = a_end(a_got, keep)
    for at in range(count):
        x_got = ()
        if at < x_count:
            x_got = (swap(token_back[at], x_send),)
            x_keep = fold(x_keep, x_got[0])
            if at + 1 < x_count:
                x_keep, x_send = x_keep
        b_got = swap(back[at], send)
        if d_at <= done:
            d_got = d_end(d_got, *x_got)
        if a_at <= done:
            a_got = a_end(a_got, *x_got, b_got)
        if at + 1 < count:
            keep, send, vector_sums = fold_vectors(keep, b_got, vector_sums, False)
        else:
            keep, vector_sums = fold_vectors(keep, b_got, vector_sums, True)
    reduce_out = d_keep
    expand_sum = a_keep.reshape(times, 2, own, width)
    input_grad = query_part + x_keep

    expand_mine, expand_other = own_half(expand_sum, 1)
    expand_other = place.swap(expand_other, 0)

    def unit_order(array):
        return jnp.concatenate([array[i] for i in range(times)], 1).reshape(own, chips, units)

    expand_mine, expand_other = unit_order(expand_mine), unit_order(expand_other)
    expand_out = jnp.stack(
        [jnp.where(even, expand_mine, expand_other), jnp.where(even, expand_other, expand_mine)], 2
    ).reshape(own, 2 * hidden_units)

    pieces = keep.reshape(2, 2, own, width)
    pieces_mine, pieces_other = own_half(pieces, 1)
    pieces_other = place.swap(pieces_other, 0)

    def weight_out(pair, second):
        at = slice(side, None) if second else slice(0, side)
        a, b = pieces_mine[pair, :, at], pieces_other[pair, :, at]
        return jnp.concatenate([jnp.where(even, a, b), jnp.where(even, b, a)], 1)

    outs = call(
        unpack_vectors_kernel,
        "unpack_vectors",
        [shaped((1, own), F32)] * 8 + [shaped((1, units), F32)],
        number_s,
        vector_sums,
        scalars=1,
        held=False,
    )
    outs = [v.reshape(-1) for v in outs]
    return (
        layer_output[None],
        input_grad[None],
        weight_out(1, False),
        outs[QUERY_B],
        weight_out(0, False),
        weight_out(0, True),
        outs[VALUE_B],
        weight_out(1, True),
        outs[OUTPUT_B],
        outs[GAIN_1],
        outs[SHIFT_1],
        expand_out,
        outs[EXPAND_B],
        reduce_out,
        outs[REDUCE_B],
        outs[GAIN_2],
        outs[SHIFT_2],
    )


def solution(mesh):
    tokens = P("seq", "ctx", None)
    matrix = P(("seq", "ctx"), None)
    vector = P(("seq", "ctx"))
    weights = (
        matrix,
        vector,
        matrix,
        matrix,
        vector,
        matrix,
        vector,
        vector,
        vector,
        matrix,
        vector,
        matrix,
        vector,
        vector,
        vector,
    )
    return jax.shard_map(
        body,
        mesh=mesh,
        in_specs=(tokens, tokens, P("seq")) + weights,
        out_specs=(tokens, tokens) + weights,
        check_vma=False,
    )
```

time: 1370 us -> 262 us (0.19)
  waiting for transfers between devices: 1130 us -> 129 us
  blocking collectives: 83.2 us -> 0 us
  matrix products: 82.9 us -> 0.37 us
  Pallas kernels: 0 us -> 47.9 us
  starting transfers between devices: 1.08 us -> 46.5 us
    reduce_scatter x5 -> x0, waiting for transfers between devices: 459 us -> none  [the longest x1 142 us: body(): lax.psum_scatter(grad_reduce, ('seq', 'ctx'), scatter_dimension=0, tiled=...]
    all_gather x8 -> x0, waiting for transfers between devices: 355 us -> none  [the longest x1 61.6 us: body(): lax.all_gather(expand_weight, ('seq', 'ctx'), axis=0, tiled=True)]
    unnamed x19 -> x0, waiting for transfers between devices: 317 us -> none
    ppermute x0 -> x48, waiting for transfers between devices: none -> 129 us  [swap(): return lax.ppermute(array, EVERY, pairs)]
    unnamed x2 -> x0, blocking collectives: 83.2 us -> none
    dot_general x24 -> x1, matrix products: 82.9 us -> 0.37 us  [dot(): return jnp.dot(left, right, preferred_element_type=F32)]
    pallas_call x0 -> x38, Pallas kernels: none -> 47.9 us  [the longest x30 17.1 us: call(): pl.pallas_call(kernel, out_shape=flat if many else flat[0], in_specs=[SME...]
    ppermute x0 -> x48, starting transfers between devices: none -> 46.5 us  [swap(): return lax.ppermute(array, EVERY, pairs)]
  transfers between devices with their start and end apart: 16 -> 48, of which waited for: 16 -> 23; matrix products, arithmetic and copies ran while one was open for 7% -> 6% of each run, Pallas kernels for 0% -> 14%
where the time goes in v1:
time: 262 us; the launch traced here: 261 us
  waiting for transfers between devices  129 us (49%)
  Pallas kernels  47.9 us (18%)
  starting transfers between devices  46.5 us (18%)
  local copies, waits for them, and re-layouts  25.4 us (10%)
  other arithmetic  9.41 us (4%)
    ppermute x48, waiting for transfers between devices, swap(): return lax.ppermute(array, EVERY, pairs)  129 us
    ppermute x48, starting transfers between devices, swap(): return lax.ppermute(array, EVERY, pairs)  46.5 us
    unnamed x125, local copies, waits for them, and re-layouts  21.4 us
    pallas_call x30, Pallas kernels, call(): pl.pallas_call(kernel, out_shape=flat if many else flat[0], in_specs=[SME...  17.1 us
    pallas_call x3, Pallas kernels, attend_back(): pl.pallas_call(attend_back_kernel, out_shape=(shaped((rows, pair), BF16),...  10.7 us
    pallas_call x1, Pallas kernels, attend(): pl.pallas_call(attend_kernel, out_shape=(shaped((rows, width), F32), shap...  8.7 us
  transfers between devices with their start and end apart: 48, of which 23 were waited for; matrix products, arithmetic and copies ran while one was open for 6% of the time, Pallas kernels for 14%

profile of v1, /device:TPU:0, one launch (start us, length us, event | category | flops | bytes accessed | tf_op | source)
XLA Modules:
  0.0 261.2 jit_solution(13382319086608955857)
XLA Ops:
  8.9 3.0 %collective-permute-start.12 = (bf16[1,128,768]{2,1,0:T(8,128)(2,1)}, bf16[1,128,768]{2,1,0:T(8,128)(2,1)S(1)}, u32[]{:S(2)}, u32[]{:S(2)}) collective-permute-start(bf16[1,128,768]{2,1,0:T(8,128)(2,1)} %param.22), channel_id=1, source_target_pairs={{0,2},{1,3},{2,0},{3,1},{4,6},{5,7},{6,4},{7,5},{8,10},{9,11},{10,... | collective-permute-start | bytes 589832 | tf_op jit(solution)/shard_map/ppermute | solution.py:84
  16.8 3.6 %collective-permute-done.4 = bf16[112,768]{1,0:T(8,128)(2,1)S(1)} collective-permute-done((bf16[112,768]{1,0:T(8,128)(2,1)S(1)}, bf16[112,768]{1,0:T(8,128)(2,1)S(1)}, u32[]{:S(2)}, u32[]{:S(2)}) %collective-permute-start.4) | collective-permute-done | bytes 172064 | tf_op jit(solution)/shard_map/ppermute | solution.py:84
  23.1 3.4 %collective-permute-start.13 = (bf16[2,128,768]{2,1,0:T(8,128)(2,1)S(1)}, bf16[2,128,768]{2,1,0:T(8,128)(2,1)S(1)}, u32[]{:S(2)}, u32[]{:S(2)}) collective-permute-start(bf16[2,128,768]{2,1,0:T(8,128)(2,1)S(1)} %pad_maximum_fusion.9), channel_id=1, source_target_pairs={{0,8},{1,5},{2,10},{3,7},{4,12},{5,1},{6,14},{7,3},{8,0},{9,13},{1... | collective-permute-start | bytes 1179656 | tf_op jit(solution)/shard_map/ppermute | solution.py:84
  26.6 12.3 %collective-permute-done.5 = bf16[208,768]{1,0:T(8,128)(2,1)S(1)} collective-permute-done((bf16[208,768]{1,0:T(8,128)(2,1)S(1)}, bf16[208,768]{1,0:T(8,128)(2,1)S(1)}, u32[]{:S(2)}, u32[]{:S(2)}) %collective-permute-start.5) | collective-permute-done | bytes 319520 | tf_op jit(solution)/shard_map/ppermute | solution.py:84
  44.0 9.7 %collective-permute-done.7 = bf16[400,768]{1,0:T(8,128)(2,1)S(1)} collective-permute-done((bf16[400,768]{1,0:T(8,128)(2,1)}, bf16[400,768]{1,0:T(8,128)(2,1)S(1)}, u32[]{:S(2)}, u32[]{:S(2)}) %collective-permute-start.7) | collective-permute-done | bytes 614432 | tf_op jit(solution)/shard_map/ppermute | solution.py:84
  56.8 8.2 %collective-permute-done.14 = bf16[4,128,768]{2,1,0:T(8,128)(2,1)} collective-permute-done((bf16[4,128,768]{2,1,0:T(8,128)(2,1)S(1)}, bf16[4,128,768]{2,1,0:T(8,128)(2,1)}, u32[]{:S(2)}, u32[]{:S(2)}) %collective-permute-start.14) | collective-permute-done | bytes 786464 | tf_op jit(solution)/shard_map/ppermute | solution.py:84
  69.7 7.9 %collective-permute-done.19 = bf16[1,96,768]{2,1,0:T(8,128)(2,1)S(1)} collective-permute-done((bf16[1,96,768]{2,1,0:T(8,128)(2,1)S(1)}, bf16[1,96,768]{2,1,0:T(8,128)(2,1)S(1)}, u32[]{:S(2)}, u32[]{:S(2)}) %collective-permute-start.19) | collective-permute-done | bytes 147488 | tf_op jit(solution)/shard_map/ppermute | solution.py:84
  82.5 3.9 %collective-permute-done.20 = bf16[2,96,768]{2,1,0:T(8,128)(2,1)S(1)} collective-permute-done((bf16[2,96,768]{2,1,0:T(8,128)(2,1)S(1)}, bf16[2,96,768]{2,1,0:T(8,128)(2,1)S(1)}, u32[]{:S(2)}, u32[]{:S(2)}) %collective-permute-start.20) | collective-permute-done | bytes 294944 | tf_op jit(solution)/shard_map/ppermute | solution.py:84
  91.4 3.2 %project.1.k_ref.v_ref = bf16[2048,768]{1,0:T(8,128)(2,1)S(1)} custom-call(bf16[1024,768]{1,0:T(8,128)(2,1)S(1)} %bitcast.158, bf16[1024,768]{1,0:T(8,128)(2,1)S(1)} %collective-permute-done.15.other_ref, bf16[768,768]{1,0:T(8,128)(2,1)S(1)} %bitcast.151, f32[8,1152]{1,0:T(8,128)S(1)} %get-tuple-element.133.bias_ref), custom_call_target="tpu_custom_call" | custom-call | flops 2415919104 | bytes 6291456 | tf_op jit(solution)/shard_map/project/pallas_call | solution.py:289
  94.7 4.7 %collective-permute-done.21 = bf16[4,96,768]{2,1,0:T(8,128)(2,1)S(1)} collective-permute-done((bf16[4,96,768]{2,1,0:T(8,128)(2,1)S(1)}, bf16[4,96,768]{2,1,0:T(8,128)(2,1)S(1)}, u32[]{:S(2)}, u32[]{:S(2)}) %collective-permute-start.21) | collective-permute-done | bytes 589856 | tf_op jit(solution)/shard_map/ppermute | solution.py:84
  102.8 8.7 %attend.1 = (f32[256,384]{1,0:T(8,128)S(1)}, f32[3,8,256]{2,1,0:T(8,128)S(1)}) custom-call(bf16[256,384]{1,0:T(8,128)(2,1)S(1)} %fusion.q_ref, bf16[2048,768]{1,0:T(8,128)(2,1)S(1)} %project.1.k_ref.v_ref, bf16[2048,768]{1,0:T(8,128)(2,1)S(1)} %project.1.k_ref.v_ref, bf16[2048,128]{1,0:T(8,128)(2,1)S(1)} %broadcast_in_dim.55.mask_ref), custom_call_target="tpu_custom_call" | custom-call | flops 3221225472 | bytes 3145728 | tf_op jit(solution)/shard_map/attend/pallas_call | solution.py:330
  115.6 7.4 %collective-permute-done.22.other_ref = bf16[8,96,768]{2,1,0:T(8,128)(2,1)S(1)} collective-permute-done((bf16[8,96,768]{2,1,0:T(8,128)(2,1)S(1)}, bf16[8,96,768]{2,1,0:T(8,128)(2,1)S(1)}, u32[]{:S(2)}, u32[]{:S(2)}) %collective-permute-start.22) | collective-permute-done | bytes 1179680 | tf_op jit(solution)/shard_map/ppermute | solution.py:84
  150.4 3.6 %attend_back.3 = (bf16[256,128]{1,0:T(8,128)(2,1)S(1)}, bf16[2048,128]{1,0:T(8,128)(2,1)S(1)}, bf16[2048,128]{1,0:T(8,128)(2,1)S(1)}, f32[8,128]{1,0:T(8,128)S(1)}) custom-call(bf16[256,384]{1,0:T(8,128)(2,1)S(1)} %copy-done.49, bf16[2048,768]{1,0:T(8,128)(2,1)S(1)} %copy-done.51, bf16[2048,768]{1,0:T(8,128)(2,1)S(1)} %copy-done.51, ...), custom_call_target="tpu_custom_call" | custom-call | flops 2684354560 | bytes 2097152 | tf_op jit(solution)/shard_map/attend_back/pallas_call | solution.py:392
  156.0 3.6 %attend_back.5 = (bf16[256,128]{1,0:T(8,128)(2,1)S(1)}, bf16[2048,128]{1,0:T(8,128)(2,1)S(1)}, bf16[2048,128]{1,0:T(8,128)(2,1)S(1)}, f32[8,128]{1,0:T(8,128)S(1)}) custom-call(bf16[256,384]{1,0:T(8,128)(2,1)S(1)} %copy-done.49, bf16[2048,768]{1,0:T(8,128)(2,1)S(1)} %copy-done.51, bf16[2048,768]{1,0:T(8,128)(2,1)S(1)} %copy-done.51, ...), custom_call_target="tpu_custom_call" | custom-call | flops 2684354560 | bytes 2097152 | tf_op jit(solution)/shard_map/attend_back/pallas_call | solution.py:392
  159.6 3.6 %attend_back.4 = (bf16[256,128]{1,0:T(8,128)(2,1)S(1)}, bf16[2048,128]{1,0:T(8,128)(2,1)S(1)}, bf16[2048,128]{1,0:T(8,128)(2,1)S(1)}, f32[8,128]{1,0:T(8,128)S(1)}) custom-call(bf16[256,384]{1,0:T(8,128)(2,1)S(1)} %copy-done.49, bf16[2048,768]{1,0:T(8,128)(2,1)S(1)} %copy-done.51, bf16[2048,768]{1,0:T(8,128)(2,1)S(1)} %copy-done.51, ...), custom_call_target="tpu_custom_call" | custom-call | flops 2684354560 | bytes 2097152 | tf_op jit(solution)/shard_map/attend_back/pallas_call | solution.py:392
  170.7 4.6 %keys_weights.1 = (bf16[8,96,768]{2,1,0:T(8,128)(2,1)S(1)}, bf16[8,96,768]{2,1,0:T(8,128)(2,1)S(1)}) custom-call(s32[16]{0:T(128)S(1)} %and_select_fusion.table_ref, bf16[1024,768]{1,0:T(8,128)(2,1)S(1)} %bitcast.159, bf16[1024,768]{1,0:T(8,128)(2,1)S(1)} %copy-done.45, bf16[16,48,384]{2,1,0:T(8,128)(2,1)S(1)} %bitcast.179, ...), custom_call_target="tpu_custom_call" | custom-call | flops 2415919104 | bytes 6291456 | tf_op jit(solution)/shard_map/keys_weights/pallas_call | solution.py:526
  180.4 16.9 %collective-permute-done.30.got_ref = bf16[4,128,768]{2,1,0:T(8,128)(2,1)S(1)} collective-permute-done((bf16[4,128,768]{2,1,0:T(8,128)(2,1)S(1)}, bf16[4,128,768]{2,1,0:T(8,128)(2,1)S(1)}, u32[]{:S(2)}, u32[]{:S(2)}) %collective-permute-start.30) | collective-permute-done | bytes 786464 | tf_op jit(solution)/shard_map/ppermute | solution.py:84
  200.1 2.7 %collective-permute-done.36.got_ref = bf16[784,768]{1,0:T(8,128)(2,1)S(1)} collective-permute-done((bf16[784,768]{1,0:T(8,128)(2,1)S(1)}, bf16[784,768]{1,0:T(8,128)(2,1)S(1)}, u32[]{:S(2)}, u32[]{:S(2)}) %collective-permute-start.36) | collective-permute-done | bytes 1204256 | tf_op jit(solution)/shard_map/ppermute | solution.py:84
  203.1 3.3 %collective-permute-start.37 = (bf16[400,768]{1,0:T(8,128)(2,1)S(1)}, bf16[400,768]{1,0:T(8,128)(2,1)S(1)}, u32[]{:S(2)}, u32[]{:S(2)}) collective-permute-start(bf16[400,768]{1,0:T(8,128)(2,1)S(1)} %get-tuple-element.195), channel_id=1, source_target_pairs={{0,2},{1,17},{2,0},{3,19},{4,6},{5,21},{6,4},{7,23},{8,10},{9,25},... | collective-permute-start | bytes 1843208 | tf_op jit(solution)/shard_map/ppermute | solution.py:84
  206.6 14.3 %collective-permute-done.31.got_ref = bf16[2,128,768]{2,1,0:T(8,128)(2,1)S(1)} collective-permute-done((bf16[2,128,768]{2,1,0:T(8,128)(2,1)S(1)}, bf16[2,128,768]{2,1,0:T(8,128)(2,1)S(1)}, u32[]{:S(2)}, u32[]{:S(2)}) %collective-permute-start.31) | collective-permute-done | bytes 393248 | tf_op jit(solution)/shard_map/ppermute | solution.py:84
  223.3 6.3 %collective-permute-done.47.got_ref = bf16[1,96,768]{2,1,0:T(8,128)(2,1)S(1)} collective-permute-done((bf16[1,96,768]{2,1,0:T(8,128)(2,1)S(1)}, bf16[1,96,768]{2,1,0:T(8,128)(2,1)S(1)}, u32[]{:S(2)}, u32[]{:S(2)}) %collective-permute-start.47) | collective-permute-done | bytes 147488 | tf_op jit(solution)/shard_map/ppermute | solution.py:84
  231.4 5.8 %collective-permute-done.43.got_ref = bf16[1,96,768]{2,1,0:T(8,128)(2,1)S(1)} collective-permute-done((bf16[1,96,768]{2,1,0:T(8,128)(2,1)S(1)}, bf16[1,96,768]{2,1,0:T(8,128)(2,1)S(1)}, u32[]{:S(2)}, u32[]{:S(2)}) %collective-permute-start.43) | collective-permute-done | bytes 147488 | tf_op jit(solution)/shard_map/ppermute | solution.py:84
  239.1 9.2 %collective-permute-done.38.got_ref = bf16[208,768]{1,0:T(8,128)(2,1)S(1)} collective-permute-done((bf16[208,768]{1,0:T(8,128)(2,1)S(1)}, bf16[208,768]{1,0:T(8,128)(2,1)S(1)}, u32[]{:S(2)}, u32[]{:S(2)}) %collective-permute-start.38) | collective-permute-done | bytes 319520 | tf_op jit(solution)/shard_map/ppermute | solution.py:84
  248.6 7.7 %collective-permute-done.39.got_ref = bf16[112,768]{1,0:T(8,128)(2,1)S(1)} collective-permute-done((bf16[112,768]{1,0:T(8,128)(2,1)S(1)}, bf16[112,768]{1,0:T(8,128)(2,1)S(1)}, u32[]{:S(2)}, u32[]{:S(2)}) %collective-permute-start.39) | collective-permute-done | bytes 172064 | tf_op jit(solution)/shard_map/ppermute | solution.py:84
  (315 shorter events, 100.9 us)
Async XLA Ops:
  8.9 14.1 %collective-permute-start.12 = (bf16[1,128,768]{2,1,0:T(8,128)(2,1)}, bf16[1,128,768]{2,1,0:T(8,128)(2,1)S(1)}, u32[]{:S(2)}, u32[]{:S(2)}) collective-permute-start(bf16[1,128,768]{2,1,0:T(8,128)(2,1)} %param.22), channel_id=1, source_target_pairs={{0,2},{1,3},{2,0},{3,1},{4,6},{5,7},{6,4},{7,5},{8,10},{9,11},{10,... | collective-permute-start | bytes 589832 | tf_op jit(solution)/shard_map/ppermute | solution.py:84
  21.1 17.8 %collective-permute-start.5 = (bf16[208,768]{1,0:T(8,128)(2,1)S(1)}, bf16[208,768]{1,0:T(8,128)(2,1)S(1)}, u32[]{:S(2)}, u32[]{:S(2)}) collective-permute-start(bf16[208,768]{1,0:T(8,128)(2,1)S(1)} %pad_maximum_fusion.11), channel_id=1, source_target_pairs={{0,4},{1,9},{2,6},{3,11},{4,0},{5,13},{6,2},{7,15},{8,12},{9,1},{1... | collective-permute-start | bytes 958472 | tf_op jit(solution)/shard_map/ppermute | solution.py:84
  23.1 18.3 %collective-permute-start.13 = (bf16[2,128,768]{2,1,0:T(8,128)(2,1)S(1)}, bf16[2,128,768]{2,1,0:T(8,128)(2,1)S(1)}, u32[]{:S(2)}, u32[]{:S(2)}) collective-permute-start(bf16[2,128,768]{2,1,0:T(8,128)(2,1)S(1)} %pad_maximum_fusion.9), channel_id=1, source_target_pairs={{0,8},{1,5},{2,10},{3,7},{4,12},{5,1},{6,14},{7,3},{8,0},{9,13},{1... | collective-permute-start | bytes 1179656 | tf_op jit(solution)/shard_map/ppermute | solution.py:84
  40.5 13.2 %collective-permute-start.7 = (bf16[400,768]{1,0:T(8,128)(2,1)}, bf16[400,768]{1,0:T(8,128)(2,1)S(1)}, u32[]{:S(2)}, u32[]{:S(2)}) collective-permute-start(bf16[400,768]{1,0:T(8,128)(2,1)} %pad_maximum_fusion.6), channel_id=1, source_target_pairs={{0,2},{1,17},{2,0},{3,19},{4,6},{5,21},{6,4},{7,23},{8,10},{9,25},... | collective-permute-start | bytes 1843208 | tf_op jit(solution)/shard_map/ppermute | solution.py:84
  40.7 61.3 %collective-permute-start.11 = (bf16[128,768]{1,0:T(8,128)(2,1)S(1)}, bf16[128,768]{1,0:T(8,128)(2,1)S(1)}, u32[]{:S(2)}, u32[]{:S(2)}) collective-permute-start(bf16[128,768]{1,0:T(8,128)(2,1)S(1)} %bitcast.146), channel_id=1, source_target_pairs={{0,1},{1,0},{2,3},{3,2},{4,5},{5,4},{6,7},{7,6},{8,9},{9,8},{10,11... | collective-permute-start | bytes 589832 | tf_op jit(solution)/shard_map/ppermute | solution.py:84
  41.5 23.5 %collective-permute-start.14 = (bf16[4,128,768]{2,1,0:T(8,128)(2,1)S(1)}, bf16[4,128,768]{2,1,0:T(8,128)(2,1)}, u32[]{:S(2)}, u32[]{:S(2)}) collective-permute-start(bf16[4,128,768]{2,1,0:T(8,128)(2,1)S(1)} %pad_maximum_fusion.5), channel_id=1, source_target_pairs={{0,4},{1,9},{2,6},{3,11},{4,0},{5,13},{6,2},{7,15},{8,12},{9,1},{1... | collective-permute-start | bytes 2359304 | tf_op jit(solution)/shard_map/ppermute | solution.py:84
  42.0 24.3 %collective-permute-start.1 = (bf16[1,96,768]{2,1,0:T(8,128)(2,1)S(1)}, bf16[1,96,768]{2,1,0:T(8,128)(2,1)S(1)}, u32[]{:S(2)}, u32[]{:S(2)}) collective-permute-start(bf16[1,96,768]{2,1,0:T(8,128)(2,1)S(1)} %bitcast.185), channel_id=1, source_target_pairs={{0,8},{1,5},{2,10},{3,7},{4,12},{5,1},{6,14},{7,3},{8,0},{9,13},{1... | collective-permute-start | bytes 442376 | tf_op jit(solution)/shard_map/ppermute | solution.py:84
  55.2 26.2 %collective-permute-start.9 = (bf16[784,768]{1,0:T(8,128)(2,1)}, bf16[784,768]{1,0:T(8,128)(2,1)S(1)}, u32[]{:S(2)}, u32[]{:S(2)}) collective-permute-start(bf16[784,768]{1,0:T(8,128)(2,1)} %constant_dynamic-update-slice_fusion), channel_id=1, source_target_pairs={{0,16},{1,3},{2,18},{3,1},{4,20},{5,7},{6,22},{7,5},{8,24},{9,11},... | collective-permute-start | bytes 3612680 | tf_op jit(solution)/shard_map/ppermute | solution.py:84
  66.3 25.1 %collective-permute-start.15 = (bf16[1024,768]{1,0:T(8,128)(2,1)S(1)}, bf16[1024,768]{1,0:T(8,128)(2,1)S(1)}, u32[]{:S(2)}, u32[]{:S(2)}) collective-permute-start(bf16[1024,768]{1,0:T(8,128)(2,1)S(1)} %bitcast.157), channel_id=1, source_target_pairs={{0,1},{1,0},{2,3},{3,2},{4,5},{5,4},{6,7},{7,6},{8,9},{9,8},{10,11... | collective-permute-start | bytes 4718600 | tf_op jit(solution)/shard_map/ppermute | solution.py:84
  89.4 24.4 %collective-permute-start.17 = (bf16[768,384]{1,0:T(8,128)(2,1)S(1)}, bf16[768,384]{1,0:T(8,128)(2,1)S(1)}, u32[]{:S(2)}, u32[]{:S(2)}) collective-permute-start(bf16[768,384]{1,0:T(8,128)(2,1)S(1)} %bitcast.154), channel_id=1, source_target_pairs={{0,1},{1,0},{2,3},{3,2},{4,5},{5,4},{6,7},{7,6},{8,9},{9,8},{10,11... | collective-permute-start | bytes 1769480 | tf_op jit(solution)/shard_map/ppermute | solution.py:84
  90.5 22.5 %collective-permute-start.10 = (bf16[8,96,768]{2,1,0:T(8,128)(2,1)S(1)}, bf16[8,96,768]{2,1,0:T(8,128)(2,1)S(1)}, u32[]{:S(2)}, u32[]{:S(2)}) collective-permute-start(bf16[8,96,768]{2,1,0:T(8,128)(2,1)S(1)} %pad_maximum_fusion.3.mine_ref), channel_id=1, source_target_pairs={{0,16},{1,3},{2,18},{3,1},{4,20},{5,7},{6,22},{7,5},{8,24},{9,11},... | collective-permute-start | bytes 3538952 | tf_op jit(solution)/shard_map/ppermute | solution.py:84
  99.5 23.6 %collective-permute-start.22 = (bf16[8,96,768]{2,1,0:T(8,128)(2,1)S(1)}, bf16[8,96,768]{2,1,0:T(8,128)(2,1)S(1)}, u32[]{:S(2)}, u32[]{:S(2)}) collective-permute-start(bf16[8,96,768]{2,1,0:T(8,128)(2,1)S(1)} %pad_maximum_fusion.4.mine_ref), channel_id=1, source_target_pairs={{0,16},{1,3},{2,18},{3,1},{4,20},{5,7},{6,22},{7,5},{8,24},{9,11},... | collective-permute-start | bytes 3538952 | tf_op jit(solution)/shard_map/ppermute | solution.py:84
  139.8 16.3 %collective-permute-start.27 = (bf16[8,96,768]{2,1,0:T(8,128)(2,1)S(1)}, bf16[8,96,768]{2,1,0:T(8,128)(2,1)S(1)}, u32[]{:S(2)}, u32[]{:S(2)}) collective-permute-start(bf16[8,96,768]{2,1,0:T(8,128)(2,1)S(1)} %get-tuple-element.160), channel_id=1, source_target_pairs={{0,16},{1,3},{2,18},{3,1},{4,20},{5,7},{6,22},{7,5},{8,24},{9,11},... | collective-permute-start | bytes 3538952 | tf_op jit(solution)/shard_map/ppermute | solution.py:84
  146.7 22.5 %collective-permute-start.33 = (bf16[8,96,768]{2,1,0:T(8,128)(2,1)S(1)}, bf16[8,96,768]{2,1,0:T(8,128)(2,1)S(1)}, u32[]{:S(2)}, u32[]{:S(2)}) collective-permute-start(bf16[8,96,768]{2,1,0:T(8,128)(2,1)S(1)} %get-tuple-element.179), channel_id=1, source_target_pairs={{0,16},{1,3},{2,18},{3,1},{4,20},{5,7},{6,22},{7,5},{8,24},{9,11},... | collective-permute-start | bytes 3538952 | tf_op jit(solution)/shard_map/ppermute | solution.py:84
  149.9 15.4 %collective-permute-start.34 = (bf16[768,384]{1,0:T(8,128)(2,1)S(1)}, bf16[768,384]{1,0:T(8,128)(2,1)S(1)}, u32[]{:S(2)}, u32[]{:S(2)}) collective-permute-start(bf16[768,384]{1,0:T(8,128)(2,1)S(1)} %get-tuple-element.184), channel_id=1, source_target_pairs={{0,1},{1,0},{2,3},{3,2},{4,5},{5,4},{6,7},{7,6},{8,9},{9,8},{10,11... | collective-permute-start | bytes 1769480 | tf_op jit(solution)/shard_map/ppermute | solution.py:84
  175.4 27.4 %collective-permute-start.36 = (bf16[784,768]{1,0:T(8,128)(2,1)S(1)}, bf16[784,768]{1,0:T(8,128)(2,1)S(1)}, u32[]{:S(2)}, u32[]{:S(2)}) collective-permute-start(bf16[784,768]{1,0:T(8,128)(2,1)S(1)} %pad_maximum_fusion.1), channel_id=1, source_target_pairs={{0,16},{1,3},{2,18},{3,1},{4,20},{5,7},{6,22},{7,5},{8,24},{9,11},... | collective-permute-start | bytes 3612680 | tf_op jit(solution)/shard_map/ppermute | solution.py:84
  177.2 20.1 %collective-permute-start.30 = (bf16[4,128,768]{2,1,0:T(8,128)(2,1)S(1)}, bf16[4,128,768]{2,1,0:T(8,128)(2,1)S(1)}, u32[]{:S(2)}, u32[]{:S(2)}) collective-permute-start(bf16[4,128,768]{2,1,0:T(8,128)(2,1)S(1)} %get-tuple-element.173), channel_id=1, source_target_pairs={{0,4},{1,9},{2,6},{3,11},{4,0},{5,13},{6,2},{7,15},{8,12},{9,1},{1... | collective-permute-start | bytes 2359304 | tf_op jit(solution)/shard_map/ppermute | solution.py:84
  177.9 20.6 %collective-permute-start.45 = (bf16[4,96,768]{2,1,0:T(8,128)(2,1)S(1)}, bf16[4,96,768]{2,1,0:T(8,128)(2,1)S(1)}, u32[]{:S(2)}, u32[]{:S(2)}) collective-permute-start(bf16[4,96,768]{2,1,0:T(8,128)(2,1)S(1)} %get-tuple-element.224), channel_id=1, source_target_pairs={{0,2},{1,17},{2,0},{3,19},{4,6},{5,21},{6,4},{7,23},{8,10},{9,25},... | collective-permute-start | bytes 1769480 | tf_op jit(solution)/shard_map/ppermute | solution.py:84
  179.8 26.6 %collective-permute-start.41 = (bf16[4,96,768]{2,1,0:T(8,128)(2,1)S(1)}, bf16[4,96,768]{2,1,0:T(8,128)(2,1)S(1)}, u32[]{:S(2)}, u32[]{:S(2)}) collective-permute-start(bf16[4,96,768]{2,1,0:T(8,128)(2,1)S(1)} %get-tuple-element.213), channel_id=1, source_target_pairs={{0,2},{1,17},{2,0},{3,19},{4,6},{5,21},{6,4},{7,23},{8,10},{9,25},... | collective-permute-start | bytes 1769480 | tf_op jit(solution)/shard_map/ppermute | solution.py:84
  197.5 23.5 %collective-permute-start.31 = (bf16[2,128,768]{2,1,0:T(8,128)(2,1)S(1)}, bf16[2,128,768]{2,1,0:T(8,128)(2,1)S(1)}, u32[]{:S(2)}, u32[]{:S(2)}) collective-permute-start(bf16[2,128,768]{2,1,0:T(8,128)(2,1)S(1)} %get-tuple-element.175), channel_id=1, source_target_pairs={{0,8},{1,5},{2,10},{3,7},{4,12},{5,1},{6,14},{7,3},{8,0},{9,13},{1... | collective-permute-start | bytes 1179656 | tf_op jit(solution)/shard_map/ppermute | solution.py:84
  198.7 23.8 %collective-permute-start.46 = (bf16[2,96,768]{2,1,0:T(8,128)(2,1)S(1)}, bf16[2,96,768]{2,1,0:T(8,128)(2,1)S(1)}, u32[]{:S(2)}, u32[]{:S(2)}) collective-permute-start(bf16[2,96,768]{2,1,0:T(8,128)(2,1)S(1)} %get-tuple-element.227), channel_id=1, source_target_pairs={{0,4},{1,9},{2,6},{3,11},{4,0},{5,13},{6,2},{7,15},{8,12},{9,1},{1... | collective-permute-start | bytes 884744 | tf_op jit(solution)/shard_map/ppermute | solution.py:84
  200.1 30.5 %collective-permute-start.28 = (f32[128,768]{1,0:T(8,128)S(1)}, f32[128,768]{1,0:T(8,128)S(1)}, u32[]{:S(2)}, u32[]{:S(2)}) collective-permute-start(f32[128,768]{1,0:T(8,128)S(1)} %get-tuple-element.165), channel_id=1, source_target_pairs={{0,1},{1,0},{2,3},{3,2},{4,5},{5,4},{6,7},{7,6},{8,9},{9,8},{10,11... | collective-permute-start | bytes 1179656 | tf_op jit(solution)/shard_map/ppermute | solution.py:84
  203.1 34.2 %collective-permute-start.37 = (bf16[400,768]{1,0:T(8,128)(2,1)S(1)}, bf16[400,768]{1,0:T(8,128)(2,1)S(1)}, u32[]{:S(2)}, u32[]{:S(2)}) collective-permute-start(bf16[400,768]{1,0:T(8,128)(2,1)S(1)} %get-tuple-element.195), channel_id=1, source_target_pairs={{0,2},{1,17},{2,0},{3,19},{4,6},{5,21},{6,4},{7,23},{8,10},{9,25},... | collective-permute-start | bytes 1843208 | tf_op jit(solution)/shard_map/ppermute | solution.py:84
  206.5 23.8 %collective-permute-start.42 = (bf16[2,96,768]{2,1,0:T(8,128)(2,1)S(1)}, bf16[2,96,768]{2,1,0:T(8,128)(2,1)S(1)}, u32[]{:S(2)}, u32[]{:S(2)}) collective-permute-start(bf16[2,96,768]{2,1,0:T(8,128)(2,1)S(1)} %get-tuple-element.216), channel_id=1, source_target_pairs={{0,4},{1,9},{2,6},{3,11},{4,0},{5,13},{6,2},{7,15},{8,12},{9,1},{1... | collective-permute-start | bytes 884744 | tf_op jit(solution)/shard_map/ppermute | solution.py:84
  (82 other events, 437.1 us)

commit v2 on v1

v2 whole, which is shorter than its diff:
```python
import functools

import jax
import jax.numpy as jnp
import numpy as np
from jax import lax
from jax.experimental import pallas as pl
from jax.experimental.pallas import tpu as pltpu
from jax.sharding import PartitionSpec as P

HEADS = 12
HEAD_DIM = 64
EPSILON = 1e-12
MASKED = -1000000000.0
EVERY = ("seq", "ctx")
F32 = jnp.float32
BF16 = jnp.bfloat16
VMEM = pl.BlockSpec(memory_space=pltpu.VMEM)
SMEM = pl.BlockSpec(memory_space=pltpu.SMEM)
QUERY_B, VALUE_B, OUTPUT_B, GAIN_1, SHIFT_1, REDUCE_B, GAIN_2, SHIFT_2, EXPAND_B = range(9)
VECTOR_ROWS = 16
SMALL_BYTES = 16 << 20
COST = pl.CostEstimate(flops=1000, bytes_accessed=1000, transcendentals=0)
FORWARD = ('XBADbxad|BAba|BADXbadx|BDXbd|', 'xAD', '', 'ad|')
BACKWARD = ('', '', 'a|A', 'da|DX', 'BA|dab|DABx|aXdbBDxd|Xb|Bx|b')
TOKEN_NEAR = 0
TOKEN_TURN = 'yba'
WEIGHT_TURNS = {'D': (1, 0, 3, 2), 'A': (3, 2, 1, 0), 'B': (3, 2, 1, 0)}
WAITS = (False, False, False, False, False, False)
FIRST_WAITS = False
INPUTS_FIRST = False
STRICT = (True, False)


def dot(left, right):
    return jnp.dot(left, right, preferred_element_type=F32)


def contract_rows(left, right):
    return lax.dot_general(left, right, (((0,), (0,)), ((), ())), preferred_element_type=F32)


def times_transpose(left, right):
    return lax.dot_general(left, right, (((1,), (1,)), ((), ())), preferred_element_type=F32)


def shaped(shape, dtype):
    return jax.ShapeDtypeStruct(tuple(shape), dtype)


def after(array, *earlier):
    return lax.optimization_barrier((array, *earlier))[0]


def in_hbm(array):
    return pltpu.with_memory_space_constraint(array, pltpu.HBM)


class Far:
    def __init__(self, array):
        self.array = array


def fetching(kernel, scalars, far, count, *refs):
    inputs, rest = list(refs[:count]), refs[count : len(refs) - len(far) - 1]
    held, sems = refs[len(refs) - len(far) - 1 : -1], refs[-1]
    copies = [pltpu.make_async_copy(inputs[at], room, sems.at[i]) for i, (at, room) in enumerate(zip(far, held))]
    for copy in copies:
        copy.start()
    for copy in copies:
        copy.wait()
    for at, room in zip(far, held):
        inputs[at] = room
    kernel(*inputs, *rest)


def call(kernel, name, outs, *args, scalars=0, scratch=(), room=16, stored=()):
    many = isinstance(outs, (tuple, list))
    far = [i for i, a in enumerate(args) if isinstance(a, Far)]
    args = [a.array if isinstance(a, Far) else a for a in args]
    flat = tuple(outs) if many else (outs,)
    small = sum(a.size * a.dtype.itemsize for a in (*args, *flat)) < SMALL_BYTES
    specs = [SMEM] * scalars + [VMEM] * (len(args) - scalars)
    scratch = list(scratch)
    if far and small:
        kernel = functools.partial(fetching, kernel, scalars, far, len(args))
        for at in far:
            specs[at] = pl.BlockSpec(memory_space=pltpu.HBM)
            args[at] = pltpu.with_memory_space_constraint(args[at], pltpu.HBM)
            scratch.append(pltpu.VMEM(args[at].shape, args[at].dtype))
        scratch.append(pltpu.SemaphoreType.DMA((len(far),)))
    out_specs = [VMEM] * len(flat)
    for at in stored:
        out_specs[at] = pl.BlockSpec(memory_space=pltpu.HBM)
        flat = flat[:at] + (pltpu.HBM(flat[at].shape, flat[at].dtype),) + flat[at + 1 :]
    return pl.pallas_call(
        kernel,
        out_shape=flat if many else flat[0],
        in_specs=specs,
        out_specs=tuple(out_specs) if many else out_specs[0],
        scratch_shapes=scratch,
        cost_estimate=COST,
        compiler_params=pltpu.CompilerParams(vmem_limit_bytes=room << 20 if small else None),
        name=name,
    )(*args)


def limit(tokens, mebibytes):
    return pltpu.CompilerParams(vmem_limit_bytes=mebibytes << 20 if tokens <= 4096 else None)


class Place:
    def __init__(self):
        self.ctx = lax.axis_size("ctx")
        self.count = lax.axis_size("seq") * self.ctx
        self.bits = self.count.bit_length() - 1
        self.context = lax.axis_index("ctx")
        self.number = lax.axis_index("seq") * self.ctx + self.context
        self.core = self.number & 1
        top = self.bits - 1
        middle = list(range(2, top))
        self.weight_stages = list(zip(middle[::-1], middle)) + [(1, top), (top, 1)]
        self.token_stages = list(zip(middle[::-1], middle))
        self.token_stages.insert(min(TOKEN_NEAR, len(middle)), (1, 1))

    def swap(self, array, even, odd=None):
        odd = even if odd is None else odd
        pairs = [(i, i ^ (1 << (odd if i & 1 else even))) for i in range(self.count)]
        return lax.ppermute(array, EVERY, pairs)

    def others(self, stages, core):
        masks = [0]
        for stage in stages:
            masks = masks + [m ^ (1 << stage[core]) for m in masks]
        return np.array(masks, np.int32)


class Order:
    def __init__(self, place, strict):
        self.place = place
        self.strict = strict
        self.last = ()
        self.ended = ()

    def close(self):
        if self.ended:
            self.last, self.ended = self.ended, ()

    def wait(self, array):
        return after(array, *self.last) if self.last else array

    def start(self, array, stage):
        return self.place.swap(self.wait(array), *stage)

    def done(self, got):
        used = self.wait(got) if self.strict else got
        self.ended += (got,)
        return used

    def ran(self, out):
        self.ended += (out,)
        return out


class Gather:
    def __init__(self, order, blocks, stages, vectors=None):
        self.order, self.held, self.stages, self.vectors = order, blocks, list(stages), vectors
        self.got = None

    def start(self):
        sent = self.held if self.vectors is None else jnp.concatenate([self.held, self.vectors])
        self.got = self.order.start(sent, self.stages.pop(0))

    def done(self):
        self.got = self.order.done(self.got)
        got = self.got
        if self.vectors is not None:
            self.vectors = self.vectors + got[-VECTOR_ROWS:]
            got = got[:-VECTOR_ROWS]
        if self.stages:
            self.held = jnp.concatenate([self.held, got])


class Scatter:
    def __init__(self, order, keep, send, stages, vectors=None, turn=None):
        self.order, self.keep, self.send, self.vectors = order, keep, send, vectors
        turn = list(range(len(stages)))[::-1] if turn is None else list(turn)
        self.stages = [stages[i] for i in turn]
        left = sorted(turn)
        self.bits = []
        for i in turn:
            self.bits.append(left.index(i))
            left.remove(i)
        self.bits.pop(0)

    def start(self):
        self.got = self.order.start(self.send, self.stages.pop(0))

    def done(self, *earlier):
        got = self.order.done(self.got)
        got = after(got, *earlier) if earlier else got
        last = not self.stages
        if self.vectors is None:
            out = fold(self.keep, got, None if last else self.bits.pop(0))
            self.keep, self.send = (out, None) if last else out
        elif last:
            self.keep, self.vectors = fold_vectors(self.keep, got, self.vectors, None)
        else:
            bit = (self.bits.pop(0), 2 << len(self.bits))
            self.keep, self.send, self.vectors = fold_vectors(self.keep, got, self.vectors, bit)


def play(events, chains):
    for event in events:
        if event == "|":
            next(iter(chains.values())).order.close()
            continue
        chain = chains[event.upper()]
        if event.isupper():
            chain.start()
        else:
            chain.done()


def plain_events(chains):
    events = ""
    left = {name: len(chain.stages) for name, chain in chains.items()}
    while any(left.values()):
        names = [n for n in left if left[n]]
        events += "".join(names) + "".join(names).lower() + "|"
        for n in names:
            left[n] -= 1
    return events


def prepare_kernel(units, number_ref, *refs):
    count = EXPAND_B + 6
    in_refs, outs = refs[:count], refs[count : count + 5]
    rows_ref, split_ref = refs[count + 5 : count + 7]
    held_refs, sems = refs[count + 7 : -1], refs[-1]
    copies = [pltpu.make_async_copy(i, h, sems.at[at]) for at, (i, h) in enumerate(zip(in_refs, held_refs))]
    for copy in copies:
        copy.start()
    key_mine_ref, key_other_ref, expand_mine_ref, expand_other_ref, vectors_ref = outs
    number = number_ref[0]
    even = number % 2 == 0
    rows_ref[...] = jnp.zeros_like(rows_ref)
    for copy in copies:
        copy.wait()
    weights, expand_ref, vectors = held_refs[:4], held_refs[4], held_refs[5:]
    own, width = weights[0].shape
    side = width // 2
    for i, ref in enumerate(weights):
        first, second = ref[:, :side], ref[:, side:]
        at = slice(i % 2 * side, (i % 2 + 1) * side)
        key_mine_ref[i // 2, :, at] = jnp.where(even, first, second)
        key_other_ref[i // 2, :, at] = jnp.where(even, second, first)
    for i in range(expand_ref.shape[1] // units):
        at = i // 2 * units
        split_ref[i % 2, :, at : at + units] = expand_ref[:, i * units : (i + 1) * units].astype(F32)
    for i in range(expand_mine_ref.shape[0]):
        at = slice(i * width, (i + 1) * width)
        first, second = split_ref[0, :, at], split_ref[1, :, at]
        expand_mine_ref[i] = jnp.where(even, first, second).astype(BF16)
        expand_other_ref[i] = jnp.where(even, second, first).astype(BF16)
    for i, ref in enumerate(vectors[:-1]):
        rows_ref[i : i + 1, :own] = ref[...].astype(F32)
    rows_ref[EXPAND_B : EXPAND_B + 1, :units] = vectors[-1][...].astype(F32)
    first = pltpu.roll(rows_ref[:8, :], number * own, 1)
    offset = (number // 2) * units
    second = pltpu.roll(rows_ref[8:, :], offset % width, 1)
    here = lax.broadcasted_iota(jnp.int32, second.shape, 0) == offset // width
    second = jnp.where(here, jnp.broadcast_to(second[:1], second.shape), 0.0)
    vectors_ref[...] = jnp.concatenate([first, second], 0).astype(BF16)


def prepare(number, weights, expand, vectors):
    own, width = weights[0].shape
    units = vectors[-1].shape[0]
    arrays = [*weights, expand, *[v.reshape(1, -1) for v in vectors]]
    arrays = [pltpu.with_memory_space_constraint(v, pltpu.HBM) for v in arrays]
    times = expand.shape[1] // 2 // width
    halves = [shaped((2, own, width), BF16)] * 2 + [shaped((times, own, width), BF16)] * 2
    return pl.pallas_call(
        functools.partial(prepare_kernel, units),
        out_shape=(*halves, shaped((VECTOR_ROWS, width), BF16)),
        in_specs=[SMEM] + [pl.BlockSpec(memory_space=pltpu.HBM)] * len(arrays),
        out_specs=(VMEM,) * 5,
        scratch_shapes=[
            pltpu.VMEM((VECTOR_ROWS, width), F32),
            pltpu.VMEM((2, own, expand.shape[1] // 2), F32),
            *[pltpu.VMEM(v.shape, v.dtype) for v in arrays],
            pltpu.SemaphoreType.DMA((len(arrays),)),
        ],
        cost_estimate=COST,
        compiler_params=pltpu.CompilerParams(vmem_limit_bytes=8 << 20),
        name="prepare",
    )(number, *arrays)


def unpack_vectors(number_ref, sums_ref, out_refs):
    own, units, width = out_refs[0].shape[1], out_refs[-1].shape[1], sums_ref.shape[1]
    number = number_ref[0]
    first = pltpu.roll(sums_ref[:8, :], width - number * own, 1)
    for i, ref in enumerate(out_refs[:-1]):
        ref[...] = first[i : i + 1, :own]
    offset = (number // 2) * units
    here = lax.broadcasted_iota(jnp.int32, (VECTOR_ROWS - 8, width), 0) == offset // width
    row = jnp.sum(jnp.where(here, sums_ref[8:, :], 0.0), axis=0, keepdims=True)
    row = pltpu.roll(jnp.broadcast_to(row, (8, width)), width - offset % width, 1)
    out_refs[-1][...] = row[:1, :units]


def place_attention_kernel(table_ref, core_ref, mine_ref, other_ref, vector_ref, kv_ref, q_ref, o_ref, bias_ref):
    half = kv_ref.shape[0] // 2
    rows, side = q_ref.shape[1], q_ref.shape[2]
    tile = mine_ref.shape[1]
    tiles = rows // tile

    def body(j, carry):
        for ref, at in ((mine_ref, j), (other_ref, j + half)):
            chip = table_ref[at]
            for i in range(tiles):
                to = slice(i * tile, (i + 1) * tile)
                kv_ref[chip, to] = ref[j * (2 * tiles) + i]
                q_ref[chip, to] = ref[j * (2 * tiles) + tiles + i, :, :side]
                o_ref[chip, to] = ref[j * (2 * tiles) + tiles + i, :, side:]
        return carry

    lax.fori_loop(0, half, body, 0)
    values = vector_ref[...].astype(F32)
    values = jnp.where(core_ref[0] == 0, values[:8, :side], values[:8, side:])
    bias_ref[:, :side] = jnp.zeros((8, side), F32)
    bias_ref[:, side : 2 * side] = jnp.broadcast_to(values[VALUE_B : VALUE_B + 1], (8, side))
    bias_ref[:, 2 * side :] = jnp.broadcast_to(values[QUERY_B : QUERY_B + 1], (8, side))


def place_hidden_kernel(table_ref, mine_a_ref, other_a_ref, mine_d_ref, other_d_ref, expand_ref, reduce_ref):
    half = mine_a_ref.shape[0]
    rows, width = expand_ref.shape[1], mine_a_ref.shape[2]

    def body(j, carry):
        for a_ref, d_ref, at in ((mine_a_ref, mine_d_ref, j), (other_a_ref, other_d_ref, j + half)):
            chip = table_ref[at]
            for i in range(expand_ref.shape[2] // width):
                expand_ref[chip, :, i * width : (i + 1) * width] = a_ref[j, i * rows : (i + 1) * rows]
            reduce_ref[chip] = d_ref[j]
        return carry

    lax.fori_loop(0, half, body, 0)


def split_expand_kernel(table_ref, expand_ref, mine_ref, other_ref):
    half = mine_ref.shape[0]
    rows, width = expand_ref.shape[1], mine_ref.shape[2]

    def body(j, carry):
        for ref, at in ((mine_ref, j), (other_ref, j + half)):
            chip = table_ref[at]
            for i in range(expand_ref.shape[2] // width):
                ref[j, i * rows : (i + 1) * rows] = expand_ref[chip, :, i * width : (i + 1) * width]
        return carry

    lax.fori_loop(0, half, body, 0)


def split_reduce_kernel(table_ref, reduce_ref, mine_ref, other_ref):
    half = mine_ref.shape[0]

    def body(j, carry):
        mine_ref[j] = reduce_ref[table_ref[j]]
        other_ref[j] = reduce_ref[table_ref[j + half]]
        return carry

    lax.fori_loop(0, half, body, 0)


def split_attention_kernel(table_ref, kv_ref, q_ref, o_ref, mine_ref, other_ref):
    half = mine_ref.shape[0]
    rows, side = q_ref.shape[1], q_ref.shape[2]

    def body(j, carry):
        for ref, at in ((mine_ref, j), (other_ref, j + half)):
            chip = table_ref[at]
            ref[j, :rows] = kv_ref[chip]
            ref[j, rows:, :side] = q_ref[chip]
            ref[j, rows:, side:] = o_ref[chip]
        return carry

    lax.fori_loop(0, half, body, 0)


def fold_kernel(bit, keep_ref, got_ref, *out_refs):
    if len(out_refs) == 1:
        out_refs[0][...] = keep_ref[...].astype(F32) + got_ref[...].astype(F32)
        return
    low = 1 << bit
    for j in range(out_refs[0].shape[0]):
        block = j % low + j // low * 2 * low
        for i, ref in enumerate(out_refs):
            at = block + i * low
            ref[j] = (keep_ref[at].astype(F32) + got_ref[at].astype(F32)).astype(BF16)


def fold(keep, got, bit):
    blocks = keep.shape[0]
    out = shaped(keep.shape, F32) if blocks == 1 else (shaped((blocks // 2,) + keep.shape[1:], BF16),) * 2
    return call(functools.partial(fold_kernel, bit), "fold", out, keep, got)


def fold_vectors_kernel(bit, keep_ref, got_ref, vector_ref, *out_refs):
    rows = keep_ref.shape[0]
    vectors = vector_ref[...] + got_ref[rows:, :].astype(F32)
    out_refs[-1][...] = vectors
    if len(out_refs) == 2:
        out_refs[0][...] = keep_ref[...].astype(F32) + got_ref[:rows, :].astype(F32)
        return
    bit, blocks = bit
    size, low = rows // blocks, 1 << bit
    for j in range(blocks // 2):
        block = j % low + j // low * 2 * low
        for i in range(2):
            at = (block + i * low) * size
            total = keep_ref[at : at + size, :].astype(F32) + got_ref[at : at + size, :].astype(F32)
            out_refs[i][j * size : (j + 1) * size, :] = total.astype(BF16)
    out_refs[1][rows // 2 :, :] = vectors.astype(BF16)


def fold_vectors(keep, got, vectors, bit):
    rows, width = keep.shape
    if bit is None:
        out = (shaped((rows, width), F32), shaped(vectors.shape, F32))
    else:
        out = (
            shaped((rows // 2, width), BF16),
            shaped((rows // 2 + VECTOR_ROWS, width), BF16),
            shaped(vectors.shape, F32),
        )
    return call(functools.partial(fold_vectors_kernel, bit), "fold_vectors", out, keep, got, vectors)


def project_kernel(mine_ref, other_ref, weight_ref, bias_ref, out_ref):
    width = weight_ref.shape[1]
    bias = bias_ref[:1, :width]

    @pl.when(pl.program_id(0) == 0)
    def _():
        out_ref[...] = (dot(mine_ref[...], weight_ref[...]) + bias).astype(BF16)

    @pl.when(pl.program_id(0) == 1)
    def _():
        out_ref[...] = (dot(other_ref[...], weight_ref[...]) + bias).astype(BF16)


def project(mine, other, weight, bias):
    rows, width = mine.shape
    step = min(rows, 512)
    steps = rows // step
    return pl.pallas_call(
        project_kernel,
        out_shape=shaped((2 * rows, width), BF16),
        grid=(2, steps),
        in_specs=[
            pl.BlockSpec((step, width), lambda i, j: (jnp.where(i == 0, j, steps - 1), 0)),
            pl.BlockSpec((step, width), lambda i, j: (jnp.where(i == 0, 0, j), 0)),
            pl.BlockSpec(weight.shape, lambda i, j: (0, 0)),
            pl.BlockSpec(bias.shape, lambda i, j: (0, 0)),
        ],
        out_specs=pl.BlockSpec((step, width), lambda i, j: (i * steps + j, 0)),
        cost_estimate=COST,
        compiler_params=limit(2 * rows, 20),
        name="project",
    )(mine, other, weight, bias)


def head_scores(half, query, key, mask):
    column = lax.broadcasted_iota(jnp.int32, (1, 2 * HEAD_DIM), 1)
    here = (column < HEAD_DIM) if half == 0 else (column >= HEAD_DIM)
    one = (column == HEAD_DIM * (1 - half)).astype(F32).astype(BF16)
    return times_transpose(jnp.where(here, key, mask), jnp.where(here, query, one))


def scaled(query):
    return (query.astype(F32) * 0.125).astype(BF16)


def attend_kernel(q_ref, k_ref, v_ref, mask_ref, out_ref, logs_ref):
    query = scaled(q_ref[...])
    outs = []
    for half in range(2):
        at = slice(half * HEAD_DIM, (half + 1) * HEAD_DIM)
        scores = head_scores(half, query, k_ref[...], mask_ref[...])
        top = jnp.max(scores, axis=0, keepdims=True)
        weights = jnp.exp(scores - top)
        total = jnp.sum(weights, axis=0, keepdims=True)
        outs.append(contract_rows(v_ref[:, at], weights.astype(BF16)) / total)
        logs_ref[0, half : half + 1, :] = top + jnp.log(total)
    out_ref[...] = jnp.transpose(jnp.concatenate(outs, 0))


def attend(query, keys, mask):
    rows, width = query.shape
    tokens = keys.shape[0]
    step = rows if tokens <= 4096 else 128
    pair = 2 * HEAD_DIM
    pairs = width // pair
    spec_q = pl.BlockSpec((step, pair), lambda h, i: (i, h))
    flops = 16 * rows * tokens * width
    return pl.pallas_call(
        attend_kernel,
        out_shape=(shaped((rows, width), F32), shaped((pairs, 8, rows), F32)),
        grid=(pairs, rows // step),
        in_specs=[
            spec_q,
            pl.BlockSpec((tokens, pair), lambda h, i: (0, h)),
            pl.BlockSpec((tokens, pair), lambda h, i: (0, h + pairs)),
            pl.BlockSpec((tokens, 128), lambda h, i: (0, 0)),
        ],
        out_specs=[spec_q, pl.BlockSpec((1, 8, step), lambda h, i: (h, 0, i))],
        cost_estimate=COST,
        compiler_params=limit(tokens, 28),
        name="attend",
    )(query, keys, keys, mask)


def attend_back_kernel(
    q_ref, k_ref, v_ref, g_ref, o_ref, logs_ref, mask_ref, dq_ref, dk_ref, dv_ref, bias_ref, dk_sum, dv_sum
):
    step = pl.program_id(0)
    column = lax.broadcasted_iota(jnp.int32, (1, 2 * HEAD_DIM), 1)
    low_query, none = scaled(q_ref[...]), jnp.zeros((), BF16)

    @pl.when(step == 0)
    def _():
        dk_sum[...] = jnp.zeros_like(dk_sum)
        dv_sum[...] = jnp.zeros_like(dv_sum)

    products = jnp.transpose(g_ref[...].astype(F32) * o_ref[...])
    grads, dk, dv = [], None, None
    for half in range(2):
        at = slice(half * HEAD_DIM, (half + 1) * HEAD_DIM)
        here = (column < HEAD_DIM) if half == 0 else (column >= HEAD_DIM)
        grad = jnp.where(here, g_ref[...], none)
        scores = head_scores(half, low_query, k_ref[...], mask_ref[...])
        probs = jnp.exp(scores - logs_ref[0, half : half + 1, :])
        dots = jnp.sum(products[at], axis=0, keepdims=True)
        grad_scores = (probs * (times_transpose(v_ref[...], grad) - dots)).astype(BF16)
        grads.append(contract_rows(k_ref[...], grad_scores)[at])
        dk_part = dot(grad_scores, jnp.where(here, q_ref[...], none))
        dv_part = dot(probs.astype(BF16), grad)
        if dk_sum.shape[0] > 4096:
            dk_sum[...] += dk_part
            dv_sum[...] += dv_part
        else:
            dk, dv = (dk_part, dv_part) if half == 0 else (dk + dk_part, dv + dv_part)
    if dk is not None:
        dk_sum[...] += dk
        dv_sum[...] += dv
    dq_ref[...] = jnp.transpose(jnp.concatenate(grads, 0) * 0.125).astype(BF16)

    @pl.when(step == pl.num_programs(0) - 1)
    def _():
        dk_ref[...] = (dk_sum[...] * 0.125).astype(BF16)
        dv_ref[...] = dv_sum[...].astype(BF16)
        bias_ref[...] = jnp.broadcast_to(columns(dv_sum[...]), bias_ref.shape)


def attend_back(which, query, keys, grad, attended, logs, mask):
    rows, width = query.shape
    tokens = keys.shape[0]
    step = rows if tokens <= 4096 else 128
    pair = 2 * HEAD_DIM
    pairs = width // pair
    single = {"pipeline_mode": pl.Buffered(1)} if tokens > 4096 else {}
    spec_q = pl.BlockSpec((step, pair), lambda i: (i, which))
    spec_dq = pl.BlockSpec((step, pair), lambda i: (i, 0))
    spec_k = pl.BlockSpec((tokens, pair), lambda i: (0, which), **single)
    spec_v = pl.BlockSpec((tokens, pair), lambda i: (0, which + pairs), **single)
    spec_dk = pl.BlockSpec((tokens, pair), lambda i: (0, 0))
    flops = 40 * rows * tokens * pair
    return pl.pallas_call(
        attend_back_kernel,
        out_shape=(
            shaped((rows, pair), BF16),
            shaped((tokens, pair), BF16),
            shaped((tokens, pair), BF16),
            shaped((8, pair), F32),
        ),
        grid=(rows // step,),
        in_specs=[
            spec_q,
            spec_k,
            spec_v,
            spec_q,
            spec_q,
            pl.BlockSpec((1, 8, step), lambda i: (which, 0, i)),
            pl.BlockSpec((tokens, 128), lambda i: (0, 0), **single),
        ],
        out_specs=[spec_dq, spec_dk, spec_dk, pl.BlockSpec((8, pair), lambda i: (0, 0))],
        scratch_shapes=[pltpu.VMEM((tokens, pair), F32), pltpu.VMEM((tokens, pair), F32)],
        cost_estimate=COST,
        compiler_params=limit(tokens, 28),
        name="attend_back",
    )(query, keys, keys, grad, attended, logs, mask)


def keys_inputs_kernel(*refs):
    *part_refs, weight_ref, out_ref = refs
    total = None
    for i, ref in enumerate(part_refs):
        width = ref.shape[1]
        if i % 2:
            continue
        both = jnp.concatenate([ref[...], part_refs[i + 1][...]], axis=1)
        term = times_transpose(both, weight_ref[:, i * width : (i + 2) * width])
        total = term if total is None else total + term
    out_ref[...] = total.astype(BF16)


def keys_inputs(which, parts, weight):
    tokens, pair = parts[0].shape
    tokens //= 2
    width = weight.shape[0]
    step = min(tokens, 512)
    spec = pl.BlockSpec((step, pair), lambda i: (i + which * (tokens // step), 0))
    return pl.pallas_call(
        keys_inputs_kernel,
        out_shape=shaped((tokens, width), BF16),
        grid=(tokens // step,),
        in_specs=[spec] * len(parts) + [pl.BlockSpec(weight.shape, lambda i: (0, 0))],
        out_specs=pl.BlockSpec((step, width), lambda i: (i, 0)),
        cost_estimate=COST,
        compiler_params=limit(tokens, 20),
        name="keys_inputs",
    )(*parts, weight)


def keys_weights_kernel(table_ref, mine_ref, other_ref, q_ref, o_ref, *refs):
    *part_refs, keep_ref, send_ref, sum_ref, held_ref = refs
    first = (pl.program_id(0) == 0) & (pl.program_id(1) == 0)
    last = (pl.program_id(0) == 1) & (pl.program_id(1) == pl.num_programs(1) - 1)
    both = jnp.concatenate([ref[...] for ref in part_refs], axis=1)
    chips, rows, width = held_ref.shape
    half, side = chips // 2, width // 2

    @pl.when(first)
    def _():
        sum_ref[...] = contract_rows(mine_ref[...], both)

    @pl.when((pl.program_id(0) == 0) & (pl.program_id(1) > 0))
    def _():
        sum_ref[...] += contract_rows(mine_ref[...], both)

    @pl.when(pl.program_id(0) == 1)
    def _():
        sum_ref[...] += contract_rows(other_ref[...], both)

    @pl.when(last)
    def _():
        held_ref[...] = sum_ref[...].astype(BF16).reshape(held_ref.shape)

        def body(j, carry):
            for ref, at in ((keep_ref, j), (send_ref, j + half)):
                chip = table_ref[at]
                ref[j, :rows] = held_ref[chip]
                ref[j, rows:, :side] = q_ref[chip]
                ref[j, rows:, side:] = o_ref[chip]
            return carry

        lax.fori_loop(0, half, body, 0)


def flat_keys_weights_kernel(mine_ref, other_ref, *refs):
    *part_refs, grad_ref, sum_ref = refs
    first = (pl.program_id(0) == 0) & (pl.program_id(1) == 0)
    last = (pl.program_id(0) == 1) & (pl.program_id(1) == pl.num_programs(1) - 1)
    both = jnp.concatenate([ref[...] for ref in part_refs], axis=1)

    @pl.when(first)
    def _():
        sum_ref[...] = jnp.zeros_like(sum_ref)

    @pl.when(pl.program_id(0) == 0)
    def _():
        sum_ref[...] += contract_rows(mine_ref[...], both)

    @pl.when(pl.program_id(0) == 1)
    def _():
        sum_ref[...] += contract_rows(other_ref[...], both)

    @pl.when(last)
    def _():
        grad_ref[...] = sum_ref[...].astype(BF16)


def keys_weights(table, mine, other, grad_q, grad_o, parts):
    rows, width = mine.shape
    pair = parts[0].shape[1]
    chips, own = grad_q.shape[:2]
    step = min(rows, 512)
    steps = rows // step
    fused = own % 16 == 0
    block = shaped((chips // 2, 2 * own, width), BF16)
    tokens = [
        pl.BlockSpec((step, width), lambda i, j, *t: (jnp.where(i == 0, j, steps - 1), 0)),
        pl.BlockSpec((step, width), lambda i, j, *t: (jnp.where(i == 0, 0, j), 0)),
    ]
    spec = pl.BlockSpec((step, pair), lambda i, j, *t: (i * steps + j, 0))
    whole = pl.BlockSpec((chips, own, width // 2), lambda i, j, *t: (0, 0, 0))
    blocks = pl.BlockSpec(block.shape, lambda i, j, *t: (0, 0, 0))
    cost = COST
    if fused:
        return pl.pallas_call(
            keys_weights_kernel,
            out_shape=(block, block),
            grid_spec=pltpu.PrefetchScalarGridSpec(
                num_scalar_prefetch=1,
                grid=(2, steps),
                in_specs=tokens + [whole, whole] + [spec] * len(parts),
                out_specs=[blocks, blocks],
                scratch_shapes=[pltpu.VMEM((width, width), F32), pltpu.VMEM((chips, own, width), BF16)],
            ),
            cost_estimate=cost,
            compiler_params=limit(2 * rows, 24),
            name="keys_weights",
        )(table, mine, other, grad_q, grad_o, *parts)
    grad = pl.pallas_call(
        flat_keys_weights_kernel,
        out_shape=shaped((width, width), BF16),
        grid=(2, steps),
        in_specs=tokens + [spec] * len(parts),
        out_specs=pl.BlockSpec((width, width), lambda i, j: (0, 0)),
        scratch_shapes=[pltpu.VMEM((width, width), F32)],
        cost_estimate=cost,
        name="keys_weights",
    )(mine, other, *parts)
    return call(
        split_attention_kernel,
        "split_attention",
        (block, block),
        table,
        grad.reshape(chips, own, width),
        grad_q,
        grad_o,
        scalars=1,
    )


def normalize(values):
    center = values - jnp.mean(values, axis=-1, keepdims=True)
    scale = lax.rsqrt(jnp.mean(center * center, axis=-1, keepdims=True) + EPSILON)
    return center * scale, scale


def normalize_back(grad, normal, scale):
    return scale * (
        grad
        - jnp.mean(grad, axis=-1, keepdims=True)
        - normal * jnp.mean(grad * normal, axis=-1, keepdims=True)
    )


def row(ref, which):
    return ref[which : which + 1, :].astype(F32)


def columns(values):
    return jnp.sum(values, axis=0, keepdims=True)


def output_kernel(
    core_ref, inputs_ref, mine_ref, other_ref, near_ref, far_ref, vector_ref, normal_ref, scale_ref, low_ref
):
    side = mine_ref.shape[1]
    core = core_ref[0]
    here, there = pl.ds(core * side, side), pl.ds((1 - core) * side, side)

    def product(ref):
        return dot(mine_ref[...], ref[here, :]) + dot(other_ref[...], ref[there, :])

    near, far = product(near_ref), product(far_ref)
    even = core == 0
    hidden = jnp.concatenate([jnp.where(even, near, far), jnp.where(even, far, near)], axis=1)
    hidden = inputs_ref[...].astype(F32) + hidden + row(vector_ref, OUTPUT_B)
    normal, scale = normalize(hidden)
    normal_ref[...] = normal
    scale_ref[...] = jnp.broadcast_to(scale, scale_ref.shape)
    low_ref[...] = (normal * row(vector_ref, GAIN_1) + row(vector_ref, SHIFT_1)).astype(BF16)


def hidden_kernel(
    mine_ref, other_ref, normal_ref, expand_ref, reduce_ref, vector_ref, active_ref, slope_ref, base_ref, far_ref,
    active_held, slope_held, base_held, sems,
):
    rows = mine_ref.shape[0]
    width = mine_ref.shape[1]
    both = jnp.concatenate([mine_ref[...], other_ref[...]], axis=0)
    total, copies = None, []
    for i in range(expand_ref.shape[1] // width):
        at = slice(i * width, (i + 1) * width)
        value = dot(both, expand_ref[:, at]) + row(vector_ref, EXPAND_B + i)
        normal = 0.5 + 0.5 * lax.erf(value * np.float32(0.7071067811865476))
        active = (value * normal).astype(BF16)
        active_held[:, at] = active
        density = jnp.exp(value * value * -0.5) * np.float32(0.3989422804014327)
        slope_held[:, at] = (normal + value * density).astype(BF16)
        for j, (held, ref) in enumerate(((active_held, active_ref), (slope_held, slope_ref))):
            copies.append(pltpu.make_async_copy(held.at[:, at], ref.at[:, at], sems.at[2 * i + j]))
            copies[-1].start()
        term = dot(active, reduce_ref[at, :])
        total = term if total is None else total + term
    middle = normal_ref[...] * row(vector_ref, GAIN_1) + row(vector_ref, SHIFT_1)
    base_held[...] = middle + total[:rows] + row(vector_ref, REDUCE_B)
    copies.append(pltpu.make_async_copy(base_held, base_ref, sems.at[len(copies)]))
    copies[-1].start()
    far_ref[...] = total[rows:].astype(BF16)
    for copy in copies:
        copy.wait()


def final_kernel(
    start_ref, base_ref, far_ref, cotangent_ref, vector_ref, out_ref, grad_ref, low_ref, sums_ref
):
    combined = base_ref[...] + far_ref[...].astype(F32)
    normal, scale = normalize(combined)
    gain = row(vector_ref, GAIN_2)
    out_ref[...] = (normal * gain + row(vector_ref, SHIFT_2)).astype(BF16)
    place = start_ref[0] + lax.broadcasted_iota(jnp.int32, combined.shape, 0)
    upstream = jnp.where(place < start_ref[1], cotangent_ref[...].astype(F32), 0.0)
    grad = normalize_back(upstream * gain, normal, scale)
    grad_ref[...] = grad
    low_ref[...] = grad.astype(BF16)
    sums_ref[...] = jnp.zeros_like(sums_ref)
    sums_ref[REDUCE_B : REDUCE_B + 1, :] = columns(grad)
    sums_ref[GAIN_2 : GAIN_2 + 1, :] = columns(upstream * normal)
    sums_ref[SHIFT_2 : SHIFT_2 + 1, :] = columns(upstream)


def hidden_back_kernel(table_a_ref, table_d_ref, *refs):
    cl_mine_ref, cl_other_ref, *far = refs[:8]
    outs, held, sems = refs[8:15], refs[15:-1], refs[-1]
    copies = [pltpu.make_async_copy(i, h, sems.at[at]) for at, (i, h) in enumerate(zip(far, held))]
    copies[0].start()
    active_ref, slope_ref, reduce_ref, expand_ref, mid_mine_ref, mid_other_ref = held[:6]
    near_ref, far_ref, sums_ref, d_keep_ref, d_send_ref, a_keep_ref, a_send_ref = outs
    d_held_ref, a_held_ref, low_ref = held[6:]
    rows, width = cl_mine_ref.shape
    times = expand_ref.shape[1] // width
    both = jnp.concatenate([cl_mine_ref[...], cl_other_ref[...]], axis=0)
    sums_ref[...] = jnp.zeros_like(sums_ref)
    copies[0].wait()
    for copy in copies[1:]:
        copy.start()
    units = d_held_ref.shape[1]
    for i in range(times):
        part = contract_rows(active_ref[:, i * width : (i + 1) * width], both).astype(BF16)
        d_held_ref[i * width // units : (i + 1) * width // units] = part.reshape(width // units, units, width)
    split_reduce_kernel(table_d_ref, d_held_ref, d_keep_ref, d_send_ref)
    for copy in copies[1:3]:
        copy.wait()
    total = None
    for i in range(times):
        at = slice(i * width, (i + 1) * width)
        active = times_transpose(both, reduce_ref[at, :]).astype(BF16)
        grad = (active.astype(F32) * slope_ref[:, at].astype(F32)).astype(BF16)
        low_ref[:, at] = grad
        sums_ref[i : i + 1, :] = columns(grad.astype(F32))
    copies[3].wait()
    for i in range(times):
        at = slice(i * width, (i + 1) * width)
        term = times_transpose(low_ref[:, at], expand_ref[:, at])
        total = term if total is None else total + term
    near_ref[...] = total[:rows]
    far_ref[...] = total[rows:].astype(BF16)
    for copy in copies[4:]:
        copy.wait()
    mid = jnp.concatenate([mid_mine_ref[...], mid_other_ref[...]], axis=0)
    own = a_held_ref.shape[1]
    for i in range(times):
        at = slice(i * width, (i + 1) * width)
        a_held_ref[:, :, at] = contract_rows(mid, low_ref[:, at]).astype(BF16).reshape(width // own, own, width)
    split_expand_kernel(table_a_ref, a_held_ref, a_keep_ref, a_send_ref)


def hidden_back_plain_kernel(mine_ref, other_ref, expand_ref, reduce_ref, slope_ref, low_ref, near_ref, far_ref, sums_ref):
    rows, width = mine_ref.shape
    both = jnp.concatenate([mine_ref[...], other_ref[...]], axis=0)
    total = None
    sums_ref[...] = jnp.zeros_like(sums_ref)
    for i in range(expand_ref.shape[1] // width):
        at = slice(i * width, (i + 1) * width)
        active = times_transpose(both, reduce_ref[at, :]).astype(BF16)
        grad = (active.astype(F32) * slope_ref[:, at].astype(F32)).astype(BF16)
        low_ref[:, at] = grad
        sums_ref[i : i + 1, :] = columns(grad.astype(F32))
        term = times_transpose(grad, expand_ref[:, at])
        total = term if total is None else total + term
    near_ref[...] = total[:rows]
    far_ref[...] = total[rows:].astype(BF16)


def hidden_back(table_a, table_d, low, low_other, active, slope, reduce, expand, middle, middle_other, units):
    rows, width = low.shape
    hidden_units = reduce.shape[0]
    chips, own, times = hidden_units // units, width * units // hidden_units, hidden_units // width
    far = [active, slope, reduce, expand, middle, middle_other]
    far = [pltpu.with_memory_space_constraint(v, pltpu.HBM) for v in far]
    return pl.pallas_call(
        hidden_back_kernel,
        out_shape=(
            shaped((rows, width), F32),
            shaped((rows, width), BF16),
            shaped((8, width), F32),
            *(shaped((chips // 2, units, width), BF16),) * 2,
            *(shaped((chips // 2, times * own, width), BF16),) * 2,
        ),
        in_specs=[SMEM] * 2 + [VMEM] * 2 + [pl.BlockSpec(memory_space=pltpu.HBM)] * len(far),
        out_specs=(VMEM,) * 7,
        scratch_shapes=[
            *[pltpu.VMEM(v.shape, v.dtype) for v in far],
            pltpu.VMEM((chips, units, width), BF16),
            pltpu.VMEM((chips, own, hidden_units), BF16),
            pltpu.VMEM((2 * rows, hidden_units), BF16),
            pltpu.SemaphoreType.DMA((len(far),)),
        ],
        cost_estimate=COST,
        compiler_params=pltpu.CompilerParams(vmem_limit_bytes=24 << 20),
        name="hidden_back",
    )(table_a, table_d, low, low_other, *far)


def reduce_grads_kernel(low_mine_ref, low_other_ref, active_ref, grad_ref):
    width = low_mine_ref.shape[1]
    low = jnp.concatenate([low_mine_ref[...], low_other_ref[...]], axis=0)
    for i in range(active_ref.shape[1] // width):
        at = slice(i * width, (i + 1) * width)
        grad_ref[at, :] = contract_rows(active_ref[:, at], low).astype(BF16)


def expand_grads_kernel(mid_mine_ref, mid_other_ref, low_ref, grad_ref):
    width = mid_mine_ref.shape[1]
    mid = jnp.concatenate([mid_mine_ref[...], mid_other_ref[...]], axis=0)
    for i in range(low_ref.shape[1] // width):
        at = slice(i * width, (i + 1) * width)
        grad_ref[:, at] = contract_rows(mid, low_ref[:, at]).astype(BF16)


def output_back_kernel(
    core_ref, normal_ref, scale_ref, grad_ref, near_sum_ref, far_sum_ref, near_ref, far_ref, vector_ref,
    hidden_ref, low_ref, mine_ref, other_ref, sums_ref,
):
    side = near_ref.shape[1]
    core = core_ref[0]
    even = core == 0
    normal = normal_ref[...]
    grad_middle = grad_ref[...] + near_sum_ref[...] + far_sum_ref[...].astype(F32)
    grad = normalize_back(grad_middle * row(vector_ref, GAIN_1), normal, scale_ref[:, :1])
    hidden_ref[...] = grad
    low = grad.astype(BF16)
    low_ref[...] = low
    low_near = jnp.where(even, low[:, :side], low[:, side:])
    low_far = jnp.where(even, low[:, side:], low[:, :side])
    here, there = pl.ds(core * side, side), pl.ds((1 - core) * side, side)

    def product(rows):
        return times_transpose(low_near, near_ref[rows, :]) + times_transpose(low_far, far_ref[rows, :])

    mine_ref[...] = product(here).astype(BF16)
    other_ref[...] = product(there).astype(BF16)
    sums_ref[...] = jnp.zeros_like(sums_ref)
    sums_ref[OUTPUT_B : OUTPUT_B + 1, :] = columns(grad)
    sums_ref[GAIN_1 : GAIN_1 + 1, :] = columns(grad_middle * normal)
    sums_ref[SHIFT_1 : SHIFT_1 + 1, :] = columns(grad_middle)


def output_grads_kernel(core_ref, mine_ref, other_ref, low_ref, near_ref, far_ref):
    side = mine_ref.shape[1]
    core = core_ref[0]
    even = core == 0
    here, there = pl.ds(core * side, side), pl.ds((1 - core) * side, side)
    for rows, ref in ((here, mine_ref), (there, other_ref)):
        product = contract_rows(ref[...], low_ref[...])
        near_ref[rows, :] = jnp.where(even, product[:, :side], product[:, side:])
        far_ref[rows, :] = jnp.where(even, product[:, side:], product[:, :side]).astype(BF16)


def join_units_kernel(units, core_ref, mine_ref, other_ref, out_ref):
    times, width = mine_ref.shape[0], mine_ref.shape[2]
    even = core_ref[0] == 0
    for i in range(times):
        mine, other = mine_ref[i], other_ref[i]
        parts = (jnp.where(even, mine, other), jnp.where(even, other, mine))
        for j in range(width // units):
            at = (i * (width // units) + j) * 2 * units
            for k, part in enumerate(parts):
                out_ref[:, at + k * units : at + (k + 1) * units] = part[:, j * units : (j + 1) * units]


def finish_kernel(number_ref, mine_ref, other_ref, sums_ref, *out_refs):
    side = mine_ref.shape[2] // 2
    even = number_ref[0] % 2 == 0
    for i, ref in enumerate(out_refs[:4]):
        at = slice(i % 2 * side, (i % 2 + 1) * side)
        mine, other = mine_ref[i // 2, :, at], other_ref[i // 2, :, at]
        ref[:, :side] = jnp.where(even, mine, other)
        ref[:, side:] = jnp.where(even, other, mine)
    unpack_vectors(number_ref, sums_ref, out_refs[4:])


def query_back_kernel(mine_ref, other_ref, weight_ref, *refs):
    *dq_refs, near_ref, far_ref, grad_ref, sums_ref = refs
    rows = mine_ref.shape[0]
    grads = jnp.concatenate([ref[...] for ref in dq_refs], axis=1)
    product = times_transpose(grads, weight_ref[...])
    near_ref[...] = product[:rows]
    far_ref[...] = product[rows:].astype(BF16)
    both = jnp.concatenate([mine_ref[...], other_ref[...]], axis=0)
    grad_ref[...] = contract_rows(both, grads).astype(BF16)
    sums_ref[...] = jnp.broadcast_to(columns(grads.astype(F32)), sums_ref.shape)


def body(
    layer_input,
    cotangent,
    lengths,
    query_weight,
    query_bias,
    key_weight,
    value_weight,
    value_bias,
    output_weight,
    output_bias,
    attn_gain,
    attn_shift,
    expand_weight,
    expand_bias,
    reduce_weight,
    reduce_bias,
    final_gain,
    final_shift,
):
    place = Place()
    core = place.core
    core_s = core.reshape(1)
    number_s = place.number.reshape(1)
    chips = place.count // 2
    inputs = layer_input[0]
    rows, width = inputs.shape
    side = width // 2
    own = query_weight.shape[0]
    units = reduce_weight.shape[0]
    hidden_units = units * chips
    times = hidden_units // width
    length = lengths[0]
    even = core == 0

    masks = [place.others(place.weight_stages, k) for k in range(2)]
    usual = len(place.weight_stages) == 4 and len(place.token_stages) == 3
    turns = WEIGHT_TURNS if usual else {}

    def chip_table(bit=None):
        blocks = np.arange(chips)
        if bit is not None:
            blocks = np.concatenate([blocks[blocks >> bit & 1 == i] for i in range(2)])
        return (place.number ^ jnp.where(even, masks[0][blocks], masks[1][blocks])) // 2

    def first_bit(name):
        return turns[name][0] if name in turns else len(place.weight_stages) - 1

    table = chip_table()
    token_masks = [place.others(place.token_stages, k) for k in range(2)]
    near_ctx = place.context ^ jnp.where(even, token_masks[0], token_masks[1])
    far_ctx = (place.context ^ 1) ^ jnp.where(even, token_masks[1], token_masks[0])
    blocks = jnp.concatenate([near_ctx, far_ctx])
    positions = (blocks[:, None] * rows + jnp.arange(rows, dtype=jnp.int32)).reshape(-1, 1)
    mask = jnp.where(positions < length, 0.0, MASKED).astype(BF16)
    mask = jnp.where(jnp.arange(2 * HEAD_DIM) % HEAD_DIM == 0, mask, 0)

    def joined(mine, other):
        return jnp.where(
            even, jnp.concatenate([mine, other], 1), jnp.concatenate([other, mine], 1)
        ).reshape(-1, width)

    vector_list = [query_bias, value_bias, output_bias, attn_gain, attn_shift, reduce_bias, final_gain, final_shift]
    attention_mine, attention_other, expand_mine, expand_other, vectors = prepare(
        number_s,
        [key_weight, value_weight, query_weight, output_weight],
        expand_weight,
        vector_list + [expand_bias],
    )
    vector_swap = place.swap(vectors, 0)
    vectors = vectors + jnp.where(jnp.arange(VECTOR_ROWS)[:, None] < 8, vector_swap, 0)

    stages = place.weight_stages
    token_stages = place.token_stages
    order = Order(place, STRICT[0])

    other_inputs = place.swap(inputs, 0)
    attention_swapped = place.swap(attention_other, 0)
    if FIRST_WAITS:
        order.last = (attention_swapped,)
    attention_blocks = Gather(order, joined(attention_mine, attention_swapped), stages, vectors)
    block_rows = attention_blocks.held.shape[0]
    expand_rows = joined(expand_mine, place.swap(expand_other, 0))
    expand_blocks = Gather(order, expand_rows[None], stages)
    reduce_blocks = Gather(order, reduce_weight[None], stages)
    token_blocks = Gather(order, inputs[None], token_stages)
    chains = {"X": token_blocks, "B": attention_blocks, "A": expand_blocks, "D": reduce_blocks}
    play(FORWARD[0] if usual else plain_events(chains), chains)

    aligned = (2 * own) % 16 == 0
    tile = 16 if aligned else 2 * own

    def tiles(array):
        array = array if aligned else array[: array.shape[0] // block_rows * block_rows]
        return array.reshape(-1, tile, width)

    weights_kv, weights_q, output_near, bias = call(
        place_attention_kernel,
        "place_attention",
        (
            shaped((chips, 2 * own, width), BF16),
            shaped((chips, 2 * own, side), BF16),
            shaped((chips, 2 * own, side), BF16),
            shaped((8, 3 * side), F32),
        ),
        table,
        core_s,
        tiles(attention_blocks.held),
        tiles(attention_blocks.got),
        attention_blocks.vectors,
        scalars=2,
    )
    vectors = attention_blocks.vectors
    weights_kv = weights_kv.reshape(width, width)
    weights_q = weights_q.reshape(width, side)
    output_near = output_near.reshape(width, side)
    if usual:
        play(FORWARD[1], chains)

    sequence_near = jnp.concatenate([token_blocks.held, token_blocks.got]).reshape(-1, width)
    sequence_far = place.swap(sequence_near, 0)
    keys = project(sequence_near, sequence_far, weights_kv, bias)
    if usual:
        play(FORWARD[2], chains)
    query = jnp.concatenate([inputs, other_inputs])
    query = (dot(query, weights_q) + bias[:1, 2 * side :]).astype(BF16)
    attended, logs = attend(query, keys, mask)
    if usual:
        play(FORWARD[3], chains)
    output_far = place.swap(output_near, 0)
    expand_matrix, reduce_matrix = call(
        place_hidden_kernel,
        "place_hidden",
        (shaped((chips, 2 * own, hidden_units), BF16), shaped((chips, units, width), BF16)),
        table,
        expand_blocks.held,
        expand_blocks.got,
        reduce_blocks.held,
        reduce_blocks.got,
        scalars=1,
    )
    expand_matrix = expand_matrix.reshape(width, hidden_units)
    reduce_matrix = reduce_matrix.reshape(hidden_units, width)
    attended_low = attended.astype(BF16)
    attended_mine = attended_low[:rows]
    attended_other = place.swap(attended_low[rows:], 0)

    normal_one, scale_one, middle_low = call(
        output_kernel,
        "output",
        (shaped((rows, width), F32), shaped((rows, 128), F32), shaped((rows, width), BF16)),
        core_s,
        Far(inputs),
        attended_mine,
        attended_other,
        Far(output_near),
        output_far,
        Far(vectors),
        scalars=1,
    )

    middle_other = place.swap(middle_low, 0)
    active, slope, base, far = call(
        hidden_kernel,
        "hidden",
        (
            shaped((2 * rows, hidden_units), BF16),
            shaped((2 * rows, hidden_units), BF16),
            shaped((rows, width), F32),
            shaped((rows, width), BF16),
        ),
        middle_low,
        middle_other,
        normal_one,
        expand_matrix,
        reduce_matrix,
        vectors,
        scratch=[
            pltpu.VMEM((2 * rows, hidden_units), BF16),
            pltpu.VMEM((2 * rows, hidden_units), BF16),
            pltpu.VMEM((rows, width), F32),
            pltpu.SemaphoreType.DMA((2 * times + 1,)),
        ],
        stored=(0, 1, 2),
    )
    far = place.swap(far, 0)
    start_s = jnp.stack([place.context * rows, length])
    layer_output, grad_combined, combined_low, sums_two = call(
        final_kernel,
        "final",
        (
            shaped((rows, width), BF16),
            shaped((rows, width), F32),
            shaped((rows, width), BF16),
            shaped((8, width), F32),
        ),
        start_s,
        Far(base),
        far,
        Far(cotangent[0]),
        Far(vectors),
        scalars=1,
        room=8,
    )
    combined_other = place.swap(combined_low, 0)
    table_d, table_a = chip_table(first_bit("D")), chip_table(first_bit("A"))
    if (2 * own) % 16 == 0:
        near, far, sums_expand, reduce_keep, reduce_send, expand_keep, expand_send = hidden_back(
            table_a,
            table_d,
            combined_low,
            combined_other,
            active,
            slope,
            reduce_matrix,
            expand_matrix,
            middle_low,
            middle_other,
            units,
        )
    else:
        grad_expanded, near, far, sums_expand = call(
            hidden_back_plain_kernel,
            "hidden_back",
            (
                shaped((2 * rows, hidden_units), BF16),
                shaped((rows, width), F32),
                shaped((rows, width), BF16),
                shaped((8, width), F32),
            ),
            combined_low,
            combined_other,
            expand_matrix,
            reduce_matrix,
            slope,
        )
        grads = call(
            reduce_grads_kernel,
            "reduce_grads",
            shaped((hidden_units, width), BF16),
            combined_low,
            combined_other,
            active,
        )
        out = (shaped((chips // 2, units, width), BF16),) * 2
        reduce_keep, reduce_send = call(
            split_reduce_kernel, "split_reduce", out, table_d, grads.reshape(chips, units, width), scalars=1
        )
        grads = call(
            expand_grads_kernel,
            "expand_grads",
            shaped((width, hidden_units), BF16),
            middle_low,
            middle_other,
            grad_expanded,
        )
        out = (shaped((chips // 2, times * 2 * own, width), BF16),) * 2
        expand_keep, expand_send = call(
            split_expand_kernel, "split_expand", out, table_a, grads.reshape(chips, 2 * own, hidden_units), scalars=1
        )
    far = place.swap(far, 0)

    grad_hidden, hidden_low, grad_mine, grad_other, sums_one = call(
        output_back_kernel,
        "output_back",
        (
            shaped((rows, width), F32),
            shaped((rows, width), BF16),
            shaped((rows, side), BF16),
            shaped((rows, side), BF16),
            shaped((8, width), F32),
        ),
        core_s,
        Far(normal_one),
        Far(scale_one),
        grad_combined,
        near,
        far,
        Far(output_near),
        Far(output_far),
        Far(vectors),
        scalars=1,
    )
    grad_heads = jnp.concatenate([grad_mine, place.swap(grad_other, 0)])
    output_near_grad, output_far_grad = call(
        output_grads_kernel,
        "output_grads",
        (shaped((width, side), F32), shaped((width, side), BF16)),
        core_s,
        Far(attended_mine),
        Far(attended_other),
        hidden_low,
        scalars=1,
    )
    grad_output = (output_near_grad + place.swap(output_far_grad, 0).astype(F32)).astype(BF16)

    def own_half(array, axis):
        first, second = lax.index_in_dim(array, 0, axis, False), lax.index_in_dim(array, 1, axis, False)
        return jnp.where(even, first, second), jnp.where(even, second, first)

    order = Order(place, STRICT[1])
    chains = {
        "D": Scatter(order, reduce_keep, reduce_send, stages, turn=turns.get("D")),
        "A": Scatter(order, expand_keep, expand_send, stages, turn=turns.get("A")),
    }
    if usual:
        play("DA", chains)

    def held_back(kernel, array):
        return order.wait(array) if usual and WAITS[kernel] else array

    parts = []
    pairs = side // (2 * HEAD_DIM)
    for which in range(pairs):
        parts.append(attend_back(which, held_back(which, query), keys, grad_heads, attended, logs, mask))
        if usual:
            play(BACKWARD[which], chains)
    grad_query, grad_keys, grad_values, value_bias_sums = zip(*parts)
    parts = grad_keys + grad_values
    near, far, grad_query_w, query_bias_sum = call(
        query_back_kernel,
        "query_back",
        (
            shaped((rows, width), F32),
            shaped((rows, width), BF16),
            shaped((width, side), BF16),
            shaped((8, side), F32),
        ),
        Far(inputs),
        Far(other_inputs),
        Far(weights_q),
        *grad_query,
    )
    query_part = grad_hidden + near + place.swap(far, 0).astype(F32)

    mine_rows = jnp.stack([query_bias_sum[0], jnp.concatenate([v[0] for v in value_bias_sums])])
    zero = jnp.zeros_like(mine_rows)
    mine_rows = jnp.where(even, jnp.concatenate([mine_rows, zero], 1), jnp.concatenate([zero, mine_rows], 1))
    vector_sums = jnp.concatenate([mine_rows, (sums_one + sums_two)[2:], sums_expand])
    vector_swap = place.swap(vector_sums, 0)
    vector_sums = vector_sums + jnp.where(jnp.arange(VECTOR_ROWS)[:, None] < 8, vector_swap, 0)

    far_part = keys_inputs(1, (held_back(4, parts[0]), *parts[1:]), weights_kv)
    far_got = place.swap(far_part, 0)
    near_part = keys_inputs(0, (held_back(5, parts[0]), *parts[1:]), weights_kv)
    blocks_shape = (sequence_near.shape[0] // rows, rows, width)
    turn = range(len(token_stages))[::-1]
    if usual:
        kinds = "ab"[:TOKEN_NEAR] + "y" + "ab"[TOKEN_NEAR:]
        turn = [kinds.index(kind) for kind in TOKEN_TURN]
    x_keep, x_send = fold(near_part.reshape(blocks_shape), far_got.reshape(blocks_shape), turn[0])
    chains["X"] = Scatter(order, x_keep, x_send, token_stages, turn=turn)
    if usual:
        play(BACKWARD[3], chains)

    inputs_first = (x_send,) if usual and INPUTS_FIRST else ()
    keep, send = keys_weights(
        chip_table(first_bit("B")),
        after(held_back(3, sequence_near), *inputs_first),
        sequence_far,
        grad_query_w.reshape(chips, 2 * own, side),
        grad_output.reshape(chips, 2 * own, side),
        parts,
    )
    keep = keep.reshape(-1, width)
    send = jnp.concatenate([send.reshape(-1, width), vector_sums.astype(BF16)])
    chains["B"] = Scatter(order, keep, send, stages, vector_sums, turns.get("B"))
    play(BACKWARD[4].rstrip("|b") if usual else plain_events(chains), chains)
    reduce_out = chains["D"].keep[0]
    expand_sum = chains["A"].keep[0].reshape(times, 2, own, width)
    input_grad = query_part + chains["X"].keep[0]

    expand_mine, expand_other = own_half(expand_sum, 1)
    expand_out = call(
        functools.partial(join_units_kernel, units),
        "join_units",
        shaped((own, 2 * hidden_units), F32),
        core_s,
        expand_mine,
        place.swap(expand_other, 0),
        scalars=1,
    )

    if usual:
        chains["B"].done(expand_out, input_grad)
    keep, vector_sums = chains["B"].keep, chains["B"].vectors
    pieces = keep.reshape(2, 2, own, width)
    pieces_mine, pieces_other = own_half(pieces, 1)
    pieces_other = place.swap(pieces_other, 0)
    outs = call(
        finish_kernel,
        "finish",
        [shaped((own, width), F32)] * 4 + [shaped((1, own), F32)] * 8 + [shaped((1, units), F32)],
        number_s,
        pieces_mine,
        pieces_other,
        vector_sums,
        scalars=1,
    )
    weights_out, outs = outs[:4], outs[4:]
    outs = [v.reshape(-1) for v in outs]
    return (
        layer_output[None],
        input_grad[None],
        weights_out[2],
        outs[QUERY_B],
        weights_out[0],
        weights_out[1],
        outs[VALUE_B],
        weights_out[3],
        outs[OUTPUT_B],
        outs[GAIN_1],
        outs[SHIFT_1],
        expand_out,
        outs[EXPAND_B],
        reduce_out,
        outs[REDUCE_B],
        outs[GAIN_2],
        outs[SHIFT_2],
    )


def solution(mesh):
    tokens = P("seq", "ctx", None)
    matrix = P(("seq", "ctx"), None)
    vector = P(("seq", "ctx"))
    weights = (
        matrix,
        vector,
        matrix,
        matrix,
        vector,
        matrix,
        vector,
        vector,
        vector,
        matrix,
        vector,
        matrix,
        vector,
        vector,
        vector,
    )
    return jax.shard_map(
        body,
        mesh=mesh,
        in_specs=(tokens, tokens, P("seq")) + weights,
        out_specs=(tokens, tokens) + weights,
        check_vma=False,
    )
```

time: 262 us -> 224 us (0.85)
  waiting for transfers between devices: 129 us -> 96.3 us
  local copies, waits for them, and re-layouts: 25.4 us -> 5.89 us
  Pallas kernels: 47.9 us -> 57.5 us
  starting transfers between devices: 46.5 us -> 56 us
  other arithmetic: 9.41 us -> 4.19 us
    ppermute x48, waiting for transfers between devices: 129 us -> 96.3 us  [swap(): return lax.ppermute(array, EVERY, pairs)]
    unnamed x125 -> x91, local copies, waits for them, and re-layouts: 21.4 us -> 5.81 us
    pallas_call x30 -> x28, Pallas kernels: 17.1 us -> 28.7 us  [the longest x26 20.4 us: call(): pl.pallas_call(kernel, out_shape=flat if many else flat[0], in_specs=spec...]
    ppermute x48, starting transfers between devices: 46.5 us -> 56 us  [swap(): return lax.ppermute(array, EVERY, pairs)]
    concatenate x18 -> x14, other arithmetic: 5.98 us -> 1.46 us  [the longest x4 0.69 us: start(): jnp.concatenate([self.held, self.vectors])]
  transfers between devices with their start and end apart: 48 -> 48, of which waited for: 23 -> 26; matrix products, arithmetic and copies ran while one was open for 6% -> 4% of each run, Pallas kernels for 14% -> 19%
where the time goes in v2:
time: 224 us
  waiting for transfers between devices  96.3 us (43%)
  Pallas kernels  57.5 us (26%)
  starting transfers between devices  56 us (25%)
  local copies, waits for them, and re-layouts  5.89 us (3%)
  other arithmetic  4.19 us (2%)
  between operations  2.54 us (1%)
    ppermute x48, waiting for transfers between devices, swap(): return lax.ppermute(array, EVERY, pairs)  96.3 us
    ppermute x48, starting transfers between devices, swap(): return lax.ppermute(array, EVERY, pairs)  56 us
    pallas_call x26, Pallas kernels, call(): pl.pallas_call(kernel, out_shape=flat if many else flat[0], in_specs=spec...  20.4 us
    pallas_call x1, Pallas kernels, attend(): pl.pallas_call(attend_kernel, out_shape=(shaped((rows, width), F32), shap...  8.99 us
    pallas_call x3, Pallas kernels, attend_back(): pl.pallas_call(attend_back_kernel, out_shape=(shaped((rows, pair), BF16),...  8.57 us
    pallas_call x1, Pallas kernels, hidden_back(): pl.pallas_call(hidden_back_kernel, out_shape=(shaped((rows, width), F32),...  6.94 us
    unnamed x91, local copies, waits for them, and re-layouts  5.81 us
    pallas_call x1, Pallas kernels, keys_weights(): pl.pallas_call(keys_weights_kernel, out_shape=(block, block), grid_spec=p...  4.81 us
  transfers between devices with their start and end apart: 48, of which 26 were waited for; matrix products, arithmetic and copies ran while one was open for 4% of the time, Pallas kernels for 19%

profile of v2, /device:TPU:0, one launch (start us, length us, event | category | flops | bytes accessed | tf_op | source)
XLA Modules:
  0.0 224.0 jit_solution(14897416538859790780)
XLA Ops:
  0.7 4.1 %collective-permute-start.7 = (bf16[1,96,768]{2,1,0:T(8,128)(2,1)}, bf16[1,96,768]{2,1,0:T(8,128)(2,1)S(1)}, u32[]{:S(2)}, u32[]{:S(2)}) collective-permute-start(bf16[1,96,768]{2,1,0:T(8,128)(2,1)} %bitcast.128), channel_id=1, source_target_pairs={{0,8},{1,5},{2,10},{3,7},{4,12},{5,1},{6,14},{7,3},{8,0},{9,13},{1... | collective-permute-start | bytes 442376 | tf_op jit(solution)/shard_map/ppermute | solution.py:129
  12.9 3.4 %collective-permute-done.3 = bf16[112,768]{1,0:T(8,128)(2,1)S(1)} collective-permute-done((bf16[112,768]{1,0:T(8,128)(2,1)S(1)}, bf16[112,768]{1,0:T(8,128)(2,1)S(1)}, u32[]{:S(2)}, u32[]{:S(2)}) %collective-permute-start.3) | collective-permute-done | bytes 172064 | tf_op jit(solution)/shard_map/ppermute | solution.py:129
  17.1 3.5 %collective-permute-done.6 = bf16[1,96,768]{2,1,0:T(8,128)(2,1)S(1)} collective-permute-done((bf16[1,96,768]{2,1,0:T(8,128)(2,1)S(1)}, bf16[1,96,768]{2,1,0:T(8,128)(2,1)S(1)}, u32[]{:S(2)}, u32[]{:S(2)}) %collective-permute-start.6) | collective-permute-done | bytes 147488 | tf_op jit(solution)/shard_map/ppermute | solution.py:129
  22.7 8.3 %collective-permute-done.8 = bf16[208,768]{1,0:T(8,128)(2,1)S(1)} collective-permute-done((bf16[208,768]{1,0:T(8,128)(2,1)S(1)}, bf16[208,768]{1,0:T(8,128)(2,1)S(1)}, u32[]{:S(2)}, u32[]{:S(2)}) %collective-permute-start.8) | collective-permute-done | bytes 319520 | tf_op jit(solution)/shard_map/ppermute | solution.py:129
  31.8 3.8 %collective-permute-done.9 = bf16[2,96,768]{2,1,0:T(8,128)(2,1)S(1)} collective-permute-done((bf16[2,96,768]{2,1,0:T(8,128)(2,1)S(1)}, bf16[2,96,768]{2,1,0:T(8,128)(2,1)S(1)}, u32[]{:S(2)}, u32[]{:S(2)}) %collective-permute-start.9) | collective-permute-done | bytes 294944 | tf_op jit(solution)/shard_map/ppermute | solution.py:129
  37.9 3.5 %collective-permute-start.13 = (bf16[2,128,768]{2,1,0:T(8,128)(2,1)S(1)}, bf16[2,128,768]{2,1,0:T(8,128)(2,1)S(1)}, u32[]{:S(2)}, u32[]{:S(2)}) collective-permute-start(bf16[2,128,768]{2,1,0:T(8,128)(2,1)S(1)} %pad_maximum_fusion.9), channel_id=1, source_target_pairs={{0,8},{1,5},{2,10},{3,7},{4,12},{5,1},{6,14},{7,3},{8,0},{9,13},{1... | collective-permute-start | bytes 1179656 | tf_op jit(solution)/shard_map/ppermute | solution.py:129
  41.4 4.3 %collective-permute-done.10 = bf16[400,768]{1,0:T(8,128)(2,1)S(1)} collective-permute-done((bf16[400,768]{1,0:T(8,128)(2,1)S(1)}, bf16[400,768]{1,0:T(8,128)(2,1)S(1)}, u32[]{:S(2)}, u32[]{:S(2)}) %collective-permute-start.10) | collective-permute-done | bytes 614432 | tf_op jit(solution)/shard_map/ppermute | solution.py:129
  47.4 6.0 %collective-permute-done.12 = bf16[2,96,768]{2,1,0:T(8,128)(2,1)S(1)} collective-permute-done((bf16[2,96,768]{2,1,0:T(8,128)(2,1)S(1)}, bf16[2,96,768]{2,1,0:T(8,128)(2,1)S(1)}, u32[]{:S(2)}, u32[]{:S(2)}) %collective-permute-start.12) | collective-permute-done | bytes 294944 | tf_op jit(solution)/shard_map/ppermute | solution.py:129
  59.1 14.9 %collective-permute-done.16 = bf16[4,96,768]{2,1,0:T(8,128)(2,1)S(1)} collective-permute-done((bf16[4,96,768]{2,1,0:T(8,128)(2,1)S(1)}, bf16[4,96,768]{2,1,0:T(8,128)(2,1)S(1)}, u32[]{:S(2)}, u32[]{:S(2)}) %collective-permute-start.16) | collective-permute-done | bytes 589856 | tf_op jit(solution)/shard_map/ppermute | solution.py:129
  83.0 3.2 %project.1.k_ref.v_ref = bf16[2048,768]{1,0:T(8,128)(2,1)S(1)} custom-call(bf16[1024,768]{1,0:T(8,128)(2,1)S(1)} %bitcast.91, bf16[1024,768]{1,0:T(8,128)(2,1)S(1)} %collective-permute-done.17.other_ref, bf16[768,768]{1,0:T(8,128)(2,1)S(1)} %bitcast.93, f32[8,1152]{1,0:T(8,128)S(1)} %get-tuple-element.168.bias_ref), custom_call_target="tpu_custom_call" | custom-call | flops 1000 | bytes 1000 | tf_op jit(solution)/shard_map/project/pallas_call | solution.py:459
  87.5 9.0 %attend.1 = (f32[256,384]{1,0:T(8,128)S(1)}, f32[3,8,256]{2,1,0:T(8,128)S(1)}) custom-call(bf16[256,384]{1,0:T(8,128)(2,1)S(1)} %fusion.q_ref, bf16[2048,768]{1,0:T(8,128)(2,1)S(1)} %project.1.k_ref.v_ref, bf16[2048,768]{1,0:T(8,128)(2,1)S(1)} %project.1.k_ref.v_ref, bf16[2048,128]{1,0:T(8,128)(2,1)S(1)} %broadcast_select_fusion.mask_ref), custom_call_target="tpu_custom_call" | custom-call | flops 1000 | bytes 1000 | tf_op jit(solution)/shard_map/attend/pallas_call | solution.py:509
  100.3 6.0 %collective-permute-done.22.other_d_ref = bf16[8,96,768]{2,1,0:T(8,128)(2,1)S(1)} collective-permute-done((bf16[8,96,768]{2,1,0:T(8,128)(2,1)S(1)}, bf16[8,96,768]{2,1,0:T(8,128)(2,1)S(1)}, u32[]{:S(2)}, u32[]{:S(2)}) %collective-permute-start.22) | collective-permute-done | bytes 1179680 | tf_op jit(solution)/shard_map/ppermute | solution.py:129
  107.3 3.5 %hidden.1 = (bf16[256,1536]{1,0:T(8,128)(2,1)}, bf16[256,1536]{1,0:T(8,128)(2,1)}, f32[128,768]{1,0:T(8,128)}, bf16[128,768]{1,0:T(8,128)(2,1)}) custom-call(bf16[128,768]{1,0:T(8,128)(2,1)S(1)} %get-tuple-element.177.mine_ref.refs_6_, bf16[128,768]{1,0:T(8,128)(2,1)S(1)} %collective-permute-done.20.other_ref.refs_7_, ...), custom_call_target="tpu_custom_call" | custom-call | flops 1000 | bytes 1000 | tf_op jit(solution)/shard_map/hidden/pallas_call | solution.py:96
  112.6 3.0 %final.1 = (bf16[128,768]{1,0:T(8,128)(2,1)}, f32[128,768]{1,0:T(8,128)S(1)}, bf16[128,768]{1,0:T(8,128)(2,1)S(1)}, f32[8,768]{1,0:T(8,128)S(1)}) custom-call(s32[2]{0:T(128)S(1)} %pad_add_fusion.refs_0_, f32[128,768]{1,0:T(8,128)} %get-tuple-element.187.refs_1_, bf16[128,768]{1,0:T(8,128)(2,1)} %collective-permute-done.23.refs_2_, ...), custom_call_target="tpu_custom_call" | custom-call | flops 1000 | bytes 1000 | tf_op jit(solution)/shard_map/final/pallas_call | solution.py:96
  117.1 6.9 %hidden_back.1 = (f32[128,768]{1,0:T(8,128)S(1)}, bf16[128,768]{1,0:T(8,128)(2,1)S(1)}, f32[8,768]{1,0:T(8,128)S(1)}, bf16[8,96,768]{2,1,0:T(8,128)(2,1)S(1)}, b...) custom-call(s32[16]{0:T(128)S(1)} %and_select_fusion.2.table_ref.table_a_ref, ...), custom_call_target="tpu_custom_call" | custom-call | flops 1000 | bytes 1000 | tf_op jit(solution)/shard_map/hidden_back/pallas_call | solution.py:908
  149.9 4.8 %keys_weights.1 = (bf16[8,96,768]{2,1,0:T(8,128)(2,1)S(1)}, bf16[8,96,768]{2,1,0:T(8,128)(2,1)S(1)}) custom-call(s32[16]{0:T(128)S(1)} %and_select_fusion.2.table_ref.table_a_ref, bf16[1024,768]{1,0:T(8,128)(2,1)S(1)} %bitcast.92, bf16[1024,768]{1,0:T(8,128)(2,1)S(1)} %copy-done.9, bf16[16,48,384]{2,1,0:T(8,128)(2,1)S(1)} %bitcast.113, ...), custom_call_target="tpu_custom_call" | custom-call | flops 1000 | bytes 1000 | tf_op jit(solution)/shard_map/keys_weights/pallas_call | solution.py:713
  162.7 9.5 %collective-permute-done.38.got_ref = bf16[784,768]{1,0:T(8,128)(2,1)S(1)} collective-permute-done((bf16[784,768]{1,0:T(8,128)(2,1)S(1)}, bf16[784,768]{1,0:T(8,128)(2,1)S(1)}, u32[]{:S(2)}, u32[]{:S(2)}) %collective-permute-start.38) | collective-permute-done | bytes 1204256 | tf_op jit(solution)/shard_map/ppermute | solution.py:129
  172.5 3.6 %collective-permute-done.34.got_ref = bf16[2,96,768]{2,1,0:T(8,128)(2,1)S(1)} collective-permute-done((bf16[2,96,768]{2,1,0:T(8,128)(2,1)S(1)}, bf16[2,96,768]{2,1,0:T(8,128)(2,1)S(1)}, u32[]{:S(2)}, u32[]{:S(2)}) %collective-permute-start.34) | collective-permute-done | bytes 294944 | tf_op jit(solution)/shard_map/ppermute | solution.py:129
  176.1 3.9 %collective-permute-done.35.got_ref = bf16[4,96,768]{2,1,0:T(8,128)(2,1)S(1)} collective-permute-done((bf16[4,96,768]{2,1,0:T(8,128)(2,1)S(1)}, bf16[4,96,768]{2,1,0:T(8,128)(2,1)S(1)}, u32[]{:S(2)}, u32[]{:S(2)}) %collective-permute-start.35) | collective-permute-done | bytes 589856 | tf_op jit(solution)/shard_map/ppermute | solution.py:129
  184.9 5.6 %collective-permute-done.40.got_ref = bf16[2,96,768]{2,1,0:T(8,128)(2,1)S(1)} collective-permute-done((bf16[2,96,768]{2,1,0:T(8,128)(2,1)S(1)}, bf16[2,96,768]{2,1,0:T(8,128)(2,1)S(1)}, u32[]{:S(2)}, u32[]{:S(2)}) %collective-permute-start.40) | collective-permute-done | bytes 294944 | tf_op jit(solution)/shard_map/ppermute | solution.py:129
  192.1 5.6 %collective-permute-start.27 = (bf16[128,768]{1,0:T(8,128)(2,1)S(1)}, bf16[128,768]{1,0:T(8,128)(2,1)S(1)}, u32[]{:S(2)}, u32[]{:S(2)}) collective-permute-start(bf16[128,768]{1,0:T(8,128)(2,1)S(1)} %get-tuple-element.205), channel_id=1, source_target_pairs={{0,1},{1,0},{2,3},{3,2},{4,5},{5,4},{6,7},{7,6},{8,9},{9,8},{10,11... | collective-permute-start | bytes 589832 | tf_op jit(solution)/shard_map/ppermute | solution.py:129
  201.3 3.9 %collective-permute-start.46 = (f32[2,24,768]{2,1,0:T(8,128)S(1)}, f32[2,24,768]{2,1,0:T(8,128)S(1)}, u32[]{:S(2)}, u32[]{:S(2)}) collective-permute-start(f32[2,24,768]{2,1,0:T(8,128)S(1)} %get-tuple-element.293), channel_id=1, source_target_pairs={{0,1},{1,0},{2,3},{3,2},{4,5},{5,4},{6,7},{7,6},{8,9},{9,8},{10,11... | collective-permute-start | bytes 442376 | tf_op jit(solution)/shard_map/ppermute | solution.py:129
  209.4 2.9 %collective-permute-done.44.got_ref = bf16[208,768]{1,0:T(8,128)(2,1)S(1)} collective-permute-done((bf16[208,768]{1,0:T(8,128)(2,1)S(1)}, bf16[208,768]{1,0:T(8,128)(2,1)S(1)}, u32[]{:S(2)}, u32[]{:S(2)}) %collective-permute-start.44) | collective-permute-done | bytes 319520 | tf_op jit(solution)/shard_map/ppermute | solution.py:129
  213.8 6.9 %collective-permute-done.45.got_ref = bf16[112,768]{1,0:T(8,128)(2,1)S(1)} collective-permute-done((bf16[112,768]{1,0:T(8,128)(2,1)S(1)}, bf16[112,768]{1,0:T(8,128)(2,1)S(1)}, u32[]{:S(2)}, u32[]{:S(2)}) %collective-permute-start.45) | collective-permute-done | bytes 172064 | tf_op jit(solution)/shard_map/ppermute | solution.py:129
  (248 shorter events, 91.2 us)
Async XLA Ops:
  0.7 16.4 %collective-permute-start.7 = (bf16[1,96,768]{2,1,0:T(8,128)(2,1)}, bf16[1,96,768]{2,1,0:T(8,128)(2,1)S(1)}, u32[]{:S(2)}, u32[]{:S(2)}) collective-permute-start(bf16[1,96,768]{2,1,0:T(8,128)(2,1)} %bitcast.128), channel_id=1, source_target_pairs={{0,8},{1,5},{2,10},{3,7},{4,12},{5,1},{6,14},{7,3},{8,0},{9,13},{1... | collective-permute-start | bytes 442376 | tf_op jit(solution)/shard_map/ppermute | solution.py:129
  20.6 15.0 %collective-permute-start.9 = (bf16[2,96,768]{2,1,0:T(8,128)(2,1)S(1)}, bf16[2,96,768]{2,1,0:T(8,128)(2,1)S(1)}, u32[]{:S(2)}, u32[]{:S(2)}) collective-permute-start(bf16[2,96,768]{2,1,0:T(8,128)(2,1)S(1)} %pad_maximum_fusion.11), channel_id=1, source_target_pairs={{0,4},{1,9},{2,6},{3,11},{4,0},{5,13},{6,2},{7,15},{8,12},{9,1},{1... | collective-permute-start | bytes 884744 | tf_op jit(solution)/shard_map/ppermute | solution.py:129
  36.2 17.2 %collective-permute-start.11 = (bf16[4,96,768]{2,1,0:T(8,128)(2,1)S(1)}, bf16[4,96,768]{2,1,0:T(8,128)(2,1)S(1)}, u32[]{:S(2)}, u32[]{:S(2)}) collective-permute-start(bf16[4,96,768]{2,1,0:T(8,128)(2,1)S(1)} %pad_maximum_fusion.7), channel_id=1, source_target_pairs={{0,2},{1,17},{2,0},{3,19},{4,6},{5,21},{6,4},{7,23},{8,10},{9,25},... | collective-permute-start | bytes 1769480 | tf_op jit(solution)/shard_map/ppermute | solution.py:129
  37.9 15.5 %collective-permute-start.12 = (bf16[2,96,768]{2,1,0:T(8,128)(2,1)S(1)}, bf16[2,96,768]{2,1,0:T(8,128)(2,1)S(1)}, u32[]{:S(2)}, u32[]{:S(2)}) collective-permute-start(bf16[2,96,768]{2,1,0:T(8,128)(2,1)S(1)} %pad_maximum_fusion.12), channel_id=1, source_target_pairs={{0,4},{1,9},{2,6},{3,11},{4,0},{5,13},{6,2},{7,15},{8,12},{9,1},{1... | collective-permute-start | bytes 884744 | tf_op jit(solution)/shard_map/ppermute | solution.py:129
  37.9 15.5 %collective-permute-start.13 = (bf16[2,128,768]{2,1,0:T(8,128)(2,1)S(1)}, bf16[2,128,768]{2,1,0:T(8,128)(2,1)S(1)}, u32[]{:S(2)}, u32[]{:S(2)}) collective-permute-start(bf16[2,128,768]{2,1,0:T(8,128)(2,1)S(1)} %pad_maximum_fusion.9), channel_id=1, source_target_pairs={{0,8},{1,5},{2,10},{3,7},{4,12},{5,1},{6,14},{7,3},{8,0},{9,13},{1... | collective-permute-start | bytes 1179656 | tf_op jit(solution)/shard_map/ppermute | solution.py:129
  53.4 23.1 %collective-permute-start.14 = (bf16[784,768]{1,0:T(8,128)(2,1)}, bf16[784,768]{1,0:T(8,128)(2,1)S(1)}, u32[]{:S(2)}, u32[]{:S(2)}) collective-permute-start(bf16[784,768]{1,0:T(8,128)(2,1)} %constant_dynamic-update-slice_fusion), channel_id=1, source_target_pairs={{0,16},{1,3},{2,18},{3,1},{4,20},{5,7},{6,22},{7,5},{8,24},{9,11},... | collective-permute-start | bytes 3612680 | tf_op jit(solution)/shard_map/ppermute | solution.py:129
  55.0 26.4 %collective-permute-start = (bf16[128,768]{1,0:T(8,128)(2,1)S(1)}, bf16[128,768]{1,0:T(8,128)(2,1)}, u32[]{:S(2)}, u32[]{:S(2)}) collective-permute-start(bf16[128,768]{1,0:T(8,128)(2,1)S(1)} %bitcast.122), channel_id=1, source_target_pairs={{0,1},{1,0},{2,3},{3,2},{4,5},{5,4},{6,7},{7,6},{8,9},{9,8},{10,11... | collective-permute-start | bytes 589832 | tf_op jit(solution)/shard_map/ppermute | solution.py:129
  55.2 20.8 %collective-permute-start.15 = (bf16[4,128,768]{2,1,0:T(8,128)(2,1)S(1)}, bf16[4,128,768]{2,1,0:T(8,128)(2,1)S(1)}, u32[]{:S(2)}, u32[]{:S(2)}) collective-permute-start(bf16[4,128,768]{2,1,0:T(8,128)(2,1)S(1)} %pad_maximum_fusion.5), channel_id=1, source_target_pairs={{0,4},{1,9},{2,6},{3,11},{4,0},{5,13},{6,2},{7,15},{8,12},{9,1},{1... | collective-permute-start | bytes 2359304 | tf_op jit(solution)/shard_map/ppermute | solution.py:129
  57.7 16.3 %collective-permute-start.16 = (bf16[4,96,768]{2,1,0:T(8,128)(2,1)S(1)}, bf16[4,96,768]{2,1,0:T(8,128)(2,1)S(1)}, u32[]{:S(2)}, u32[]{:S(2)}) collective-permute-start(bf16[4,96,768]{2,1,0:T(8,128)(2,1)S(1)} %pad_maximum_fusion.8), channel_id=1, source_target_pairs={{0,2},{1,17},{2,0},{3,19},{4,6},{5,21},{6,4},{7,23},{8,10},{9,25},... | collective-permute-start | bytes 1769480 | tf_op jit(solution)/shard_map/ppermute | solution.py:129
  77.4 22.9 %collective-permute-start.21 = (bf16[8,96,768]{2,1,0:T(8,128)(2,1)S(1)}, bf16[8,96,768]{2,1,0:T(8,128)(2,1)S(1)}, u32[]{:S(2)}, u32[]{:S(2)}) collective-permute-start(bf16[8,96,768]{2,1,0:T(8,128)(2,1)S(1)} %pad_maximum_fusion.3.mine_a_ref), channel_id=1, source_target_pairs={{0,16},{1,3},{2,18},{3,1},{4,20},{5,7},{6,22},{7,5},{8,24},{9,11},... | collective-permute-start | bytes 3538952 | tf_op jit(solution)/shard_map/ppermute | solution.py:129
  78.9 27.4 %collective-permute-start.22 = (bf16[8,96,768]{2,1,0:T(8,128)(2,1)S(1)}, bf16[8,96,768]{2,1,0:T(8,128)(2,1)S(1)}, u32[]{:S(2)}, u32[]{:S(2)}) collective-permute-start(bf16[8,96,768]{2,1,0:T(8,128)(2,1)S(1)} %pad_maximum_fusion.4.mine_d_ref), channel_id=1, source_target_pairs={{0,16},{1,3},{2,18},{3,1},{4,20},{5,7},{6,22},{7,5},{8,24},{9,11},... | collective-permute-start | bytes 3538952 | tf_op jit(solution)/shard_map/ppermute | solution.py:129
  81.3 15.7 %collective-permute-start.19 = (bf16[768,384]{1,0:T(8,128)(2,1)S(1)}, bf16[768,384]{1,0:T(8,128)(2,1)S(1)}, u32[]{:S(2)}, u32[]{:S(2)}) collective-permute-start(bf16[768,384]{1,0:T(8,128)(2,1)S(1)} %bitcast.102), channel_id=1, source_target_pairs={{0,1},{1,0},{2,3},{3,2},{4,5},{5,4},{6,7},{7,6},{8,9},{9,8},{10,11... | collective-permute-start | bytes 1769480 | tf_op jit(solution)/shard_map/ppermute | solution.py:129
  124.3 30.5 %collective-permute-start.29 = (bf16[8,96,768]{2,1,0:T(8,128)(2,1)S(1)}, bf16[8,96,768]{2,1,0:T(8,128)(2,1)S(1)}, u32[]{:S(2)}, u32[]{:S(2)}) collective-permute-start(bf16[8,96,768]{2,1,0:T(8,128)(2,1)S(1)} %get-tuple-element.214), channel_id=1, source_target_pairs={{0,4},{1,9},{2,6},{3,11},{4,0},{5,13},{6,2},{7,15},{8,12},{9,1},{1... | collective-permute-start | bytes 3538952 | tf_op jit(solution)/shard_map/ppermute | solution.py:129
  126.6 18.9 %collective-permute-start.30 = (bf16[8,96,768]{2,1,0:T(8,128)(2,1)S(1)}, bf16[8,96,768]{2,1,0:T(8,128)(2,1)S(1)}, u32[]{:S(2)}, u32[]{:S(2)}) collective-permute-start(bf16[8,96,768]{2,1,0:T(8,128)(2,1)S(1)} %get-tuple-element.216), channel_id=1, source_target_pairs={{0,16},{1,3},{2,18},{3,1},{4,20},{5,7},{6,22},{7,5},{8,24},{9,11},... | collective-permute-start | bytes 3538952 | tf_op jit(solution)/shard_map/ppermute | solution.py:129
  132.0 16.5 %collective-permute-start.36 = (bf16[768,384]{1,0:T(8,128)(2,1)S(1)}, bf16[768,384]{1,0:T(8,128)(2,1)S(1)}, u32[]{:S(2)}, u32[]{:S(2)}) collective-permute-start(bf16[768,384]{1,0:T(8,128)(2,1)S(1)} %get-tuple-element.236), channel_id=1, source_target_pairs={{0,1},{1,0},{2,3},{3,2},{4,5},{5,4},{6,7},{7,6},{8,9},{9,8},{10,11... | collective-permute-start | bytes 1769480 | tf_op jit(solution)/shard_map/ppermute | solution.py:129
  144.9 15.1 %collective-permute-start.28 = (bf16[1024,768]{1,0:T(8,128)(2,1)S(1)}, bf16[1024,768]{1,0:T(8,128)(2,1)S(1)}, u32[]{:S(2)}, u32[]{:S(2)}) collective-permute-start(bf16[1024,768]{1,0:T(8,128)(2,1)S(1)} %keys_inputs.3), channel_id=1, source_target_pairs={{0,1},{1,0},{2,3},{3,2},{4,5},{5,4},{6,7},{7,6},{8,9},{9,8},{10,11... | collective-permute-start | bytes 4718600 | tf_op jit(solution)/shard_map/ppermute | solution.py:129
  155.8 16.5 %collective-permute-start.38 = (bf16[784,768]{1,0:T(8,128)(2,1)S(1)}, bf16[784,768]{1,0:T(8,128)(2,1)S(1)}, u32[]{:S(2)}, u32[]{:S(2)}) collective-permute-start(bf16[784,768]{1,0:T(8,128)(2,1)S(1)} %pad_maximum_fusion.1), channel_id=1, source_target_pairs={{0,16},{1,3},{2,18},{3,1},{4,20},{5,7},{6,22},{7,5},{8,24},{9,11},... | collective-permute-start | bytes 3612680 | tf_op jit(solution)/shard_map/ppermute | solution.py:129
  156.5 23.5 %collective-permute-start.35 = (bf16[4,96,768]{2,1,0:T(8,128)(2,1)S(1)}, bf16[4,96,768]{2,1,0:T(8,128)(2,1)S(1)}, u32[]{:S(2)}, u32[]{:S(2)}) collective-permute-start(bf16[4,96,768]{2,1,0:T(8,128)(2,1)S(1)} %get-tuple-element.232), channel_id=1, source_target_pairs={{0,8},{1,5},{2,10},{3,7},{4,12},{5,1},{6,14},{7,3},{8,0},{9,13},{1... | collective-permute-start | bytes 1769480 | tf_op jit(solution)/shard_map/ppermute | solution.py:129
  160.4 21.9 %collective-permute-start.32 = (bf16[4,128,768]{2,1,0:T(8,128)(2,1)S(1)}, bf16[4,128,768]{2,1,0:T(8,128)(2,1)S(1)}, u32[]{:S(2)}, u32[]{:S(2)}) collective-permute-start(bf16[4,128,768]{2,1,0:T(8,128)(2,1)S(1)} %get-tuple-element.219), channel_id=1, source_target_pairs={{0,2},{1,3},{2,0},{3,1},{4,6},{5,7},{6,4},{7,5},{8,10},{9,11},{10,... | collective-permute-start | bytes 2359304 | tf_op jit(solution)/shard_map/ppermute | solution.py:129
  161.1 15.0 %collective-permute-start.34 = (bf16[2,96,768]{2,1,0:T(8,128)(2,1)S(1)}, bf16[2,96,768]{2,1,0:T(8,128)(2,1)S(1)}, u32[]{:S(2)}, u32[]{:S(2)}) collective-permute-start(bf16[2,96,768]{2,1,0:T(8,128)(2,1)S(1)} %get-tuple-element.228), channel_id=1, source_target_pairs={{0,4},{1,9},{2,6},{3,11},{4,0},{5,13},{6,2},{7,15},{8,12},{9,1},{1... | collective-permute-start | bytes 884744 | tf_op jit(solution)/shard_map/ppermute | solution.py:129
  180.0 17.8 %collective-permute-start.41 = (bf16[400,768]{1,0:T(8,128)(2,1)S(1)}, bf16[400,768]{1,0:T(8,128)(2,1)S(1)}, u32[]{:S(2)}, u32[]{:S(2)}) collective-permute-start(bf16[400,768]{1,0:T(8,128)(2,1)S(1)} %get-tuple-element.252), channel_id=1, source_target_pairs={{0,2},{1,17},{2,0},{3,19},{4,6},{5,21},{6,4},{7,23},{8,10},{9,25},... | collective-permute-start | bytes 1843208 | tf_op jit(solution)/shard_map/ppermute | solution.py:129
  182.4 15.3 %collective-permute-start.33 = (bf16[2,128,768]{2,1,0:T(8,128)(2,1)S(1)}, bf16[2,128,768]{2,1,0:T(8,128)(2,1)S(1)}, u32[]{:S(2)}, u32[]{:S(2)}) collective-permute-start(bf16[2,128,768]{2,1,0:T(8,128)(2,1)S(1)} %get-tuple-element.222), channel_id=1, source_target_pairs={{0,4},{1,9},{2,6},{3,11},{4,0},{5,13},{6,2},{7,15},{8,12},{9,1},{1... | collective-permute-start | bytes 1179656 | tf_op jit(solution)/shard_map/ppermute | solution.py:129
  182.6 15.2 %collective-permute-start.39 = (bf16[1,96,768]{2,1,0:T(8,128)(2,1)S(1)}, bf16[1,96,768]{2,1,0:T(8,128)(2,1)S(1)}, u32[]{:S(2)}, u32[]{:S(2)}) collective-permute-start(bf16[1,96,768]{2,1,0:T(8,128)(2,1)S(1)} %get-tuple-element.246), channel_id=1, source_target_pairs={{0,8},{1,5},{2,10},{3,7},{4,12},{5,1},{6,14},{7,3},{8,0},{9,13},{1... | collective-permute-start | bytes 442376 | tf_op jit(solution)/shard_map/ppermute | solution.py:129
  192.1 20.8 %collective-permute-start.27 = (bf16[128,768]{1,0:T(8,128)(2,1)S(1)}, bf16[128,768]{1,0:T(8,128)(2,1)S(1)}, u32[]{:S(2)}, u32[]{:S(2)}) collective-permute-start(bf16[128,768]{1,0:T(8,128)(2,1)S(1)} %get-tuple-element.205), channel_id=1, source_target_pairs={{0,1},{1,0},{2,3},{3,2},{4,5},{5,4},{6,7},{7,6},{8,9},{9,8},{10,11... | collective-permute-start | bytes 589832 | tf_op jit(solution)/shard_map/ppermute | solution.py:129
  (67 other events, 425.7 us)

commit v3 on v2

--- a/solution.py
+++ b/solution.py
@@ -22,13 +22,14 @@
 SMALL_BYTES = 16 << 20
 COST = pl.CostEstimate(flops=1000, bytes_accessed=1000, transcendentals=0)
 FORWARD = ('XBADbxad|BAba|BADXbadx|BDXbd|', 'xAD', '', 'ad|')
-BACKWARD = ('', '', 'a|A', 'da|DX', 'BA|dab|DABx|aXdbBDxd|Xb|Bx|b')
+BACKWARD = ('', '', 'a|A', 'da|DX', 'B|Adab|DABx|aXdbBDxd|Xb|B|xb')
 TOKEN_NEAR = 0
-TOKEN_TURN = 'yba'
+TOKEN_TURN = 'mix'
 WEIGHT_TURNS = {'D': (1, 0, 3, 2), 'A': (3, 2, 1, 0), 'B': (3, 2, 1, 0)}
 WAITS = (False, False, False, False, False, False)
 FIRST_WAITS = False
 INPUTS_FIRST = False
+REDUCE_FIRST = False
 STRICT = (True, False)
 
 
@@ -408,6 +409,15 @@
     return call(functools.partial(fold_kernel, bit), "fold", out, keep, got)
 
 
+def fold_mixed_kernel(core_ref, keep_ref, got_ref, *out_refs):
+    core = core_ref[0]
+    for j in range(4):
+        low, high = j % 2, j // 2 * 4
+        for i, ref in enumerate(out_refs):
+            at = jnp.where(core == 0, high + low * 2 + i, high + low + 2 * i)
+            ref[j] = (keep_ref[at].astype(F32) + got_ref[at].astype(F32)).astype(BF16)
+
+
 def fold_vectors_kernel(bit, keep_ref, got_ref, vector_ref, *out_refs):
     rows = keep_ref.shape[0]
     vectors = vector_ref[...] + got_ref[rows:, :].astype(F32)
@@ -605,7 +615,7 @@
 
 
 def keys_inputs_kernel(*refs):
-    *part_refs, weight_ref, out_ref = refs
+    *part_refs, own_ref, weight_ref, out_ref = refs
     total = None
     for i, ref in enumerate(part_refs):
         width = ref.shape[1]
@@ -616,23 +626,29 @@
         total = term if total is None else total + term
     out_ref[...] = total.astype(BF16)
 
-
-def keys_inputs(which, parts, weight):
+    @pl.when(pl.program_id(0) == 0)
+    def _():
+        rows = own_ref.shape[0]
+        out_ref[:rows, :] = (total[:rows] + own_ref[...]).astype(BF16)
+
+
+def keys_inputs(which, parts, own, weight):
     tokens, pair = parts[0].shape
     tokens //= 2
     width = weight.shape[0]
     step = min(tokens, 512)
     spec = pl.BlockSpec((step, pair), lambda i: (i + which * (tokens // step), 0))
+    whole = [pl.BlockSpec(v.shape, lambda i: (0, 0)) for v in (own, weight)]
     return pl.pallas_call(
         keys_inputs_kernel,
         out_shape=shaped((tokens, width), BF16),
         grid=(tokens // step,),
-        in_specs=[spec] * len(parts) + [pl.BlockSpec(weight.shape, lambda i: (0, 0))],
+        in_specs=[spec] * len(parts) + whole,
         out_specs=pl.BlockSpec((step, width), lambda i: (i, 0)),
         cost_estimate=COST,
         compiler_params=limit(tokens, 20),
         name="keys_inputs",
-    )(*parts, weight)
+    )(*parts, own, weight)
 
 
 def keys_weights_kernel(table_ref, mine_ref, other_ref, q_ref, o_ref, *refs):
@@ -840,7 +856,8 @@
     cl_mine_ref, cl_other_ref, *far = refs[:8]
     outs, held, sems = refs[8:15], refs[15:-1], refs[-1]
     copies = [pltpu.make_async_copy(i, h, sems.at[at]) for at, (i, h) in enumerate(zip(far, held))]
-    copies[0].start()
+    for copy in copies:
+        copy.start()
     active_ref, slope_ref, reduce_ref, expand_ref, mid_mine_ref, mid_other_ref = held[:6]
     near_ref, far_ref, sums_ref, d_keep_ref, d_send_ref, a_keep_ref, a_send_ref = outs
     d_held_ref, a_held_ref, low_ref = held[6:]
@@ -849,8 +866,6 @@
     both = jnp.concatenate([cl_mine_ref[...], cl_other_ref[...]], axis=0)
     sums_ref[...] = jnp.zeros_like(sums_ref)
     copies[0].wait()
-    for copy in copies[1:]:
-        copy.start()
     units = d_held_ref.shape[1]
     for i in range(times):
         part = contract_rows(active_ref[:, i * width : (i + 1) * width], both).astype(BF16)
@@ -984,11 +999,10 @@
         far_ref[rows, :] = jnp.where(even, product[:, side:], product[:, :side]).astype(BF16)
 
 
-def join_units_kernel(units, core_ref, mine_ref, other_ref, out_ref):
+def join_units(units, even, mine_ref, other_ref, out_ref):
     times, width = mine_ref.shape[0], mine_ref.shape[2]
-    even = core_ref[0] == 0
     for i in range(times):
-        mine, other = mine_ref[i], other_ref[i]
+        mine, other = mine_ref[i], other_ref[2 + i]
         parts = (jnp.where(even, mine, other), jnp.where(even, other, mine))
         for j in range(width // units):
             at = (i * (width // units) + j) * 2 * units
@@ -996,7 +1010,7 @@
                 out_ref[:, at + k * units : at + (k + 1) * units] = part[:, j * units : (j + 1) * units]
 
 
-def finish_kernel(number_ref, mine_ref, other_ref, sums_ref, *out_refs):
+def finish_kernel(units, number_ref, mine_ref, expand_ref, other_ref, sums_ref, expand_out_ref, *out_refs):
     side = mine_ref.shape[2] // 2
     even = number_ref[0] % 2 == 0
     for i, ref in enumerate(out_refs[:4]):
@@ -1004,6 +1018,7 @@
         mine, other = mine_ref[i // 2, :, at], other_ref[i // 2, :, at]
         ref[:, :side] = jnp.where(even, mine, other)
         ref[:, side:] = jnp.where(even, other, mine)
+    join_units(units, even, expand_ref, other_ref, expand_out_ref)
     unpack_vectors(number_ref, sums_ref, out_refs[4:])
 
 
@@ -1013,7 +1028,7 @@
     grads = jnp.concatenate([ref[...] for ref in dq_refs], axis=1)
     product = times_transpose(grads, weight_ref[...])
     near_ref[...] = product[:rows]
-    far_ref[...] = product[rows:].astype(BF16)
+    far_ref[...] = product[rows:]
     both = jnp.concatenate([mine_ref[...], other_ref[...]], axis=0)
     grad_ref[...] = contract_rows(both, grads).astype(BF16)
     sums_ref[...] = jnp.broadcast_to(columns(grads.astype(F32)), sums_ref.shape)
@@ -1343,7 +1358,7 @@
         "query_back",
         (
             shaped((rows, width), F32),
-            shaped((rows, width), BF16),
+            shaped((rows, width), F32),
             shaped((width, side), BF16),
             shaped((8, side), F32),
         ),
@@ -1352,7 +1367,7 @@
         Far(weights_q),
         *grad_query,
     )
-    query_part = grad_hidden + near + place.swap(far, 0).astype(F32)
+    query_near, query_far = near, far
 
     mine_rows = jnp.stack([query_bias_sum[0], jnp.concatenate([v[0] for v in value_bias_sums])])
     zero = jnp.zeros_like(mine_rows)
@@ -1361,16 +1376,26 @@
     vector_swap = place.swap(vector_sums, 0)
     vector_sums = vector_sums + jnp.where(jnp.arange(VECTOR_ROWS)[:, None] < 8, vector_swap, 0)
 
-    far_part = keys_inputs(1, (held_back(4, parts[0]), *parts[1:]), weights_kv)
+    far_part = keys_inputs(1, (held_back(4, parts[0]), *parts[1:]), query_far, weights_kv)
     far_got = place.swap(far_part, 0)
-    near_part = keys_inputs(0, (held_back(5, parts[0]), *parts[1:]), weights_kv)
+    near_part = keys_inputs(0, (held_back(5, parts[0]), *parts[1:]), query_near, weights_kv)
     blocks_shape = (sequence_near.shape[0] // rows, rows, width)
-    turn = range(len(token_stages))[::-1]
-    if usual:
-        kinds = "ab"[:TOKEN_NEAR] + "y" + "ab"[TOKEN_NEAR:]
-        turn = [kinds.index(kind) for kind in TOKEN_TURN]
-    x_keep, x_send = fold(near_part.reshape(blocks_shape), far_got.reshape(blocks_shape), turn[0])
-    chains["X"] = Scatter(order, x_keep, x_send, token_stages, turn=turn)
+    near_part, far_part = near_part.reshape(blocks_shape), far_got.reshape(blocks_shape)
+    if usual and TOKEN_TURN == "mix":
+        half_shape = (blocks_shape[0] // 2,) + blocks_shape[1:]
+        x_keep, x_send = call(
+            fold_mixed_kernel, "fold_mixed", (shaped(half_shape, BF16),) * 2, core_s, near_part, far_part, scalars=1
+        )
+        (near_even, near_odd), (even_bit, odd_bit), last_stage = token_stages
+        mixed = [(even_bit, near_odd), last_stage, (near_even, odd_bit)]
+        chains["X"] = Scatter(order, x_keep, x_send, mixed)
+    else:
+        turn = range(len(token_stages))[::-1]
+        if usual:
+            kinds = "ab"[:TOKEN_NEAR] + "y" + "ab"[TOKEN_NEAR:]
+            turn = [kinds.index(kind) for kind in TOKEN_TURN]
+        x_keep, x_send = fold(near_part, far_part, turn[0])
+        chains["X"] = Scatter(order, x_keep, x_send, token_stages, turn=turn)
     if usual:
         play(BACKWARD[3], chains)
 
@@ -1389,32 +1414,26 @@
     play(BACKWARD[4].rstrip("|b") if usual else plain_events(chains), chains)
     reduce_out = chains["D"].keep[0]
     expand_sum = chains["A"].keep[0].reshape(times, 2, own, width)
-    input_grad = query_part + chains["X"].keep[0]
-
+    input_grad = grad_hidden + chains["X"].keep[0]
+
+    if usual:
+        chains["B"].done(input_grad, *((reduce_out,) if REDUCE_FIRST else ()))
+    keep, vector_sums = chains["B"].keep, chains["B"].vectors
     expand_mine, expand_other = own_half(expand_sum, 1)
-    expand_out = call(
-        functools.partial(join_units_kernel, units),
-        "join_units",
-        shaped((own, 2 * hidden_units), F32),
-        core_s,
-        expand_mine,
-        place.swap(expand_other, 0),
-        scalars=1,
-    )
-
-    if usual:
-        chains["B"].done(expand_out, input_grad)
-    keep, vector_sums = chains["B"].keep, chains["B"].vectors
     pieces = keep.reshape(2, 2, own, width)
     pieces_mine, pieces_other = own_half(pieces, 1)
-    pieces_other = place.swap(pieces_other, 0)
-    outs = call(
-        finish_kernel,
+    swapped = place.swap(jnp.concatenate([pieces_other, expand_other]), 0)
+    expand_out, *outs = call(
+        functools.partial(finish_kernel, units),
         "finish",
-        [shaped((own, width), F32)] * 4 + [shaped((1, own), F32)] * 8 + [shaped((1, units), F32)],
+        [shaped((own, 2 * hidden_units), F32)]
+        + [shaped((own, width), F32)] * 4
+        + [shaped((1, own), F32)] * 8
+        + [shaped((1, units), F32)],
         number_s,
         pieces_mine,
-        pieces_other,
+        expand_mine,
+        swapped,
         vector_sums,
         scalars=1,
     )

time: 224 us -> 220 us (0.982)
  starting transfers between devices: 56 us -> 50.4 us
  waiting for transfers between devices: 96.3 us -> 99.1 us
    ppermute x48 -> x46, starting transfers between devices: 56 us -> 50.4 us  [swap(): return lax.ppermute(array, EVERY, pairs)]
    ppermute x48 -> x46, waiting for transfers between devices: 96.3 us -> 99.1 us  [swap(): return lax.ppermute(array, EVERY, pairs)]
    pallas_call x26 -> x25, Pallas kernels: 20.4 us -> 19.8 us  [call(): pl.pallas_call(kernel, out_shape=flat if many else flat[0], in_specs=spec...]
  transfers between devices with their start and end apart: 48 -> 46, of which waited for: 26 -> 25; matrix products, arithmetic and copies ran while one was open for 4% -> 4% of each run, Pallas kernels for 19% -> 19%
where the time goes in v3:
time: 220 us
  waiting for transfers between devices  99.1 us (45%)
  Pallas kernels  56.1 us (26%)
  starting transfers between devices  50.4 us (23%)
  local copies, waits for them, and re-layouts  5.88 us (3%)
  other arithmetic  4.18 us (2%)
  between operations  2.53 us (1%)
    ppermute x46, waiting for transfers between devices, swap(): return lax.ppermute(array, EVERY, pairs)  99.1 us
    ppermute x46, starting transfers between devices, swap(): return lax.ppermute(array, EVERY, pairs)  50.4 us
    pallas_call x25, Pallas kernels, call(): pl.pallas_call(kernel, out_shape=flat if many else flat[0], in_specs=spec...  19.8 us
    pallas_call x1, Pallas kernels, attend(): pl.pallas_call(attend_kernel, out_shape=(shaped((rows, width), F32), shap...  8.99 us
    pallas_call x3, Pallas kernels, attend_back(): pl.pallas_call(attend_back_kernel, out_shape=(shaped((rows, pair), BF16),...  8.57 us
    pallas_call x1, Pallas kernels, hidden_back(): pl.pallas_call(hidden_back_kernel, out_shape=(shaped((rows, width), F32),...  6.04 us
    unnamed x91, local copies, waits for them, and re-layouts  5.81 us
    pallas_call x1, Pallas kernels, keys_weights(): pl.pallas_call(keys_weights_kernel, out_shape=(block, block), grid_spec=p...  4.8 us
  transfers between devices with their start and end apart: 46, of which 25 were waited for; matrix products, arithmetic and copies ran while one was open for 4% of the time, Pallas kernels for 19%

profile of v3, /device:TPU:0, one launch (start us, length us, event | category | flops | bytes accessed | tf_op | source)
XLA Modules:
  0.0 219.8 jit_solution(18127025381652787453)
XLA Ops:
  0.7 4.1 %collective-permute-start.7 = (bf16[1,96,768]{2,1,0:T(8,128)(2,1)}, bf16[1,96,768]{2,1,0:T(8,128)(2,1)S(1)}, u32[]{:S(2)}, u32[]{:S(2)}) collective-permute-start(bf16[1,96,768]{2,1,0:T(8,128)(2,1)} %bitcast.128), channel_id=1, source_target_pairs={{0,8},{1,5},{2,10},{3,7},{4,12},{5,1},{6,14},{7,3},{8,0},{9,13},{1... | collective-permute-start | bytes 442376 | tf_op jit(solution)/shard_map/ppermute | solution.py:130
  12.9 3.4 %collective-permute-done.3 = bf16[112,768]{1,0:T(8,128)(2,1)S(1)} collective-permute-done((bf16[112,768]{1,0:T(8,128)(2,1)S(1)}, bf16[112,768]{1,0:T(8,128)(2,1)S(1)}, u32[]{:S(2)}, u32[]{:S(2)}) %collective-permute-start.3) | collective-permute-done | bytes 172064 | tf_op jit(solution)/shard_map/ppermute | solution.py:130
  17.1 3.5 %collective-permute-done.6 = bf16[1,96,768]{2,1,0:T(8,128)(2,1)S(1)} collective-permute-done((bf16[1,96,768]{2,1,0:T(8,128)(2,1)S(1)}, bf16[1,96,768]{2,1,0:T(8,128)(2,1)S(1)}, u32[]{:S(2)}, u32[]{:S(2)}) %collective-permute-start.6) | collective-permute-done | bytes 147488 | tf_op jit(solution)/shard_map/ppermute | solution.py:130
  22.7 8.3 %collective-permute-done.8 = bf16[208,768]{1,0:T(8,128)(2,1)S(1)} collective-permute-done((bf16[208,768]{1,0:T(8,128)(2,1)S(1)}, bf16[208,768]{1,0:T(8,128)(2,1)S(1)}, u32[]{:S(2)}, u32[]{:S(2)}) %collective-permute-start.8) | collective-permute-done | bytes 319520 | tf_op jit(solution)/shard_map/ppermute | solution.py:130
  31.8 3.8 %collective-permute-done.9 = bf16[2,96,768]{2,1,0:T(8,128)(2,1)S(1)} collective-permute-done((bf16[2,96,768]{2,1,0:T(8,128)(2,1)S(1)}, bf16[2,96,768]{2,1,0:T(8,128)(2,1)S(1)}, u32[]{:S(2)}, u32[]{:S(2)}) %collective-permute-start.9) | collective-permute-done | bytes 294944 | tf_op jit(solution)/shard_map/ppermute | solution.py:130
  37.9 3.5 %collective-permute-start.13 = (bf16[2,128,768]{2,1,0:T(8,128)(2,1)S(1)}, bf16[2,128,768]{2,1,0:T(8,128)(2,1)S(1)}, u32[]{:S(2)}, u32[]{:S(2)}) collective-permute-start(bf16[2,128,768]{2,1,0:T(8,128)(2,1)S(1)} %pad_maximum_fusion.9), channel_id=1, source_target_pairs={{0,8},{1,5},{2,10},{3,7},{4,12},{5,1},{6,14},{7,3},{8,0},{9,13},{1... | collective-permute-start | bytes 1179656 | tf_op jit(solution)/shard_map/ppermute | solution.py:130
  41.4 4.3 %collective-permute-done.10 = bf16[400,768]{1,0:T(8,128)(2,1)S(1)} collective-permute-done((bf16[400,768]{1,0:T(8,128)(2,1)S(1)}, bf16[400,768]{1,0:T(8,128)(2,1)S(1)}, u32[]{:S(2)}, u32[]{:S(2)}) %collective-permute-start.10) | collective-permute-done | bytes 614432 | tf_op jit(solution)/shard_map/ppermute | solution.py:130
  47.3 6.0 %collective-permute-done.12 = bf16[2,96,768]{2,1,0:T(8,128)(2,1)S(1)} collective-permute-done((bf16[2,96,768]{2,1,0:T(8,128)(2,1)S(1)}, bf16[2,96,768]{2,1,0:T(8,128)(2,1)S(1)}, u32[]{:S(2)}, u32[]{:S(2)}) %collective-permute-start.12) | collective-permute-done | bytes 294944 | tf_op jit(solution)/shard_map/ppermute | solution.py:130
  59.1 14.9 %collective-permute-done.16 = bf16[4,96,768]{2,1,0:T(8,128)(2,1)S(1)} collective-permute-done((bf16[4,96,768]{2,1,0:T(8,128)(2,1)S(1)}, bf16[4,96,768]{2,1,0:T(8,128)(2,1)S(1)}, u32[]{:S(2)}, u32[]{:S(2)}) %collective-permute-start.16) | collective-permute-done | bytes 589856 | tf_op jit(solution)/shard_map/ppermute | solution.py:130
  83.0 3.2 %project.1.k_ref.v_ref = bf16[2048,768]{1,0:T(8,128)(2,1)S(1)} custom-call(bf16[1024,768]{1,0:T(8,128)(2,1)S(1)} %bitcast.91, bf16[1024,768]{1,0:T(8,128)(2,1)S(1)} %collective-permute-done.17.other_ref, bf16[768,768]{1,0:T(8,128)(2,1)S(1)} %bitcast.93, f32[8,1152]{1,0:T(8,128)S(1)} %get-tuple-element.169.bias_ref), custom_call_target="tpu_custom_call" | custom-call | flops 1000 | bytes 1000 | tf_op jit(solution)/shard_map/project/pallas_call | solution.py:469
  87.5 9.0 %attend.1 = (f32[256,384]{1,0:T(8,128)S(1)}, f32[3,8,256]{2,1,0:T(8,128)S(1)}) custom-call(bf16[256,384]{1,0:T(8,128)(2,1)S(1)} %fusion.q_ref, bf16[2048,768]{1,0:T(8,128)(2,1)S(1)} %project.1.k_ref.v_ref, bf16[2048,768]{1,0:T(8,128)(2,1)S(1)} %project.1.k_ref.v_ref, bf16[2048,128]{1,0:T(8,128)(2,1)S(1)} %broadcast_select_fusion.mask_ref), custom_call_target="tpu_custom_call" | custom-call | flops 1000 | bytes 1000 | tf_op jit(solution)/shard_map/attend/pallas_call | solution.py:519
  100.3 6.0 %collective-permute-done.22.other_d_ref = bf16[8,96,768]{2,1,0:T(8,128)(2,1)S(1)} collective-permute-done((bf16[8,96,768]{2,1,0:T(8,128)(2,1)S(1)}, bf16[8,96,768]{2,1,0:T(8,128)(2,1)S(1)}, u32[]{:S(2)}, u32[]{:S(2)}) %collective-permute-start.22) | collective-permute-done | bytes 1179680 | tf_op jit(solution)/shard_map/ppermute | solution.py:130
  107.3 3.4 %hidden.1 = (bf16[256,1536]{1,0:T(8,128)(2,1)}, bf16[256,1536]{1,0:T(8,128)(2,1)}, f32[128,768]{1,0:T(8,128)}, bf16[128,768]{1,0:T(8,128)(2,1)}) custom-call(bf16[128,768]{1,0:T(8,128)(2,1)S(1)} %get-tuple-element.178.mine_ref.refs_6_, bf16[128,768]{1,0:T(8,128)(2,1)S(1)} %collective-permute-done.20.other_ref.refs_7_, ...), custom_call_target="tpu_custom_call" | custom-call | flops 1000 | bytes 1000 | tf_op jit(solution)/shard_map/hidden/pallas_call | solution.py:97
  112.6 3.0 %final.1 = (bf16[128,768]{1,0:T(8,128)(2,1)}, f32[128,768]{1,0:T(8,128)S(1)}, bf16[128,768]{1,0:T(8,128)(2,1)S(1)}, f32[8,768]{1,0:T(8,128)S(1)}) custom-call(s32[2]{0:T(128)S(1)} %pad_add_fusion.refs_0_, f32[128,768]{1,0:T(8,128)} %get-tuple-element.188.refs_1_, bf16[128,768]{1,0:T(8,128)(2,1)} %collective-permute-done.23.refs_2_, ...), custom_call_target="tpu_custom_call" | custom-call | flops 1000 | bytes 1000 | tf_op jit(solution)/shard_map/final/pallas_call | solution.py:97
  117.1 6.0 %hidden_back.1 = (f32[128,768]{1,0:T(8,128)S(1)}, bf16[128,768]{1,0:T(8,128)(2,1)S(1)}, f32[8,768]{1,0:T(8,128)S(1)}, bf16[8,96,768]{2,1,0:T(8,128)(2,1)S(1)}, b...) custom-call(s32[16]{0:T(128)S(1)} %and_select_fusion.2.table_ref.table_a_ref, ...), custom_call_target="tpu_custom_call" | custom-call | flops 1000 | bytes 1000 | tf_op jit(solution)/shard_map/hidden_back/pallas_call | solution.py:923
  131.7 2.9 %attend_back.5 = (bf16[256,128]{1,0:T(8,128)(2,1)S(1)}, bf16[2048,128]{1,0:T(8,128)(2,1)S(1)}, bf16[2048,128]{1,0:T(8,128)(2,1)S(1)}, f32[8,128]{1,0:T(8,128)S(1)}) custom-call(bf16[256,384]{1,0:T(8,128)(2,1)S(1)} %copy-done.11, bf16[2048,768]{1,0:T(8,128)(2,1)S(1)} %project.1.k_ref.v_ref, bf16[2048,768]{1,0:T(8,128)(2,1)S(1)} %project.1.k_ref.v_ref, ...), custom_call_target="tpu_custom_call" | custom-call | flops 1000 | bytes 1000 | tf_op jit(solution)/shard_map/attend_back/pallas_call | solution.py:591
  134.6 2.9 %attend_back.4 = (bf16[256,128]{1,0:T(8,128)(2,1)S(1)}, bf16[2048,128]{1,0:T(8,128)(2,1)S(1)}, bf16[2048,128]{1,0:T(8,128)(2,1)S(1)}, f32[8,128]{1,0:T(8,128)S(1)}) custom-call(bf16[256,384]{1,0:T(8,128)(2,1)S(1)} %copy-done.11, bf16[2048,768]{1,0:T(8,128)(2,1)S(1)} %project.1.k_ref.v_ref, bf16[2048,768]{1,0:T(8,128)(2,1)S(1)} %project.1.k_ref.v_ref, ...), custom_call_target="tpu_custom_call" | custom-call | flops 1000 | bytes 1000 | tf_op jit(solution)/shard_map/attend_back/pallas_call | solution.py:591
  137.4 2.9 %attend_back.3 = (bf16[256,128]{1,0:T(8,128)(2,1)S(1)}, bf16[2048,128]{1,0:T(8,128)(2,1)S(1)}, bf16[2048,128]{1,0:T(8,128)(2,1)S(1)}, f32[8,128]{1,0:T(8,128)S(1)}) custom-call(bf16[256,384]{1,0:T(8,128)(2,1)S(1)} %copy-done.11, bf16[2048,768]{1,0:T(8,128)(2,1)S(1)} %project.1.k_ref.v_ref, bf16[2048,768]{1,0:T(8,128)(2,1)S(1)} %project.1.k_ref.v_ref, ...), custom_call_target="tpu_custom_call" | custom-call | flops 1000 | bytes 1000 | tf_op jit(solution)/shard_map/attend_back/pallas_call | solution.py:591
  149.1 4.8 %keys_weights.1 = (bf16[8,96,768]{2,1,0:T(8,128)(2,1)S(1)}, bf16[8,96,768]{2,1,0:T(8,128)(2,1)S(1)}) custom-call(s32[16]{0:T(128)S(1)} %and_select_fusion.2.table_ref.table_a_ref, bf16[1024,768]{1,0:T(8,128)(2,1)S(1)} %bitcast.92, bf16[1024,768]{1,0:T(8,128)(2,1)S(1)} %copy-done.9, bf16[16,48,384]{2,1,0:T(8,128)(2,1)S(1)} %bitcast.113, ...), custom_call_target="tpu_custom_call" | custom-call | flops 1000 | bytes 1000 | tf_op jit(solution)/shard_map/keys_weights/pallas_call | solution.py:729
  162.0 9.5 %collective-permute-done.37.got_ref = bf16[784,768]{1,0:T(8,128)(2,1)S(1)} collective-permute-done((bf16[784,768]{1,0:T(8,128)(2,1)S(1)}, bf16[784,768]{1,0:T(8,128)(2,1)S(1)}, u32[]{:S(2)}, u32[]{:S(2)}) %collective-permute-start.37) | collective-permute-done | bytes 1204256 | tf_op jit(solution)/shard_map/ppermute | solution.py:130
  171.7 6.0 %collective-permute-done.33.got_ref = bf16[2,96,768]{2,1,0:T(8,128)(2,1)S(1)} collective-permute-done((bf16[2,96,768]{2,1,0:T(8,128)(2,1)S(1)}, bf16[2,96,768]{2,1,0:T(8,128)(2,1)S(1)}, u32[]{:S(2)}, u32[]{:S(2)}) %collective-permute-start.33) | collective-permute-done | bytes 294944 | tf_op jit(solution)/shard_map/ppermute | solution.py:130
  192.1 3.5 %collective-permute-start.42 = (bf16[1,128,768]{2,1,0:T(8,128)(2,1)S(1)}, bf16[1,128,768]{2,1,0:T(8,128)(2,1)S(1)}, u32[]{:S(2)}, u32[]{:S(2)}) collective-permute-start(bf16[1,128,768]{2,1,0:T(8,128)(2,1)S(1)} %get-tuple-element.257), channel_id=1, source_target_pairs={{0,8},{1,3},{2,10},{3,1},{4,12},{5,7},{6,14},{7,5},{8,0},{9,11},{1... | collective-permute-start | bytes 589832 | tf_op jit(solution)/shard_map/ppermute | solution.py:130
  195.6 12.0 %collective-permute-done.42.got_ref = bf16[1,128,768]{2,1,0:T(8,128)(2,1)S(1)} collective-permute-done((bf16[1,128,768]{2,1,0:T(8,128)(2,1)S(1)}, bf16[1,128,768]{2,1,0:T(8,128)(2,1)S(1)}, u32[]{:S(2)}, u32[]{:S(2)}) %collective-permute-start.42) | collective-permute-done | bytes 196640 | tf_op jit(solution)/shard_map/ppermute | solution.py:130
  208.6 6.3 %collective-permute-done.44.got_ref = bf16[112,768]{1,0:T(8,128)(2,1)S(1)} collective-permute-done((bf16[112,768]{1,0:T(8,128)(2,1)S(1)}, bf16[112,768]{1,0:T(8,128)(2,1)S(1)}, u32[]{:S(2)}, u32[]{:S(2)}) %collective-permute-start.44) | collective-permute-done | bytes 172064 | tf_op jit(solution)/shard_map/ppermute | solution.py:130
  (244 shorter events, 84.1 us)
Async XLA Ops:
  0.7 16.4 %collective-permute-start.7 = (bf16[1,96,768]{2,1,0:T(8,128)(2,1)}, bf16[1,96,768]{2,1,0:T(8,128)(2,1)S(1)}, u32[]{:S(2)}, u32[]{:S(2)}) collective-permute-start(bf16[1,96,768]{2,1,0:T(8,128)(2,1)} %bitcast.128), channel_id=1, source_target_pairs={{0,8},{1,5},{2,10},{3,7},{4,12},{5,1},{6,14},{7,3},{8,0},{9,13},{1... | collective-permute-start | bytes 442376 | tf_op jit(solution)/shard_map/ppermute | solution.py:130
  4.8 12.3 %collective-permute-start.4 = (bf16[1,128,768]{2,1,0:T(8,128)(2,1)}, bf16[1,128,768]{2,1,0:T(8,128)(2,1)S(1)}, u32[]{:S(2)}, u32[]{:S(2)}) collective-permute-start(bf16[1,128,768]{2,1,0:T(8,128)(2,1)} %param.28), channel_id=1, source_target_pairs={{0,2},{1,3},{2,0},{3,1},{4,6},{5,7},{6,4},{7,5},{8,10},{9,11},{10,... | collective-permute-start | bytes 589832 | tf_op jit(solution)/shard_map/ppermute | solution.py:130
  10.0 10.6 %collective-permute-start.6 = (bf16[1,96,768]{2,1,0:T(8,128)(2,1)S(1)}, bf16[1,96,768]{2,1,0:T(8,128)(2,1)S(1)}, u32[]{:S(2)}, u32[]{:S(2)}) collective-permute-start(bf16[1,96,768]{2,1,0:T(8,128)(2,1)S(1)} %bitcast.124), channel_id=1, source_target_pairs={{0,8},{1,5},{2,10},{3,7},{4,12},{5,1},{6,14},{7,3},{8,0},{9,13},{1... | collective-permute-start | bytes 442376 | tf_op jit(solution)/shard_map/ppermute | solution.py:130
  20.6 15.0 %collective-permute-start.9 = (bf16[2,96,768]{2,1,0:T(8,128)(2,1)S(1)}, bf16[2,96,768]{2,1,0:T(8,128)(2,1)S(1)}, u32[]{:S(2)}, u32[]{:S(2)}) collective-permute-start(bf16[2,96,768]{2,1,0:T(8,128)(2,1)S(1)} %pad_maximum_fusion.11), channel_id=1, source_target_pairs={{0,4},{1,9},{2,6},{3,11},{4,0},{5,13},{6,2},{7,15},{8,12},{9,1},{1... | collective-permute-start | bytes 884744 | tf_op jit(solution)/shard_map/ppermute | solution.py:130
  36.2 17.2 %collective-permute-start.11 = (bf16[4,96,768]{2,1,0:T(8,128)(2,1)S(1)}, bf16[4,96,768]{2,1,0:T(8,128)(2,1)S(1)}, u32[]{:S(2)}, u32[]{:S(2)}) collective-permute-start(bf16[4,96,768]{2,1,0:T(8,128)(2,1)S(1)} %pad_maximum_fusion.7), channel_id=1, source_target_pairs={{0,2},{1,17},{2,0},{3,19},{4,6},{5,21},{6,4},{7,23},{8,10},{9,25},... | collective-permute-start | bytes 1769480 | tf_op jit(solution)/shard_map/ppermute | solution.py:130
  37.9 15.5 %collective-permute-start.12 = (bf16[2,96,768]{2,1,0:T(8,128)(2,1)S(1)}, bf16[2,96,768]{2,1,0:T(8,128)(2,1)S(1)}, u32[]{:S(2)}, u32[]{:S(2)}) collective-permute-start(bf16[2,96,768]{2,1,0:T(8,128)(2,1)S(1)} %pad_maximum_fusion.12), channel_id=1, source_target_pairs={{0,4},{1,9},{2,6},{3,11},{4,0},{5,13},{6,2},{7,15},{8,12},{9,1},{1... | collective-permute-start | bytes 884744 | tf_op jit(solution)/shard_map/ppermute | solution.py:130
  37.9 15.5 %collective-permute-start.13 = (bf16[2,128,768]{2,1,0:T(8,128)(2,1)S(1)}, bf16[2,128,768]{2,1,0:T(8,128)(2,1)S(1)}, u32[]{:S(2)}, u32[]{:S(2)}) collective-permute-start(bf16[2,128,768]{2,1,0:T(8,128)(2,1)S(1)} %pad_maximum_fusion.9), channel_id=1, source_target_pairs={{0,8},{1,5},{2,10},{3,7},{4,12},{5,1},{6,14},{7,3},{8,0},{9,13},{1... | collective-permute-start | bytes 1179656 | tf_op jit(solution)/shard_map/ppermute | solution.py:130
  53.4 23.1 %collective-permute-start.14 = (bf16[784,768]{1,0:T(8,128)(2,1)}, bf16[784,768]{1,0:T(8,128)(2,1)S(1)}, u32[]{:S(2)}, u32[]{:S(2)}) collective-permute-start(bf16[784,768]{1,0:T(8,128)(2,1)} %constant_dynamic-update-slice_fusion), channel_id=1, source_target_pairs={{0,16},{1,3},{2,18},{3,1},{4,20},{5,7},{6,22},{7,5},{8,24},{9,11},... | collective-permute-start | bytes 3612680 | tf_op jit(solution)/shard_map/ppermute | solution.py:130
  55.0 26.4 %collective-permute-start = (bf16[128,768]{1,0:T(8,128)(2,1)S(1)}, bf16[128,768]{1,0:T(8,128)(2,1)}, u32[]{:S(2)}, u32[]{:S(2)}) collective-permute-start(bf16[128,768]{1,0:T(8,128)(2,1)S(1)} %bitcast.122), channel_id=1, source_target_pairs={{0,1},{1,0},{2,3},{3,2},{4,5},{5,4},{6,7},{7,6},{8,9},{9,8},{10,11... | collective-permute-start | bytes 589832 | tf_op jit(solution)/shard_map/ppermute | solution.py:130
  55.2 20.8 %collective-permute-start.15 = (bf16[4,128,768]{2,1,0:T(8,128)(2,1)S(1)}, bf16[4,128,768]{2,1,0:T(8,128)(2,1)S(1)}, u32[]{:S(2)}, u32[]{:S(2)}) collective-permute-start(bf16[4,128,768]{2,1,0:T(8,128)(2,1)S(1)} %pad_maximum_fusion.5), channel_id=1, source_target_pairs={{0,4},{1,9},{2,6},{3,11},{4,0},{5,13},{6,2},{7,15},{8,12},{9,1},{1... | collective-permute-start | bytes 2359304 | tf_op jit(solution)/shard_map/ppermute | solution.py:130
  57.7 16.3 %collective-permute-start.16 = (bf16[4,96,768]{2,1,0:T(8,128)(2,1)S(1)}, bf16[4,96,768]{2,1,0:T(8,128)(2,1)S(1)}, u32[]{:S(2)}, u32[]{:S(2)}) collective-permute-start(bf16[4,96,768]{2,1,0:T(8,128)(2,1)S(1)} %pad_maximum_fusion.8), channel_id=1, source_target_pairs={{0,2},{1,17},{2,0},{3,19},{4,6},{5,21},{6,4},{7,23},{8,10},{9,25},... | collective-permute-start | bytes 1769480 | tf_op jit(solution)/shard_map/ppermute | solution.py:130
  77.4 23.0 %collective-permute-start.21 = (bf16[8,96,768]{2,1,0:T(8,128)(2,1)S(1)}, bf16[8,96,768]{2,1,0:T(8,128)(2,1)S(1)}, u32[]{:S(2)}, u32[]{:S(2)}) collective-permute-start(bf16[8,96,768]{2,1,0:T(8,128)(2,1)S(1)} %pad_maximum_fusion.3.mine_a_ref), channel_id=1, source_target_pairs={{0,16},{1,3},{2,18},{3,1},{4,20},{5,7},{6,22},{7,5},{8,24},{9,11},... | collective-permute-start | bytes 3538952 | tf_op jit(solution)/shard_map/ppermute | solution.py:130
  78.9 27.4 %collective-permute-start.22 = (bf16[8,96,768]{2,1,0:T(8,128)(2,1)S(1)}, bf16[8,96,768]{2,1,0:T(8,128)(2,1)S(1)}, u32[]{:S(2)}, u32[]{:S(2)}) collective-permute-start(bf16[8,96,768]{2,1,0:T(8,128)(2,1)S(1)} %pad_maximum_fusion.4.mine_d_ref), channel_id=1, source_target_pairs={{0,16},{1,3},{2,18},{3,1},{4,20},{5,7},{6,22},{7,5},{8,24},{9,11},... | collective-permute-start | bytes 3538952 | tf_op jit(solution)/shard_map/ppermute | solution.py:130
  81.3 15.7 %collective-permute-start.19 = (bf16[768,384]{1,0:T(8,128)(2,1)S(1)}, bf16[768,384]{1,0:T(8,128)(2,1)S(1)}, u32[]{:S(2)}, u32[]{:S(2)}) collective-permute-start(bf16[768,384]{1,0:T(8,128)(2,1)S(1)} %bitcast.102), channel_id=1, source_target_pairs={{0,1},{1,0},{2,3},{3,2},{4,5},{5,4},{6,7},{7,6},{8,9},{9,8},{10,11... | collective-permute-start | bytes 1769480 | tf_op jit(solution)/shard_map/ppermute | solution.py:130
  123.4 30.6 %collective-permute-start.28 = (bf16[8,96,768]{2,1,0:T(8,128)(2,1)S(1)}, bf16[8,96,768]{2,1,0:T(8,128)(2,1)S(1)}, u32[]{:S(2)}, u32[]{:S(2)}) collective-permute-start(bf16[8,96,768]{2,1,0:T(8,128)(2,1)S(1)} %get-tuple-element.215), channel_id=1, source_target_pairs={{0,4},{1,9},{2,6},{3,11},{4,0},{5,13},{6,2},{7,15},{8,12},{9,1},{1... | collective-permute-start | bytes 3538952 | tf_op jit(solution)/shard_map/ppermute | solution.py:130
  125.7 19.0 %collective-permute-start.29 = (bf16[8,96,768]{2,1,0:T(8,128)(2,1)S(1)}, bf16[8,96,768]{2,1,0:T(8,128)(2,1)S(1)}, u32[]{:S(2)}, u32[]{:S(2)}) collective-permute-start(bf16[8,96,768]{2,1,0:T(8,128)(2,1)S(1)} %get-tuple-element.217), channel_id=1, source_target_pairs={{0,16},{1,3},{2,18},{3,1},{4,20},{5,7},{6,22},{7,5},{8,24},{9,11},... | collective-permute-start | bytes 3538952 | tf_op jit(solution)/shard_map/ppermute | solution.py:130
  131.1 16.6 %collective-permute-start.35 = (bf16[768,384]{1,0:T(8,128)(2,1)S(1)}, bf16[768,384]{1,0:T(8,128)(2,1)S(1)}, u32[]{:S(2)}, u32[]{:S(2)}) collective-permute-start(bf16[768,384]{1,0:T(8,128)(2,1)S(1)} %get-tuple-element.237), channel_id=1, source_target_pairs={{0,1},{1,0},{2,3},{3,2},{4,5},{5,4},{6,7},{7,6},{8,9},{9,8},{10,11... | collective-permute-start | bytes 1769480 | tf_op jit(solution)/shard_map/ppermute | solution.py:130
  144.1 15.2 %collective-permute-start.27 = (bf16[1024,768]{1,0:T(8,128)(2,1)S(1)}, bf16[1024,768]{1,0:T(8,128)(2,1)S(1)}, u32[]{:S(2)}, u32[]{:S(2)}) collective-permute-start(bf16[1024,768]{1,0:T(8,128)(2,1)S(1)} %keys_inputs.3), channel_id=1, source_target_pairs={{0,1},{1,0},{2,3},{3,2},{4,5},{5,4},{6,7},{7,6},{8,9},{9,8},{10,11... | collective-permute-start | bytes 4718600 | tf_op jit(solution)/shard_map/ppermute | solution.py:130
  155.0 16.5 %collective-permute-start.37 = (bf16[784,768]{1,0:T(8,128)(2,1)S(1)}, bf16[784,768]{1,0:T(8,128)(2,1)S(1)}, u32[]{:S(2)}, u32[]{:S(2)}) collective-permute-start(bf16[784,768]{1,0:T(8,128)(2,1)S(1)} %pad_maximum_fusion.1), channel_id=1, source_target_pairs={{0,16},{1,3},{2,18},{3,1},{4,20},{5,7},{6,22},{7,5},{8,24},{9,11},... | collective-permute-start | bytes 3612680 | tf_op jit(solution)/shard_map/ppermute | solution.py:130
  155.8 22.0 %collective-permute-start.34 = (bf16[4,96,768]{2,1,0:T(8,128)(2,1)S(1)}, bf16[4,96,768]{2,1,0:T(8,128)(2,1)S(1)}, u32[]{:S(2)}, u32[]{:S(2)}) collective-permute-start(bf16[4,96,768]{2,1,0:T(8,128)(2,1)S(1)} %get-tuple-element.233), channel_id=1, source_target_pairs={{0,8},{1,5},{2,10},{3,7},{4,12},{5,1},{6,14},{7,3},{8,0},{9,13},{1... | collective-permute-start | bytes 1769480 | tf_op jit(solution)/shard_map/ppermute | solution.py:130
  159.6 20.8 %collective-permute-start.31 = (bf16[4,128,768]{2,1,0:T(8,128)(2,1)S(1)}, bf16[4,128,768]{2,1,0:T(8,128)(2,1)S(1)}, u32[]{:S(2)}, u32[]{:S(2)}) collective-permute-start(bf16[4,128,768]{2,1,0:T(8,128)(2,1)S(1)} %get-tuple-element.220), channel_id=1, source_target_pairs={{0,2},{1,5},{2,0},{3,7},{4,6},{5,1},{6,4},{7,3},{8,10},{9,13},{10,... | collective-permute-start | bytes 2359304 | tf_op jit(solution)/shard_map/ppermute | solution.py:130
  160.4 17.4 %collective-permute-start.33 = (bf16[2,96,768]{2,1,0:T(8,128)(2,1)S(1)}, bf16[2,96,768]{2,1,0:T(8,128)(2,1)S(1)}, u32[]{:S(2)}, u32[]{:S(2)}) collective-permute-start(bf16[2,96,768]{2,1,0:T(8,128)(2,1)S(1)} %get-tuple-element.229), channel_id=1, source_target_pairs={{0,4},{1,9},{2,6},{3,11},{4,0},{5,13},{6,2},{7,15},{8,12},{9,1},{1... | collective-permute-start | bytes 884744 | tf_op jit(solution)/shard_map/ppermute | solution.py:130
  188.1 19.6 %collective-permute-start.43 = (bf16[208,768]{1,0:T(8,128)(2,1)S(1)}, bf16[208,768]{1,0:T(8,128)(2,1)S(1)}, u32[]{:S(2)}, u32[]{:S(2)}) collective-permute-start(bf16[208,768]{1,0:T(8,128)(2,1)S(1)} %get-tuple-element.262), channel_id=1, source_target_pairs={{0,4},{1,9},{2,6},{3,11},{4,0},{5,13},{6,2},{7,15},{8,12},{9,1},{1... | collective-permute-start | bytes 958472 | tf_op jit(solution)/shard_map/ppermute | solution.py:130
  192.1 15.5 %collective-permute-start.42 = (bf16[1,128,768]{2,1,0:T(8,128)(2,1)S(1)}, bf16[1,128,768]{2,1,0:T(8,128)(2,1)S(1)}, u32[]{:S(2)}, u32[]{:S(2)}) collective-permute-start(bf16[1,128,768]{2,1,0:T(8,128)(2,1)S(1)} %get-tuple-element.257), channel_id=1, source_target_pairs={{0,8},{1,3},{2,10},{3,1},{4,12},{5,7},{6,14},{7,5},{8,0},{9,11},{1... | collective-permute-start | bytes 589832 | tf_op jit(solution)/shard_map/ppermute | solution.py:130
  (65 other events, 396.3 us)

commit v4 on v3

--- a/solution.py
+++ b/solution.py
@@ -22,14 +22,16 @@
 SMALL_BYTES = 16 << 20
 COST = pl.CostEstimate(flops=1000, bytes_accessed=1000, transcendentals=0)
 FORWARD = ('XBADbxad|BAba|BADXbadx|BDXbd|', 'xAD', '', 'ad|')
-BACKWARD = ('', '', 'a|A', 'da|DX', 'B|Adab|DABx|aXdbBDxd|Xb|B|xb')
+BACKWARD = ('', '', 'a|A', 'da|DX', '|AdBab|DABxadXbDBxd|XbB|xb')
 TOKEN_NEAR = 0
 TOKEN_TURN = 'mix'
 WEIGHT_TURNS = {'D': (1, 0, 3, 2), 'A': (3, 2, 1, 0), 'B': (3, 2, 1, 0)}
-WAITS = (False, False, False, False, False, False)
+WAITS = (False, False, True, False, False, False)
 FIRST_WAITS = False
 INPUTS_FIRST = False
 REDUCE_FIRST = False
+OUTPUT_FIRST = False
+VECTORS_LATE = True
 STRICT = (True, False)
 
 
@@ -1335,6 +1337,8 @@
         return jnp.where(even, first, second), jnp.where(even, second, first)
 
     order = Order(place, STRICT[1])
+    if OUTPUT_FIRST:
+        order.last = (hidden_low,)
     chains = {
         "D": Scatter(order, reduce_keep, reduce_send, stages, turn=turns.get("D")),
         "A": Scatter(order, expand_keep, expand_send, stages, turn=turns.get("A")),
@@ -1374,7 +1378,6 @@
     mine_rows = jnp.where(even, jnp.concatenate([mine_rows, zero], 1), jnp.concatenate([zero, mine_rows], 1))
     vector_sums = jnp.concatenate([mine_rows, (sums_one + sums_two)[2:], sums_expand])
     vector_swap = place.swap(vector_sums, 0)
-    vector_sums = vector_sums + jnp.where(jnp.arange(VECTOR_ROWS)[:, None] < 8, vector_swap, 0)
 
     far_part = keys_inputs(1, (held_back(4, parts[0]), *parts[1:]), query_far, weights_kv)
     far_got = place.swap(far_part, 0)
@@ -1408,6 +1411,8 @@
         grad_output.reshape(chips, 2 * own, side),
         parts,
     )
+    vector_swap = after(vector_swap, keep) if VECTORS_LATE else vector_swap
+    vector_sums = vector_sums + jnp.where(jnp.arange(VECTOR_ROWS)[:, None] < 8, vector_swap, 0)
     keep = keep.reshape(-1, width)
     send = jnp.concatenate([send.reshape(-1, width), vector_sums.astype(BF16)])
     chains["B"] = Scatter(order, keep, send, stages, vector_sums, turns.get("B"))

time: 220 us -> 220 us (level)
  no operation moved by 1% of the time
where the time goes in v4:
time: 220 us
  waiting for transfers between devices  99.2 us (45%)
  Pallas kernels  56.1 us (26%)
  starting transfers between devices  50.5 us (23%)
  local copies, waits for them, and re-layouts  5.56 us (3%)
  other arithmetic  4.2 us (2%)
  between operations  2.53 us (1%)
    ppermute x46, waiting for transfers between devices, swap(): return lax.ppermute(array, EVERY, pairs)  99.2 us
    ppermute x46, starting transfers between devices, swap(): return lax.ppermute(array, EVERY, pairs)  50.5 us
    pallas_call x25, Pallas kernels, call(): pl.pallas_call(kernel, out_shape=flat if many else flat[0], in_specs=spec...  19.8 us
    pallas_call x1, Pallas kernels, attend(): pl.pallas_call(attend_kernel, out_shape=(shaped((rows, width), F32), shap...  8.99 us
    pallas_call x3, Pallas kernels, attend_back(): pl.pallas_call(attend_back_kernel, out_shape=(shaped((rows, pair), BF16),...  8.57 us
    pallas_call x1, Pallas kernels, hidden_back(): pl.pallas_call(hidden_back_kernel, out_shape=(shaped((rows, width), F32),...  6.04 us
    unnamed x91, local copies, waits for them, and re-layouts  5.48 us
    pallas_call x1, Pallas kernels, keys_weights(): pl.pallas_call(keys_weights_kernel, out_shape=(block, block), grid_spec=p...  4.8 us
  transfers between devices with their start and end apart: 46, of which 25 were waited for; matrix products, arithmetic and copies ran while one was open for 4% of the time, Pallas kernels for 19%

profile of v4, /device:TPU:0, one launch (start us, length us, event | category | flops | bytes accessed | tf_op | source)
XLA Modules:
  0.0 219.6 jit_solution(3657880878537903482)
XLA Ops:
  0.7 4.1 %collective-permute-start.7 = (bf16[1,96,768]{2,1,0:T(8,128)(2,1)}, bf16[1,96,768]{2,1,0:T(8,128)(2,1)S(1)}, u32[]{:S(2)}, u32[]{:S(2)}) collective-permute-start(bf16[1,96,768]{2,1,0:T(8,128)(2,1)} %bitcast.128), channel_id=1, source_target_pairs={{0,8},{1,5},{2,10},{3,7},{4,12},{5,1},{6,14},{7,3},{8,0},{9,13},{1... | collective-permute-start | bytes 442376 | tf_op jit(solution)/shard_map/ppermute | solution.py:132
  12.9 3.4 %collective-permute-done.3 = bf16[112,768]{1,0:T(8,128)(2,1)S(1)} collective-permute-done((bf16[112,768]{1,0:T(8,128)(2,1)S(1)}, bf16[112,768]{1,0:T(8,128)(2,1)S(1)}, u32[]{:S(2)}, u32[]{:S(2)}) %collective-permute-start.3) | collective-permute-done | bytes 172064 | tf_op jit(solution)/shard_map/ppermute | solution.py:132
  17.1 3.5 %collective-permute-done.6 = bf16[1,96,768]{2,1,0:T(8,128)(2,1)S(1)} collective-permute-done((bf16[1,96,768]{2,1,0:T(8,128)(2,1)S(1)}, bf16[1,96,768]{2,1,0:T(8,128)(2,1)S(1)}, u32[]{:S(2)}, u32[]{:S(2)}) %collective-permute-start.6) | collective-permute-done | bytes 147488 | tf_op jit(solution)/shard_map/ppermute | solution.py:132
  22.7 8.3 %collective-permute-done.8 = bf16[208,768]{1,0:T(8,128)(2,1)S(1)} collective-permute-done((bf16[208,768]{1,0:T(8,128)(2,1)S(1)}, bf16[208,768]{1,0:T(8,128)(2,1)S(1)}, u32[]{:S(2)}, u32[]{:S(2)}) %collective-permute-start.8) | collective-permute-done | bytes 319520 | tf_op jit(solution)/shard_map/ppermute | solution.py:132
  31.8 3.8 %collective-permute-done.9 = bf16[2,96,768]{2,1,0:T(8,128)(2,1)S(1)} collective-permute-done((bf16[2,96,768]{2,1,0:T(8,128)(2,1)S(1)}, bf16[2,96,768]{2,1,0:T(8,128)(2,1)S(1)}, u32[]{:S(2)}, u32[]{:S(2)}) %collective-permute-start.9) | collective-permute-done | bytes 294944 | tf_op jit(solution)/shard_map/ppermute | solution.py:132
  37.9 3.5 %collective-permute-start.13 = (bf16[2,128,768]{2,1,0:T(8,128)(2,1)S(1)}, bf16[2,128,768]{2,1,0:T(8,128)(2,1)S(1)}, u32[]{:S(2)}, u32[]{:S(2)}) collective-permute-start(bf16[2,128,768]{2,1,0:T(8,128)(2,1)S(1)} %pad_maximum_fusion.9), channel_id=1, source_target_pairs={{0,8},{1,5},{2,10},{3,7},{4,12},{5,1},{6,14},{7,3},{8,0},{9,13},{1... | collective-permute-start | bytes 1179656 | tf_op jit(solution)/shard_map/ppermute | solution.py:132
  41.4 4.3 %collective-permute-done.10 = bf16[400,768]{1,0:T(8,128)(2,1)S(1)} collective-permute-done((bf16[400,768]{1,0:T(8,128)(2,1)S(1)}, bf16[400,768]{1,0:T(8,128)(2,1)S(1)}, u32[]{:S(2)}, u32[]{:S(2)}) %collective-permute-start.10) | collective-permute-done | bytes 614432 | tf_op jit(solution)/shard_map/ppermute | solution.py:132
  47.3 6.0 %collective-permute-done.12 = bf16[2,96,768]{2,1,0:T(8,128)(2,1)S(1)} collective-permute-done((bf16[2,96,768]{2,1,0:T(8,128)(2,1)S(1)}, bf16[2,96,768]{2,1,0:T(8,128)(2,1)S(1)}, u32[]{:S(2)}, u32[]{:S(2)}) %collective-permute-start.12) | collective-permute-done | bytes 294944 | tf_op jit(solution)/shard_map/ppermute | solution.py:132
  59.1 14.9 %collective-permute-done.16 = bf16[4,96,768]{2,1,0:T(8,128)(2,1)S(1)} collective-permute-done((bf16[4,96,768]{2,1,0:T(8,128)(2,1)S(1)}, bf16[4,96,768]{2,1,0:T(8,128)(2,1)S(1)}, u32[]{:S(2)}, u32[]{:S(2)}) %collective-permute-start.16) | collective-permute-done | bytes 589856 | tf_op jit(solution)/shard_map/ppermute | solution.py:132
  83.0 3.2 %project.1.k_ref.v_ref = bf16[2048,768]{1,0:T(8,128)(2,1)S(1)} custom-call(bf16[1024,768]{1,0:T(8,128)(2,1)S(1)} %bitcast.91, bf16[1024,768]{1,0:T(8,128)(2,1)S(1)} %collective-permute-done.17.other_ref, bf16[768,768]{1,0:T(8,128)(2,1)S(1)} %bitcast.93, f32[8,1152]{1,0:T(8,128)S(1)} %get-tuple-element.170.bias_ref), custom_call_target="tpu_custom_call" | custom-call | flops 1000 | bytes 1000 | tf_op jit(solution)/shard_map/project/pallas_call | solution.py:471
  87.5 9.0 %attend.1 = (f32[256,384]{1,0:T(8,128)S(1)}, f32[3,8,256]{2,1,0:T(8,128)S(1)}) custom-call(bf16[256,384]{1,0:T(8,128)(2,1)S(1)} %fusion.q_ref, bf16[2048,768]{1,0:T(8,128)(2,1)S(1)} %project.1.k_ref.v_ref, bf16[2048,768]{1,0:T(8,128)(2,1)S(1)} %project.1.k_ref.v_ref, bf16[2048,128]{1,0:T(8,128)(2,1)S(1)} %broadcast_select_fusion.mask_ref), custom_call_target="tpu_custom_call" | custom-call | flops 1000 | bytes 1000 | tf_op jit(solution)/shard_map/attend/pallas_call | solution.py:521
  100.3 6.0 %collective-permute-done.22.other_d_ref = bf16[8,96,768]{2,1,0:T(8,128)(2,1)S(1)} collective-permute-done((bf16[8,96,768]{2,1,0:T(8,128)(2,1)S(1)}, bf16[8,96,768]{2,1,0:T(8,128)(2,1)S(1)}, u32[]{:S(2)}, u32[]{:S(2)}) %collective-permute-start.22) | collective-permute-done | bytes 1179680 | tf_op jit(solution)/shard_map/ppermute | solution.py:132
  107.3 3.4 %hidden.1 = (bf16[256,1536]{1,0:T(8,128)(2,1)}, bf16[256,1536]{1,0:T(8,128)(2,1)}, f32[128,768]{1,0:T(8,128)}, bf16[128,768]{1,0:T(8,128)(2,1)}) custom-call(bf16[128,768]{1,0:T(8,128)(2,1)S(1)} %get-tuple-element.179.mine_ref.refs_6_, bf16[128,768]{1,0:T(8,128)(2,1)S(1)} %collective-permute-done.20.other_ref.refs_7_, ...), custom_call_target="tpu_custom_call" | custom-call | flops 1000 | bytes 1000 | tf_op jit(solution)/shard_map/hidden/pallas_call | solution.py:99
  112.6 3.0 %final.1 = (bf16[128,768]{1,0:T(8,128)(2,1)}, f32[128,768]{1,0:T(8,128)S(1)}, bf16[128,768]{1,0:T(8,128)(2,1)S(1)}, f32[8,768]{1,0:T(8,128)S(1)}) custom-call(s32[2]{0:T(128)S(1)} %pad_add_fusion.refs_0_, f32[128,768]{1,0:T(8,128)} %get-tuple-element.189.refs_1_, bf16[128,768]{1,0:T(8,128)(2,1)} %collective-permute-done.23.refs_2_, ...), custom_call_target="tpu_custom_call" | custom-call | flops 1000 | bytes 1000 | tf_op jit(solution)/shard_map/final/pallas_call | solution.py:99
  117.1 6.0 %hidden_back.1 = (f32[128,768]{1,0:T(8,128)S(1)}, bf16[128,768]{1,0:T(8,128)(2,1)S(1)}, f32[8,768]{1,0:T(8,128)S(1)}, bf16[8,96,768]{2,1,0:T(8,128)(2,1)S(1)}, b...) custom-call(s32[16]{0:T(128)S(1)} %and_select_fusion.2.table_ref.table_a_ref, ...), custom_call_target="tpu_custom_call" | custom-call | flops 1000 | bytes 1000 | tf_op jit(solution)/shard_map/hidden_back/pallas_call | solution.py:925
  134.6 2.9 %attend_back.4 = (bf16[256,128]{1,0:T(8,128)(2,1)S(1)}, bf16[2048,128]{1,0:T(8,128)(2,1)S(1)}, bf16[2048,128]{1,0:T(8,128)(2,1)S(1)}, f32[8,128]{1,0:T(8,128)S(1)}) custom-call(bf16[256,384]{1,0:T(8,128)(2,1)S(1)} %copy-done.11, bf16[2048,768]{1,0:T(8,128)(2,1)S(1)} %project.1.k_ref.v_ref, bf16[2048,768]{1,0:T(8,128)(2,1)S(1)} %project.1.k_ref.v_ref, ...), custom_call_target="tpu_custom_call" | custom-call | flops 1000 | bytes 1000 | tf_op jit(solution)/shard_map/attend_back/pallas_call | solution.py:593
  137.4 2.9 %attend_back.3 = (bf16[256,128]{1,0:T(8,128)(2,1)S(1)}, bf16[2048,128]{1,0:T(8,128)(2,1)S(1)}, bf16[2048,128]{1,0:T(8,128)(2,1)S(1)}, f32[8,128]{1,0:T(8,128)S(1)}) custom-call(bf16[256,384]{1,0:T(8,128)(2,1)S(1)} %copy-done.11, bf16[2048,768]{1,0:T(8,128)(2,1)S(1)} %project.1.k_ref.v_ref, bf16[2048,768]{1,0:T(8,128)(2,1)S(1)} %project.1.k_ref.v_ref, ...), custom_call_target="tpu_custom_call" | custom-call | flops 1000 | bytes 1000 | tf_op jit(solution)/shard_map/attend_back/pallas_call | solution.py:593
  146.7 4.8 %keys_weights.1 = (bf16[8,96,768]{2,1,0:T(8,128)(2,1)S(1)}, bf16[8,96,768]{2,1,0:T(8,128)(2,1)S(1)}) custom-call(s32[16]{0:T(128)S(1)} %and_select_fusion.2.table_ref.table_a_ref, bf16[1024,768]{1,0:T(8,128)(2,1)S(1)} %bitcast.92, bf16[1024,768]{1,0:T(8,128)(2,1)S(1)} %copy-done.9, bf16[16,48,384]{2,1,0:T(8,128)(2,1)S(1)} %bitcast.113, ...), custom_call_target="tpu_custom_call" | custom-call | flops 1000 | bytes 1000 | tf_op jit(solution)/shard_map/keys_weights/pallas_call | solution.py:731
  162.0 9.5 %collective-permute-done.36.got_ref = bf16[784,768]{1,0:T(8,128)(2,1)S(1)} collective-permute-done((bf16[784,768]{1,0:T(8,128)(2,1)S(1)}, bf16[784,768]{1,0:T(8,128)(2,1)S(1)}, u32[]{:S(2)}, u32[]{:S(2)}) %collective-permute-start.36) | collective-permute-done | bytes 1204256 | tf_op jit(solution)/shard_map/ppermute | solution.py:132
  171.7 6.0 %collective-permute-done.33.got_ref = bf16[2,96,768]{2,1,0:T(8,128)(2,1)S(1)} collective-permute-done((bf16[2,96,768]{2,1,0:T(8,128)(2,1)S(1)}, bf16[2,96,768]{2,1,0:T(8,128)(2,1)S(1)}, u32[]{:S(2)}, u32[]{:S(2)}) %collective-permute-start.33) | collective-permute-done | bytes 294944 | tf_op jit(solution)/shard_map/ppermute | solution.py:132
  188.1 3.0 %collective-permute-start.43 = (bf16[208,768]{1,0:T(8,128)(2,1)S(1)}, bf16[208,768]{1,0:T(8,128)(2,1)S(1)}, u32[]{:S(2)}, u32[]{:S(2)}) collective-permute-start(bf16[208,768]{1,0:T(8,128)(2,1)S(1)} %get-tuple-element.264), channel_id=1, source_target_pairs={{0,4},{1,9},{2,6},{3,11},{4,0},{5,13},{6,2},{7,15},{8,12},{9,1},{1... | collective-permute-start | bytes 958472 | tf_op jit(solution)/shard_map/ppermute | solution.py:132
  192.1 3.5 %collective-permute-start.42 = (bf16[1,128,768]{2,1,0:T(8,128)(2,1)S(1)}, bf16[1,128,768]{2,1,0:T(8,128)(2,1)S(1)}, u32[]{:S(2)}, u32[]{:S(2)}) collective-permute-start(bf16[1,128,768]{2,1,0:T(8,128)(2,1)S(1)} %get-tuple-element.259), channel_id=1, source_target_pairs={{0,8},{1,3},{2,10},{3,1},{4,12},{5,7},{6,14},{7,5},{8,0},{9,11},{1... | collective-permute-start | bytes 589832 | tf_op jit(solution)/shard_map/ppermute | solution.py:132
  195.6 11.8 %collective-permute-done.42.got_ref = bf16[1,128,768]{2,1,0:T(8,128)(2,1)S(1)} collective-permute-done((bf16[1,128,768]{2,1,0:T(8,128)(2,1)S(1)}, bf16[1,128,768]{2,1,0:T(8,128)(2,1)S(1)}, u32[]{:S(2)}, u32[]{:S(2)}) %collective-permute-start.42) | collective-permute-done | bytes 196640 | tf_op jit(solution)/shard_map/ppermute | solution.py:132
  208.5 6.4 %collective-permute-done.44.got_ref = bf16[112,768]{1,0:T(8,128)(2,1)S(1)} collective-permute-done((bf16[112,768]{1,0:T(8,128)(2,1)S(1)}, bf16[112,768]{1,0:T(8,128)(2,1)S(1)}, u32[]{:S(2)}, u32[]{:S(2)}) %collective-permute-start.44) | collective-permute-done | bytes 172064 | tf_op jit(solution)/shard_map/ppermute | solution.py:132
  (244 shorter events, 83.9 us)
Async XLA Ops:
  0.7 16.4 %collective-permute-start.7 = (bf16[1,96,768]{2,1,0:T(8,128)(2,1)}, bf16[1,96,768]{2,1,0:T(8,128)(2,1)S(1)}, u32[]{:S(2)}, u32[]{:S(2)}) collective-permute-start(bf16[1,96,768]{2,1,0:T(8,128)(2,1)} %bitcast.128), channel_id=1, source_target_pairs={{0,8},{1,5},{2,10},{3,7},{4,12},{5,1},{6,14},{7,3},{8,0},{9,13},{1... | collective-permute-start | bytes 442376 | tf_op jit(solution)/shard_map/ppermute | solution.py:132
  4.8 12.3 %collective-permute-start.4 = (bf16[1,128,768]{2,1,0:T(8,128)(2,1)}, bf16[1,128,768]{2,1,0:T(8,128)(2,1)S(1)}, u32[]{:S(2)}, u32[]{:S(2)}) collective-permute-start(bf16[1,128,768]{2,1,0:T(8,128)(2,1)} %param.28), channel_id=1, source_target_pairs={{0,2},{1,3},{2,0},{3,1},{4,6},{5,7},{6,4},{7,5},{8,10},{9,11},{10,... | collective-permute-start | bytes 589832 | tf_op jit(solution)/shard_map/ppermute | solution.py:132
  10.0 10.6 %collective-permute-start.6 = (bf16[1,96,768]{2,1,0:T(8,128)(2,1)S(1)}, bf16[1,96,768]{2,1,0:T(8,128)(2,1)S(1)}, u32[]{:S(2)}, u32[]{:S(2)}) collective-permute-start(bf16[1,96,768]{2,1,0:T(8,128)(2,1)S(1)} %bitcast.124), channel_id=1, source_target_pairs={{0,8},{1,5},{2,10},{3,7},{4,12},{5,1},{6,14},{7,3},{8,0},{9,13},{1... | collective-permute-start | bytes 442376 | tf_op jit(solution)/shard_map/ppermute | solution.py:132
  20.6 15.0 %collective-permute-start.9 = (bf16[2,96,768]{2,1,0:T(8,128)(2,1)S(1)}, bf16[2,96,768]{2,1,0:T(8,128)(2,1)S(1)}, u32[]{:S(2)}, u32[]{:S(2)}) collective-permute-start(bf16[2,96,768]{2,1,0:T(8,128)(2,1)S(1)} %pad_maximum_fusion.11), channel_id=1, source_target_pairs={{0,4},{1,9},{2,6},{3,11},{4,0},{5,13},{6,2},{7,15},{8,12},{9,1},{1... | collective-permute-start | bytes 884744 | tf_op jit(solution)/shard_map/ppermute | solution.py:132
  36.2 17.2 %collective-permute-start.11 = (bf16[4,96,768]{2,1,0:T(8,128)(2,1)S(1)}, bf16[4,96,768]{2,1,0:T(8,128)(2,1)S(1)}, u32[]{:S(2)}, u32[]{:S(2)}) collective-permute-start(bf16[4,96,768]{2,1,0:T(8,128)(2,1)S(1)} %pad_maximum_fusion.7), channel_id=1, source_target_pairs={{0,2},{1,17},{2,0},{3,19},{4,6},{5,21},{6,4},{7,23},{8,10},{9,25},... | collective-permute-start | bytes 1769480 | tf_op jit(solution)/shard_map/ppermute | solution.py:132
  37.9 15.5 %collective-permute-start.12 = (bf16[2,96,768]{2,1,0:T(8,128)(2,1)S(1)}, bf16[2,96,768]{2,1,0:T(8,128)(2,1)S(1)}, u32[]{:S(2)}, u32[]{:S(2)}) collective-permute-start(bf16[2,96,768]{2,1,0:T(8,128)(2,1)S(1)} %pad_maximum_fusion.12), channel_id=1, source_target_pairs={{0,4},{1,9},{2,6},{3,11},{4,0},{5,13},{6,2},{7,15},{8,12},{9,1},{1... | collective-permute-start | bytes 884744 | tf_op jit(solution)/shard_map/ppermute | solution.py:132
  37.9 15.5 %collective-permute-start.13 = (bf16[2,128,768]{2,1,0:T(8,128)(2,1)S(1)}, bf16[2,128,768]{2,1,0:T(8,128)(2,1)S(1)}, u32[]{:S(2)}, u32[]{:S(2)}) collective-permute-start(bf16[2,128,768]{2,1,0:T(8,128)(2,1)S(1)} %pad_maximum_fusion.9), channel_id=1, source_target_pairs={{0,8},{1,5},{2,10},{3,7},{4,12},{5,1},{6,14},{7,3},{8,0},{9,13},{1... | collective-permute-start | bytes 1179656 | tf_op jit(solution)/shard_map/ppermute | solution.py:132
  53.4 23.1 %collective-permute-start.14 = (bf16[784,768]{1,0:T(8,128)(2,1)}, bf16[784,768]{1,0:T(8,128)(2,1)S(1)}, u32[]{:S(2)}, u32[]{:S(2)}) collective-permute-start(bf16[784,768]{1,0:T(8,128)(2,1)} %constant_dynamic-update-slice_fusion), channel_id=1, source_target_pairs={{0,16},{1,3},{2,18},{3,1},{4,20},{5,7},{6,22},{7,5},{8,24},{9,11},... | collective-permute-start | bytes 3612680 | tf_op jit(solution)/shard_map/ppermute | solution.py:132
  55.0 26.4 %collective-permute-start = (bf16[128,768]{1,0:T(8,128)(2,1)S(1)}, bf16[128,768]{1,0:T(8,128)(2,1)}, u32[]{:S(2)}, u32[]{:S(2)}) collective-permute-start(bf16[128,768]{1,0:T(8,128)(2,1)S(1)} %bitcast.122), channel_id=1, source_target_pairs={{0,1},{1,0},{2,3},{3,2},{4,5},{5,4},{6,7},{7,6},{8,9},{9,8},{10,11... | collective-permute-start | bytes 589832 | tf_op jit(solution)/shard_map/ppermute | solution.py:132
  55.2 20.8 %collective-permute-start.15 = (bf16[4,128,768]{2,1,0:T(8,128)(2,1)S(1)}, bf16[4,128,768]{2,1,0:T(8,128)(2,1)S(1)}, u32[]{:S(2)}, u32[]{:S(2)}) collective-permute-start(bf16[4,128,768]{2,1,0:T(8,128)(2,1)S(1)} %pad_maximum_fusion.5), channel_id=1, source_target_pairs={{0,4},{1,9},{2,6},{3,11},{4,0},{5,13},{6,2},{7,15},{8,12},{9,1},{1... | collective-permute-start | bytes 2359304 | tf_op jit(solution)/shard_map/ppermute | solution.py:132
  57.7 16.3 %collective-permute-start.16 = (bf16[4,96,768]{2,1,0:T(8,128)(2,1)S(1)}, bf16[4,96,768]{2,1,0:T(8,128)(2,1)S(1)}, u32[]{:S(2)}, u32[]{:S(2)}) collective-permute-start(bf16[4,96,768]{2,1,0:T(8,128)(2,1)S(1)} %pad_maximum_fusion.8), channel_id=1, source_target_pairs={{0,2},{1,17},{2,0},{3,19},{4,6},{5,21},{6,4},{7,23},{8,10},{9,25},... | collective-permute-start | bytes 1769480 | tf_op jit(solution)/shard_map/ppermute | solution.py:132
  77.4 23.0 %collective-permute-start.21 = (bf16[8,96,768]{2,1,0:T(8,128)(2,1)S(1)}, bf16[8,96,768]{2,1,0:T(8,128)(2,1)S(1)}, u32[]{:S(2)}, u32[]{:S(2)}) collective-permute-start(bf16[8,96,768]{2,1,0:T(8,128)(2,1)S(1)} %pad_maximum_fusion.3.mine_a_ref), channel_id=1, source_target_pairs={{0,16},{1,3},{2,18},{3,1},{4,20},{5,7},{6,22},{7,5},{8,24},{9,11},... | collective-permute-start | bytes 3538952 | tf_op jit(solution)/shard_map/ppermute | solution.py:132
  78.9 27.4 %collective-permute-start.22 = (bf16[8,96,768]{2,1,0:T(8,128)(2,1)S(1)}, bf16[8,96,768]{2,1,0:T(8,128)(2,1)S(1)}, u32[]{:S(2)}, u32[]{:S(2)}) collective-permute-start(bf16[8,96,768]{2,1,0:T(8,128)(2,1)S(1)} %pad_maximum_fusion.4.mine_d_ref), channel_id=1, source_target_pairs={{0,16},{1,3},{2,18},{3,1},{4,20},{5,7},{6,22},{7,5},{8,24},{9,11},... | collective-permute-start | bytes 3538952 | tf_op jit(solution)/shard_map/ppermute | solution.py:132
  81.3 15.7 %collective-permute-start.19 = (bf16[768,384]{1,0:T(8,128)(2,1)S(1)}, bf16[768,384]{1,0:T(8,128)(2,1)S(1)}, u32[]{:S(2)}, u32[]{:S(2)}) collective-permute-start(bf16[768,384]{1,0:T(8,128)(2,1)S(1)} %bitcast.102), channel_id=1, source_target_pairs={{0,1},{1,0},{2,3},{3,2},{4,5},{5,4},{6,7},{7,6},{8,9},{9,8},{10,11... | collective-permute-start | bytes 1769480 | tf_op jit(solution)/shard_map/ppermute | solution.py:132
  123.4 29.1 %collective-permute-start.28 = (bf16[8,96,768]{2,1,0:T(8,128)(2,1)S(1)}, bf16[8,96,768]{2,1,0:T(8,128)(2,1)S(1)}, u32[]{:S(2)}, u32[]{:S(2)}) collective-permute-start(bf16[8,96,768]{2,1,0:T(8,128)(2,1)S(1)} %get-tuple-element.216), channel_id=1, source_target_pairs={{0,4},{1,9},{2,6},{3,11},{4,0},{5,13},{6,2},{7,15},{8,12},{9,1},{1... | collective-permute-start | bytes 3538952 | tf_op jit(solution)/shard_map/ppermute | solution.py:132
  125.7 19.0 %collective-permute-start.29 = (bf16[8,96,768]{2,1,0:T(8,128)(2,1)S(1)}, bf16[8,96,768]{2,1,0:T(8,128)(2,1)S(1)}, u32[]{:S(2)}, u32[]{:S(2)}) collective-permute-start(bf16[8,96,768]{2,1,0:T(8,128)(2,1)S(1)} %get-tuple-element.218), channel_id=1, source_target_pairs={{0,16},{1,3},{2,18},{3,1},{4,20},{5,7},{6,22},{7,5},{8,24},{9,11},... | collective-permute-start | bytes 3538952 | tf_op jit(solution)/shard_map/ppermute | solution.py:132
  131.1 14.5 %collective-permute-start.34 = (bf16[768,384]{1,0:T(8,128)(2,1)S(1)}, bf16[768,384]{1,0:T(8,128)(2,1)S(1)}, u32[]{:S(2)}, u32[]{:S(2)}) collective-permute-start(bf16[768,384]{1,0:T(8,128)(2,1)S(1)} %get-tuple-element.233), channel_id=1, source_target_pairs={{0,1},{1,0},{2,3},{3,2},{4,5},{5,4},{6,7},{7,6},{8,9},{9,8},{10,11... | collective-permute-start | bytes 1769480 | tf_op jit(solution)/shard_map/ppermute | solution.py:132
  144.1 15.2 %collective-permute-start.27 = (bf16[1024,768]{1,0:T(8,128)(2,1)S(1)}, bf16[1024,768]{1,0:T(8,128)(2,1)S(1)}, u32[]{:S(2)}, u32[]{:S(2)}) collective-permute-start(bf16[1024,768]{1,0:T(8,128)(2,1)S(1)} %keys_inputs.3), channel_id=1, source_target_pairs={{0,1},{1,0},{2,3},{3,2},{4,5},{5,4},{6,7},{7,6},{8,9},{9,8},{10,11... | collective-permute-start | bytes 4718600 | tf_op jit(solution)/shard_map/ppermute | solution.py:132
  155.0 16.5 %collective-permute-start.36 = (bf16[784,768]{1,0:T(8,128)(2,1)S(1)}, bf16[784,768]{1,0:T(8,128)(2,1)S(1)}, u32[]{:S(2)}, u32[]{:S(2)}) collective-permute-start(bf16[784,768]{1,0:T(8,128)(2,1)S(1)} %pad_maximum_fusion.1), channel_id=1, source_target_pairs={{0,16},{1,3},{2,18},{3,1},{4,20},{5,7},{6,22},{7,5},{8,24},{9,11},... | collective-permute-start | bytes 3612680 | tf_op jit(solution)/shard_map/ppermute | solution.py:132
  155.8 22.0 %collective-permute-start.32 = (bf16[4,96,768]{2,1,0:T(8,128)(2,1)S(1)}, bf16[4,96,768]{2,1,0:T(8,128)(2,1)S(1)}, u32[]{:S(2)}, u32[]{:S(2)}) collective-permute-start(bf16[4,96,768]{2,1,0:T(8,128)(2,1)S(1)} %get-tuple-element.226), channel_id=1, source_target_pairs={{0,8},{1,5},{2,10},{3,7},{4,12},{5,1},{6,14},{7,3},{8,0},{9,13},{1... | collective-permute-start | bytes 1769480 | tf_op jit(solution)/shard_map/ppermute | solution.py:132
  159.6 20.8 %collective-permute-start.31 = (bf16[4,128,768]{2,1,0:T(8,128)(2,1)S(1)}, bf16[4,128,768]{2,1,0:T(8,128)(2,1)S(1)}, u32[]{:S(2)}, u32[]{:S(2)}) collective-permute-start(bf16[4,128,768]{2,1,0:T(8,128)(2,1)S(1)} %get-tuple-element.221), channel_id=1, source_target_pairs={{0,2},{1,5},{2,0},{3,7},{4,6},{5,1},{6,4},{7,3},{8,10},{9,13},{10,... | collective-permute-start | bytes 2359304 | tf_op jit(solution)/shard_map/ppermute | solution.py:132
  160.4 17.4 %collective-permute-start.33 = (bf16[2,96,768]{2,1,0:T(8,128)(2,1)S(1)}, bf16[2,96,768]{2,1,0:T(8,128)(2,1)S(1)}, u32[]{:S(2)}, u32[]{:S(2)}) collective-permute-start(bf16[2,96,768]{2,1,0:T(8,128)(2,1)S(1)} %get-tuple-element.229), channel_id=1, source_target_pairs={{0,4},{1,9},{2,6},{3,11},{4,0},{5,13},{6,2},{7,15},{8,12},{9,1},{1... | collective-permute-start | bytes 884744 | tf_op jit(solution)/shard_map/ppermute | solution.py:132
  188.1 19.4 %collective-permute-start.43 = (bf16[208,768]{1,0:T(8,128)(2,1)S(1)}, bf16[208,768]{1,0:T(8,128)(2,1)S(1)}, u32[]{:S(2)}, u32[]{:S(2)}) collective-permute-start(bf16[208,768]{1,0:T(8,128)(2,1)S(1)} %get-tuple-element.264), channel_id=1, source_target_pairs={{0,4},{1,9},{2,6},{3,11},{4,0},{5,13},{6,2},{7,15},{8,12},{9,1},{1... | collective-permute-start | bytes 958472 | tf_op jit(solution)/shard_map/ppermute | solution.py:132
  192.1 15.3 %collective-permute-start.42 = (bf16[1,128,768]{2,1,0:T(8,128)(2,1)S(1)}, bf16[1,128,768]{2,1,0:T(8,128)(2,1)S(1)}, u32[]{:S(2)}, u32[]{:S(2)}) collective-permute-start(bf16[1,128,768]{2,1,0:T(8,128)(2,1)S(1)} %get-tuple-element.259), channel_id=1, source_target_pairs={{0,8},{1,3},{2,10},{3,1},{4,12},{5,7},{6,14},{7,5},{8,0},{9,11},{1... | collective-permute-start | bytes 589832 | tf_op jit(solution)/shard_map/ppermute | solution.py:132
  (65 other events, 399.1 us)
